TPU v7x, 32 devices: a whole 2x2x4 slice. The times are simulated.
32 devices in a mesh: fsdp: 16 (over z, y, core), tp: 2 (over x).
Axes of the slice: x: 2, y: 2, z: 4, core: 2. Of those that a mesh axis runs over, the one named last changes fastest.
Arguments:
- block_input: bfloat16 [4096, 2048], P(('fsdp', 'tp')), may hold values from -6 to 6
- segments: int32 [16, 256], P('fsdp'), may hold values from 0 to 3, never falling along the last dimension, each value on 1 to 128 neighbouring positions
- cotangent: bfloat16 [4096, 2048], P(('fsdp', 'tp')), may hold values from -6 to 6
- norm_gain: bfloat16 [1, 2, 2048], P(None, None, 'fsdp'), may hold values from 0.5 to 1.5
- norm_shift: bfloat16 [1, 2, 2048], P(None, None, 'fsdp'), may hold values from -1.5 to 1.5
- qkv_weight: bfloat16 [1, 2048, 3, 2048], P(None, 'fsdp', None, 'tp'), may hold values from -0.125 to 0.125
- qkv_bias: bfloat16 [1, 3, 32, 64], P(None, None, 'tp', 'fsdp'), may hold values from -6 to 6
- out_weight: bfloat16 [1, 2048, 2048], P(None, 'tp', 'fsdp'), may hold values from -0.375 to 0.375
- gate_up_weight: bfloat16 [1, 2048, 2, 5632], P(None, 'fsdp', None, 'tp'), may hold values from -0.125 to 0.125
- down_weight: bfloat16 [1, 5632, 2048], P(None, 'tp', 'fsdp'), may hold values from -0.078125 to 0.078125
Outputs:
- block_output: bfloat16 [4096, 2048], P(('fsdp', 'tp'))
- input_grad: bfloat16 [4096, 2048], P(('fsdp', 'tp'))
- norm_gain_grad: float32 [1, 2, 2048], P(None, None, 'fsdp')
- norm_shift_grad: float32 [1, 2, 2048], P(None, None, 'fsdp')
- qkv_weight_grad: float32 [1, 2048, 3, 2048], P(None, 'fsdp', None, 'tp')
- qkv_bias_grad: float32 [1, 3, 32, 64], P(None, None, 'tp', 'fsdp')
- out_weight_grad: float32 [1, 2048, 2048], P(None, 'tp', 'fsdp')
- gate_up_grad: float32 [1, 2048, 2, 5632], P(None, 'fsdp', None, 'tp')
- down_grad: float32 [1, 5632, 2048], P(None, 'tp', 'fsdp')
Inputs may be any that keep to these rules, and one draw needn't show every extreme that they name: `segments`: along each sequence segment numbers never fall; each of the 4 documents has 1 to 128 tokens, one exactly 128.
All inputs are finite; a program needn't handle non-finite values.
Results may differ from a plain program's by a relative error of at most 0.019.
The roundings to bfloat16 on the way count: a program that leaves them out, or rounds other values in their place, can miss the bound.
Values may be sent and summed in bfloat16 or wider, within the bound.
No kernel may reach another device: no remote copies, remote signals or barrier semaphores. Data moves between devices by JAX's collectives and lax.ppermute only.
A program may use at most 256 MiB of HBM per device.

v0:
```python
import jax
import jax.numpy as jnp
from jax import lax
from jax.experimental import pallas as pl
from jax.experimental.pallas import tpu as pltpu
from jax.sharding import PartitionSpec as P


HEAD = 64
ROTARY = 16

EPS = 1e-05
NEG = -1e30
SCALE = 0.125
ROPE_BASE = 10000.0

BF16 = jnp.bfloat16
F32 = jnp.float32


def times(left, right):
    return lax.dot_general(left, right, (((1,), (0,)), ((), ())), preferred_element_type=F32)


def times_transposed(left, right):
    return lax.dot_general(left, right, (((1,), (1,)), ((), ())), preferred_element_type=F32)


class Grid:
    def __init__(self, mesh):
        self.count = mesh.shape["fsdp"]
        column = list(mesh.devices[:, 0])
        spots = [tuple(d.coords) for d in column]
        self.cores = 2 if self.count > 1 and spots[0] == spots[1] else 1
        run = 1
        while run < self.count and spots[run][2] == spots[0][2]:
            run += 1
        self.slow = self.count // run
        self.mid = run // self.cores

    def place(self, slow, mid, core):
        return ((slow % self.slow) * self.mid + mid % self.mid) * self.cores + core % self.cores

    def moves(self, slow=0, mid=0, core=0):
        return [
            (self.place(s, m, c), self.place(s + slow, m + mid, c + core))
            for s in range(self.slow)
            for m in range(self.mid)
            for c in range(self.cores)
        ]

    def shift(self, rows, **by):
        return lax.ppermute(rows, "fsdp", self.moves(**by))

    def order(self):
        here = lax.axis_index("fsdp")
        core = here % self.cores
        mid = (here // self.cores) % self.mid
        slow = here // (self.cores * self.mid)
        step = jnp.arange(self.count, dtype=jnp.int32)
        core = (core + step // (self.mid * self.slow)) % self.cores
        mid = (mid + (step // self.slow) % self.mid) % self.mid
        slow = (slow + step % self.slow) % self.slow
        return ((slow * self.mid + mid) * self.cores + core).astype(jnp.int32)


def flip_kernel(order_ref, rows_ref, out_ref):
    count = order_ref.shape[0]
    block = rows_ref.shape[1] // count

    def move(j, carry):
        start = pl.multiple_of(order_ref[j] * block, block)
        out_ref[pl.ds(pl.multiple_of(j * block, block), block), :] = rows_ref[:, pl.ds(start, block)].T
        return carry

    lax.fori_loop(0, count, move, 0)


def turned(rows, order):
    tokens, width = rows.shape
    count = order.shape[0]
    block = width // count
    if block % 128:
        return rows.T.reshape(count, block, tokens)[order].reshape(width, tokens)
    return pl.pallas_call(
        flip_kernel,
        grid_spec=pltpu.PrefetchScalarGridSpec(
            num_scalar_prefetch=1,
            grid=(1,),
            in_specs=[pl.BlockSpec((tokens, width), lambda i, order: (0, 0))],
            out_specs=pl.BlockSpec((width, tokens), lambda i, order: (0, 0)),
        ),
        out_shape=jax.ShapeDtypeStruct((width, tokens), rows.dtype),
    )(order, rows)


def scatter_product(grid, left, right):
    block = left.shape[0] // grid.count
    per_mid = block * grid.slow
    per_core = per_mid * grid.mid
    from_core = []
    for c in range(1, grid.cores):
        out = times(left[c * per_core : (c + 1) * per_core], right).astype(BF16)
        from_core.append(grid.shift(out, core=c))
    from_mid = []
    for m in range(1, grid.mid):
        part = times(left[m * per_mid : (m + 1) * per_mid], right)
        for got in from_core:
            part = part + got[m * per_mid : (m + 1) * per_mid].astype(F32)
        part = part.astype(BF16)
        from_mid.append(grid.shift(part, mid=m))
    from_slow = []
    for s in range(grid.slow):
        span = slice(s * block, (s + 1) * block)
        part = times(left[span], right)
        for got in from_core + from_mid:
            part = part + got[span].astype(F32)
        if s == 0:
            total = part
            continue
        part = part.astype(BF16)
        from_slow.append(grid.shift(part, slow=s))
    for got in from_slow:
        total = total + got.astype(F32)
    return total


def other(rows):
    return lax.ppermute(rows, "tp", [(0, 1), (1, 0)])


def pair(rows):
    return jnp.concatenate([rows, other(rows)], axis=0)


def collect(term):
    half = term.shape[0] // 2
    return term[:half] + other(term[half:].astype(BF16)).astype(F32)


def norm_forward(rows, gain, shift):
    center = rows - jnp.mean(rows, axis=1, keepdims=True)
    inv_std = lax.rsqrt(jnp.mean(center * center, axis=1, keepdims=True) + EPS)
    normed = center * inv_std
    return (normed * gain + shift, normed, inv_std)


def norm_backward(grad_out, normed, inv_std, gain):
    scaled = grad_out * gain
    grad_in = inv_std * (
        scaled
        - jnp.mean(scaled, axis=1, keepdims=True)
        - normed * jnp.mean(scaled * normed, axis=1, keepdims=True)
    )
    return (grad_in, jnp.sum(grad_out * normed, axis=0), jnp.sum(grad_out, axis=0))


def rope_tables(position):
    half = ROTARY // 2
    inverse = ROPE_BASE ** (-jnp.arange(half).astype(F32) * 2.0 / ROTARY)
    angles = position.astype(F32)[:, None] * inverse[None, :]
    return (jnp.cos(angles)[:, None, :], jnp.sin(angles)[:, None, :])


def rotate(values, cosine, sine):
    half = ROTARY // 2
    first = values[..., :half]
    second = values[..., half:ROTARY]
    return jnp.concatenate(
        [first * cosine - second * sine, second * cosine + first * sine, values[..., ROTARY:]],
        axis=-1,
    )


def masked_scores(queries, key_rows, allowed):
    scores = jnp.einsum("qhd,khd->hqk", queries, key_rows, preferred_element_type=F32) * SCALE
    return jnp.where(allowed, scores, NEG)


def attend(queries, key_rows, value_rows, allowed):
    scores = masked_scores(queries, key_rows, allowed)
    top = jnp.max(scores, axis=-1, keepdims=True)
    log_total = top + jnp.log(jnp.sum(jnp.exp(scores - top), axis=-1, keepdims=True))
    probs = jnp.exp(scores - log_total).astype(BF16)
    mixed = jnp.einsum("hqk,khd->qhd", probs, value_rows, preferred_element_type=F32).astype(BF16)
    return (mixed, log_total)


def attend_back(queries, key_rows, value_rows, mixed, log_total, grad_mixed, allowed):
    scores = masked_scores(queries, key_rows, allowed)
    probs = jnp.exp(scores - log_total)
    grad_values = jnp.einsum("hqk,qhd->khd", probs.astype(BF16), grad_mixed, preferred_element_type=F32)
    grad_probs = jnp.einsum("qhd,khd->hqk", grad_mixed, value_rows, preferred_element_type=F32)
    delta = jnp.sum(grad_mixed.astype(F32) * mixed.astype(F32), axis=-1)
    delta = jnp.transpose(delta, (1, 0))[..., None]
    grad_scores = (probs * (grad_probs - delta) * SCALE).astype(BF16)
    grad_queries = jnp.einsum("hqk,khd->qhd", grad_scores, key_rows, preferred_element_type=F32)
    grad_keys = jnp.einsum("hqk,qhd->khd", grad_scores, queries, preferred_element_type=F32)
    return (grad_queries, grad_keys, grad_values)


def shards(
    grid,
    block_input,
    segments,
    cotangent,
    norm_gain,
    norm_shift,
    qkv_weight,
    qkv_bias,
    out_weight,
    gate_up_weight,
    down_weight,
):
    count = grid.count
    mine = block_input.shape[0]
    length = segments.shape[1]
    width = block_input.shape[1]
    block = width // count
    wide = qkv_weight.shape[3]
    heads = qkv_bias.shape[2]
    piece = qkv_bias.shape[3]
    turn = lax.axis_index("tp")

    small = jnp.concatenate(
        [norm_gain.reshape(-1), norm_shift.reshape(-1), qkv_bias.reshape(-1)]
    )
    n_small = small.shape[0]
    small_rows = 16 * (-(-n_small // (16 * wide)))
    small = jnp.pad(small, (0, small_rows * wide - n_small)).reshape(small_rows, wide)
    pack = jnp.concatenate(
        [qkv_weight[0, :, 0], qkv_weight[0, :, 1], qkv_weight[0, :, 2], out_weight[0].T, small], axis=0
    )
    packs = lax.all_gather(pack, "fsdp", axis=0)
    gate_up_all = lax.all_gather(jnp.swapaxes(gate_up_weight[0], 0, 1), "fsdp", axis=1, tiled=True)
    w_down = lax.all_gather(down_weight[0], "fsdp", axis=1, tiled=True)

    w_q, w_k, w_v, w_out_t = (
        packs[:, i * block : (i + 1) * block].reshape(width, wide) for i in range(4)
    )
    small_all = packs[:, 4 * block :].reshape(count, -1)
    gains = jnp.swapaxes(small_all[:, : 2 * block].reshape(count, 2, block), 0, 1).reshape(2, width)
    shifts = jnp.swapaxes(small_all[:, 2 * block : 4 * block].reshape(count, 2, block), 0, 1).reshape(2, width)
    bias = small_all[:, 4 * block : 4 * block + 3 * heads * piece].reshape(count, 3, heads, piece)
    bias = jnp.transpose(bias, (1, 2, 0, 3)).reshape(3, heads * HEAD).astype(F32)
    gains = gains.astype(F32)
    shifts = shifts.astype(F32)
    w_gate = gate_up_all[0]
    w_up = gate_up_all[1]

    position = (jnp.arange(length, dtype=jnp.int32) + turn * mine) % length
    cosine, sine = rope_tables(position)
    seg_row = segments[0]
    seg_row = jnp.where(turn == 0, seg_row, jnp.roll(seg_row, mine))
    allowed = (seg_row[:, None] == seg_row[None, :]) & (position[:, None] >= position[None, :])

    order = grid.order()
    down_cot = pair(cotangent)
    down_cot_t = turned(down_cot, order)
    rows_all = pair(block_input).astype(F32)
    resid = block_input.astype(F32)

    first_norm, _, _ = norm_forward(rows_all, gains[0], shifts[0])
    attn_in = first_norm.astype(BF16)
    queries = (times(attn_in, w_q) + bias[0]).reshape(length, heads, HEAD)
    key_rows = (times(attn_in, w_k) + bias[1]).reshape(length, heads, HEAD)
    value_rows = (times(attn_in, w_v) + bias[2]).reshape(length, heads, HEAD)
    queries = rotate(queries, cosine, sine).astype(BF16)
    key_rows = rotate(key_rows, cosine, sine).astype(BF16)
    value_rows = value_rows.astype(BF16)
    mixed, log_total = attend(queries, key_rows, value_rows, allowed)
    mixed_flat = mixed.reshape(length, -1)
    resid_two = resid + collect(times_transposed(mixed_flat, w_out_t))
    second_norm, normed_two, inv_two = norm_forward(resid_two, gains[1], shifts[1])
    mlp_in = pair(second_norm.astype(BF16))
    gate = times(mlp_in, w_gate)
    upper = times(mlp_in, w_up)
    sigma = jax.nn.sigmoid(gate)
    hidden = (gate * sigma * upper).astype(BF16)
    gate, upper, hidden = lax.optimization_barrier((gate, upper, hidden))
    sigma = jax.nn.sigmoid(gate)
    down_grad = scatter_product(grid, down_cot_t, hidden)
    resid_three = resid_two + collect(times(hidden, w_down))
    block_output = resid_three.astype(BF16)

    grad_three = cotangent.astype(F32)
    grad_hidden = times_transposed(down_cot, w_down)
    grad_gate = (grad_hidden * upper * sigma * (1.0 + gate * (1.0 - sigma))).astype(BF16)
    grad_up = (grad_hidden * gate * sigma).astype(BF16)
    mlp_in_t = turned(mlp_in, order)
    half = grad_gate.shape[1] // 2
    gate_grad, up_grad = (
        jnp.concatenate(
            [scatter_product(grid, mlp_in_t, grad[:, :half]), scatter_product(grid, mlp_in_t, grad[:, half:])],
            axis=1,
        )
        for grad in (grad_gate, grad_up)
    )
    grad_mlp_in = collect(times_transposed(grad_gate, w_gate) + times_transposed(grad_up, w_up))
    grad_norm_two, gain_two, shift_two = norm_backward(grad_mlp_in, normed_two, inv_two, gains[1])
    grad_two = grad_three + grad_norm_two
    attn_cot = pair(grad_two.astype(BF16))
    grad_mixed = times(attn_cot, w_out_t).astype(BF16).reshape(mixed.shape)
    out_grad = scatter_product(grid, turned(attn_cot, order), mixed_flat)
    grad_queries, grad_keys, grad_values = attend_back(
        queries, key_rows, value_rows, mixed, log_total, grad_mixed, allowed
    )
    grad_queries = rotate(grad_queries, cosine, -sine)
    grad_keys = rotate(grad_keys, cosine, -sine)
    bias_terms = jnp.stack([jnp.sum(g, axis=0) for g in (grad_queries, grad_keys, grad_values)])
    attn_in_t = turned(attn_in, order)
    grad_proj = [g.astype(BF16).reshape(length, -1) for g in (grad_queries, grad_keys, grad_values)]
    v_grad = scatter_product(grid, attn_in_t, grad_proj[2])
    q_grad = scatter_product(grid, attn_in_t, grad_proj[0])
    k_grad = scatter_product(grid, attn_in_t, grad_proj[1])
    grad_attn_in = collect(
        times_transposed(grad_proj[0], w_q) + times_transposed(grad_proj[1], w_k) + times_transposed(grad_proj[2], w_v)
    )
    _, normed_one, inv_one = norm_forward(resid, gains[0], shifts[0])
    grad_norm_one, gain_one, shift_one = norm_backward(grad_attn_in, normed_one, inv_one, gains[0])
    input_grad = (grad_two + grad_norm_one).astype(BF16)

    norm_terms = jnp.stack([gain_one, gain_two, shift_one, shift_two])
    norm_terms = jnp.swapaxes(norm_terms.reshape(4, count, block), 0, 1).reshape(count, 4 * block)
    bias_terms = jnp.transpose(bias_terms.reshape(3, heads, count, piece), (2, 0, 1, 3)).reshape(count, -1)
    terms = jnp.concatenate([norm_terms, bias_terms], axis=1)
    n_terms = terms.shape[1]
    term_rows = 8 * (-(-n_terms // (8 * 128)))
    terms = jnp.pad(terms, ((0, 0), (0, term_rows * 128 - n_terms))).reshape(count * term_rows, 128)
    terms = lax.psum(terms, "fsdp")
    terms = lax.dynamic_slice_in_dim(terms, lax.axis_index("fsdp") * term_rows, term_rows, 0).reshape(-1)
    norm_part = terms[: 4 * block].reshape(4, block)
    norm_part = norm_part + other(norm_part)
    bias_part = terms[4 * block : n_terms].reshape(3, heads, piece)
    return (
        block_output,
        input_grad,
        norm_part[None, 0:2],
        norm_part[None, 2:4],
        jnp.stack([q_grad, k_grad, v_grad], axis=1)[None],
        bias_part[None],
        out_grad.T[None],
        jnp.stack([gate_grad, up_grad], axis=1)[None],
        down_grad.T[None],
    )


def solution(mesh):
    placed = (
        P(("fsdp", "tp"), None),
        P("fsdp", None),
        P(("fsdp", "tp"), None),
        P(None, None, "fsdp"),
        P(None, None, "fsdp"),
        P(None, "fsdp", None, "tp"),
        P(None, None, "tp", "fsdp"),
        P(None, "tp", "fsdp"),
        P(None, "fsdp", None, "tp"),
        P(None, "tp", "fsdp"),
    )

    def body(*args):
        return shards(Grid(mesh), *args)

    return jax.shard_map(
        body,
        mesh=mesh,
        in_specs=placed,
        out_specs=(
            P(("fsdp", "tp"), None),
            P(("fsdp", "tp"), None),
            P(None, None, "fsdp"),
            P(None, None, "fsdp"),
            P(None, "fsdp", None, "tp"),
            P(None, None, "tp", "fsdp"),
            P(None, "tp", "fsdp"),
            P(None, "fsdp", None, "tp"),
            P(None, "tp", "fsdp"),
        ),
        check_vma=False,
    )
```

profile of v0, /device:TPU:0, one launch (start us, length us, event | category | flops | bytes accessed | tf_op | source)
XLA Modules:
  0.0 1046.2 jit_solution(1877389102216770814)
XLA Ops:
  12.7 2.6 copy.95
  16.2 3.0 collective-permute-start
  20.8 11.1 %collective-permute-done = bf16[128,2048]{1,0:T(8,128)(2,1)S(1)} collective-permute-done((bf16[128,2048]{1,0:T(8,128)(2,1)S(1)}, bf16[128,2048]{1,0:T(8,128)(2,1)S(1)}, u32[]{:S(2)}, u32[]{:S(2)}) %collective-permute-start) | collective-permute-done | bytes 524320 | tf_op jit(solution)/shard_map/ppermute | solution.py:129
  32.6 74.4 %all-gather.8.cloned.1.call-done = bf16[8448,1024]{1,0:T(8,128)(2,1)} async-done(((bf16[528,1024]{1,0:T(8,128)(2,1)}), bf16[8448,1024]{1,0:T(8,128)(2,1)}) %all-gather.8.cloned.1.call-update) | async-done | bytes 17301520 | tf_op jit(solution)/shard_map/all_gather | solution.py:234
  110.5 11.7 %fusion.252 = (bf16[16,128,1024]{2,1,0:T(8,128)(2,1)}, bf16[16,128,1024]{2,1,0:T(8,128)(2,1)}, bf16[16,128,1024]{2,1,0:T(8,128)(2,1)}, bf16[16,128,1024]{2,1,0:T(8,128)(2,1)S(1)}) fusion(bf16[16,528,1024]{2,1,0:T(8,128)(2,1)} %bitcast.212), kind=kLoop, calls=%fused_computation.405 | loop fusion | bytes 33554432 | tf_op jit(solution)/shard_map/slice | solution.py:239
  126.8 4.5 convolution_add_fusion.26
  133.3 4.6 convolution_add_fusion.27
  152.1 11.3 %collective-permute-done.1 = bf16[128,2048]{1,0:T(8,128)(2,1)} collective-permute-done((bf16[128,2048]{1,0:T(8,128)(2,1)S(1)}, bf16[128,2048]{1,0:T(8,128)(2,1)}, u32[]{:S(2)}, u32[]{:S(2)}) %collective-permute-start.1) | collective-permute-done | bytes 524320 | tf_op jit(solution)/shard_map/ppermute | solution.py:129
  170.8 4.0 shard_map.172
  174.8 4.1 shard_map.169
  182.4 4.1 shard_map.171
  186.5 41.3 %all-gather.6.cloned.1.call-done = bf16[2,2048,2816]{2,1,0:T(8,128)(2,1)} async-done(((bf16[2,128,2816]{2,1,0:T(8,128)(2,1)}), bf16[2,2048,2816]{2,1,0:T(8,128)(2,1)}) %all-gather.6.cloned.1.call-update) | async-done | bytes 23068688 | tf_op jit(solution)/shard_map/all_gather | solution.py:235
  227.8 6.7 fusion.5
  234.5 11.2 %multiply_convert_fusion.3 = (bf16[256,2816]{1,0:T(8,128)(2,1)S(1)}, f32[256,2816]{1,0:T(8,128)}) fusion(f32[256,2816]{1,0:T(8,128)S(1)} %fusion.5, bf16[2,2048,2816]{2,1,0:T(8,128)(2,1)} %all-gather.6.cloned.1.call-done, bf16[128,2048]{1,0:T(8,128)(2,1)} %collective-permute-done.2, bf16[128,2048]{1,0:T(8,128)(2,1)} %add_convert_fusion.5), kind=kOutput, calls=%fused_computation.48 | convolution fusion | flops 2959212544 | bytes 19791872 | tf_op jit(solution)/shard_map/dot_general | solution.py:22
  245.6 81.2 %all-gather.10.cloned.1.call-done = bf16[1,2816,2048]{2,1,0:T(8,128)(2,1)} async-done(((bf16[1,2816,128]{2,1,0:T(8,128)(2,1)}), bf16[1,2816,2048]{2,1,0:T(8,128)(2,1)}) %all-gather.10.cloned.1.call-update) | async-done | bytes 11534352 | tf_op jit(solution)/shard_map/all_gather | solution.py:236
  326.9 10.2 multiply_convert_fusion.1
  337.1 7.1 fusion.4
  344.1 6.1 fusion.25
  351.8 6.4 fusion.2
  358.9 2.6 convolution_convert_fusion.1
  361.5 2.6 convolution_convert_fusion.2
  367.7 8.0 collective-permute-done.3
  375.7 2.9 fusion.250
  383.6 4.1 convolution_convert_fusion
  387.7 4.1 collective-permute-done.6
  396.2 3.8 multiply_convert_fusion
  430.1 4.1 shard_map.170
  434.2 3.3 convolution_convert_fusion.8
  449.8 81.7 %all-reduce.4.cloned.1.call-done = f32[128,128]{1,0:T(8,128)} async-done(((f32[128,128]{1,0:T(8,128)}), f32[128,128]{1,0:T(8,128)}) %all-reduce.4.cloned.1.call-update) | async-done | bytes 65552 | tf_op jit(solution)/shard_map/psum | solution.py:330
  536.6 3.0 fusion.93
  560.7 17.1 %collective-permute-done.20 = bf16[512,1024]{1,0:T(8,128)(2,1)S(1)} collective-permute-done((bf16[512,1024]{1,0:T(8,128)(2,1)S(1)}, bf16[512,1024]{1,0:T(8,128)(2,1)S(1)}, u32[]{:S(2)}, u32[]{:S(2)}) %collective-permute-start.20) | collective-permute-done | bytes 1048608 | tf_op jit(solution)/shard_map/ppermute | solution.py:53
  582.5 79.6 %collective-permute-done.15 = bf16[512,1024]{1,0:T(8,128)(2,1)S(1)} collective-permute-done((bf16[512,1024]{1,0:T(8,128)(2,1)S(1)}, bf16[512,1024]{1,0:T(8,128)(2,1)S(1)}, u32[]{:S(2)}, u32[]{:S(2)}) %collective-permute-start.15) | collective-permute-done | bytes 1048608 | tf_op jit(solution)/shard_map/ppermute | solution.py:53
  666.8 17.8 %collective-permute-done.10 = bf16[512,1024]{1,0:T(8,128)(2,1)S(1)} collective-permute-done((bf16[512,1024]{1,0:T(8,128)(2,1)S(1)}, bf16[512,1024]{1,0:T(8,128)(2,1)S(1)}, u32[]{:S(2)}, u32[]{:S(2)}) %collective-permute-start.10) | collective-permute-done | bytes 1048608 | tf_op jit(solution)/shard_map/ppermute | solution.py:53
  686.4 20.6 %collective-permute-done.25 = bf16[512,1024]{1,0:T(8,128)(2,1)S(1)} collective-permute-done((bf16[512,1024]{1,0:T(8,128)(2,1)S(1)}, bf16[512,1024]{1,0:T(8,128)(2,1)S(1)}, u32[]{:S(2)}, u32[]{:S(2)}) %collective-permute-start.25) | collective-permute-done | bytes 1048608 | tf_op jit(solution)/shard_map/ppermute | solution.py:53
  708.9 4.6 collective-permute-start.23
  723.3 14.6 %collective-permute-done.35 = bf16[512,1408]{1,0:T(8,128)(2,1)S(1)} collective-permute-done((bf16[512,1408]{1,0:T(8,128)(2,1)S(1)}, bf16[512,1408]{1,0:T(8,128)(2,1)S(1)}, u32[]{:S(2)}, u32[]{:S(2)}) %collective-permute-start.35) | collective-permute-done | bytes 1441824 | tf_op jit(solution)/shard_map/ppermute | solution.py:53
  737.9 4.2 collective-permute-start.21
  748.2 20.2 %collective-permute-done.30 = bf16[512,1408]{1,0:T(8,128)(2,1)S(1)} collective-permute-done((bf16[512,1408]{1,0:T(8,128)(2,1)S(1)}, bf16[512,1408]{1,0:T(8,128)(2,1)S(1)}, u32[]{:S(2)}, u32[]{:S(2)}) %collective-permute-start.30) | collective-permute-done | bytes 1441824 | tf_op jit(solution)/shard_map/ppermute | solution.py:53
  768.3 4.9 collective-permute-start.18
  777.8 2.9 add_convert_fusion
  783.5 3.7 collective-permute-start.13
  787.4 9.8 collective-permute-done.17
  798.4 6.2 collective-permute-start.28
  804.6 8.4 collective-permute-start.27
  813.1 11.7 %collective-permute-done.12 = bf16[128,1024]{1,0:T(8,128)(2,1)S(1)} collective-permute-done((bf16[128,1024]{1,0:T(8,128)(2,1)S(1)}, bf16[128,1024]{1,0:T(8,128)(2,1)S(1)}, u32[]{:S(2)}, u32[]{:S(2)}) %collective-permute-start.12) | collective-permute-done | bytes 262176 | tf_op jit(solution)/shard_map/ppermute | solution.py:53
  825.1 3.5 collective-permute-start.48
  829.8 5.8 collective-permute-start.47
  835.6 6.3 collective-permute-done.27
  841.9 10.0 collective-permute-start.46
  851.9 2.8 collective-permute-start.43
  854.9 9.5 collective-permute-start.42
  864.8 15.5 %collective-permute-done.47 = bf16[128,1408]{1,0:T(8,128)(2,1)S(1)} collective-permute-done((bf16[128,1408]{1,0:T(8,128)(2,1)S(1)}, bf16[128,1408]{1,0:T(8,128)(2,1)S(1)}, u32[]{:S(2)}, u32[]{:S(2)}) %collective-permute-start.47) | collective-permute-done | bytes 360480 | tf_op jit(solution)/shard_map/ppermute | solution.py:53
  881.5 3.5 collective-permute-start.38
  885.0 10.4 collective-permute-start.37
  897.6 13.8 %collective-permute-done.42 = bf16[128,1408]{1,0:T(8,128)(2,1)} collective-permute-done((bf16[128,1408]{1,0:T(8,128)(2,1)}, bf16[128,1408]{1,0:T(8,128)(2,1)}, u32[]{:S(2)}, u32[]{:S(2)}) %collective-permute-start.42) | collective-permute-done | bytes 360480 | tf_op jit(solution)/shard_map/ppermute | solution.py:53
  913.8 3.5 collective-permute-start.33
  917.4 9.0 collective-permute-start.32
  926.4 15.9 %collective-permute-done.37 = bf16[128,1408]{1,0:T(8,128)(2,1)} collective-permute-done((bf16[128,1408]{1,0:T(8,128)(2,1)}, bf16[128,1408]{1,0:T(8,128)(2,1)}, u32[]{:S(2)}, u32[]{:S(2)}) %collective-permute-start.37) | collective-permute-done | bytes 360480 | tf_op jit(solution)/shard_map/ppermute | solution.py:53
  946.6 18.7 %collective-permute-done.32 = bf16[128,1408]{1,0:T(8,128)(2,1)S(1)} collective-permute-done((bf16[128,1408]{1,0:T(8,128)(2,1)S(1)}, bf16[128,1408]{1,0:T(8,128)(2,1)S(1)}, u32[]{:S(2)}, u32[]{:S(2)}) %collective-permute-start.32) | collective-permute-done | bytes 360480 | tf_op jit(solution)/shard_map/ppermute | solution.py:53
  976.6 3.8 copy.84
  980.4 6.1 collective-permute-done.53
  986.5 47.1 %collective-permute-done.52 = bf16[128,2816]{1,0:T(8,128)(2,1)S(1)} collective-permute-done((bf16[128,2816]{1,0:T(8,128)(2,1)S(1)}, bf16[128,2816]{1,0:T(8,128)(2,1)S(1)}, u32[]{:S(2)}, u32[]{:S(2)}) %collective-permute-start.52) | collective-permute-done | bytes 720928 | tf_op jit(solution)/shard_map/ppermute | solution.py:53
  1033.5 2.9 fusion.15
  1036.5 2.9 copy.85
  (417 shorter events, 187.6 us)
Async XLA Ops:
  7.2 99.8 %all-gather.8.cloned.1.call-start = ((), (), s32[]{:S(2)}) async-start(), calls=%async_computation.2 | async-start | bytes 18382848 | tf_op jit(solution)/shard_map/all_gather | solution.py:234
  12.6 215.1 %all-gather.6.cloned.1.call-start = ((), (), s32[]{:S(2)}) async-start(), calls=%async_computation | async-start | bytes 24510464 | tf_op jit(solution)/shard_map/all_gather | solution.py:235
  15.4 311.5 %all-gather.10.cloned.1.call-start = ((), (), s32[]{:S(2)}) async-start(), calls=%async_computation.3 | async-start | bytes 12255232 | tf_op jit(solution)/shard_map/all_gather | solution.py:236
  16.1 515.4 %all-reduce.4.cloned.1.call-start = ((), (), s32[]{:S(2)}) async-start(), calls=%async_computation.1 | async-start | bytes 131072 | tf_op jit(solution)/shard_map/psum | solution.py:330
  16.2 15.8 %collective-permute-start = (bf16[128,2048]{1,0:T(8,128)(2,1)S(1)}, bf16[128,2048]{1,0:T(8,128)(2,1)S(1)}, u32[]{:S(2)}, u32[]{:S(2)}) collective-permute-start(bf16[128,2048]{1,0:T(8,128)(2,1)S(1)} %copy-done), channel_id=1, source_target_pairs={{0,1},{1,0},{2,3},{3,2},{4,5},{5,4},{6,7},{7,6},{8,9},{9,8},{10,11... | collective-permute-start | bytes 1572872 | tf_op jit(solution)/shard_map/ppermute | solution.py:129
  19.2 149.4 %collective-permute-start.4 = (bf16[128,2048]{1,0:T(8,128)(2,1)}, bf16[128,2048]{1,0:T(8,128)(2,1)}, u32[]{:S(2)}, u32[]{:S(2)}) collective-permute-start(bf16[128,2048]{1,0:T(8,128)(2,1)} %param.12), channel_id=1, source_target_pairs={{0,1},{1,0},{2,3},{3,2},{4,5},{5,4},{6,7},{7,6},{8,9},{9,8},{10,11... | collective-permute-start | bytes 1572872 | tf_op jit(solution)/shard_map/ppermute | solution.py:129
  149.2 14.2 %collective-permute-start.1 = (bf16[128,2048]{1,0:T(8,128)(2,1)S(1)}, bf16[128,2048]{1,0:T(8,128)(2,1)}, u32[]{:S(2)}, u32[]{:S(2)}) collective-permute-start(bf16[128,2048]{1,0:T(8,128)(2,1)S(1)} %slice.1151), channel_id=1, source_target_pairs={{0,1},{1,0},{2,3},{3,2},{4,5},{5,4},{6,7},{7,6},{8,9},{9,8},{10,11... | collective-permute-start | bytes 1572872 | tf_op jit(solution)/shard_map/ppermute | solution.py:129
  166.5 13.5 %collective-permute-start.2 = (bf16[128,2048]{1,0:T(8,128)(2,1)}, bf16[128,2048]{1,0:T(8,128)(2,1)}, u32[]{:S(2)}, u32[]{:S(2)}) collective-permute-start(bf16[128,2048]{1,0:T(8,128)(2,1)} %add_convert_fusion.5), channel_id=1, source_target_pairs={{0,1},{1,0},{2,3},{3,2},{4,5},{5,4},{6,7},{7,6},{8,9},{9,8},{10,11... | collective-permute-start | bytes 1572872 | tf_op jit(solution)/shard_map/ppermute | solution.py:129
  337.0 43.0 %copy-start.14 = (bf16[256,2816]{1,0:T(8,128)(2,1)}, bf16[256,2816]{1,0:T(8,128)(2,1)S(1)}, u32[]{:S(2)}) copy-start(bf16[256,2816]{1,0:T(8,128)(2,1)S(1)} %get-tuple-element.59) | copy-start | bytes 4325380
  350.3 16.4 %collective-permute-start.5 = (bf16[128,2048]{1,0:T(8,128)(2,1)S(1)}, bf16[128,2048]{1,0:T(8,128)(2,1)S(1)}, u32[]{:S(2)}, u32[]{:S(2)}) collective-permute-start(bf16[128,2048]{1,0:T(8,128)(2,1)S(1)} %slice.1149), channel_id=1, source_target_pairs={{0,1},{1,0},{2,3},{3,2},{4,5},{5,4},{6,7},{7,6},{8,9},{9,8},{10,11... | collective-permute-start | bytes 1572872 | tf_op jit(solution)/shard_map/ppermute | solution.py:129
  358.3 17.3 %collective-permute-start.3 = (bf16[128,2048]{1,0:T(8,128)(2,1)S(1)}, bf16[128,2048]{1,0:T(8,128)(2,1)S(1)}, u32[]{:S(2)}, u32[]{:S(2)}) collective-permute-start(bf16[128,2048]{1,0:T(8,128)(2,1)S(1)} %slice.1150), channel_id=1, source_target_pairs={{0,1},{1,0},{2,3},{3,2},{4,5},{5,4},{6,7},{7,6},{8,9},{9,8},{10,11... | collective-permute-start | bytes 1572872 | tf_op jit(solution)/shard_map/ppermute | solution.py:129
  378.5 13.2 %collective-permute-start.6 = (bf16[128,2048]{1,0:T(8,128)(2,1)S(1)}, bf16[128,2048]{1,0:T(8,128)(2,1)S(1)}, u32[]{:S(2)}, u32[]{:S(2)}) collective-permute-start(bf16[128,2048]{1,0:T(8,128)(2,1)S(1)} %get-tuple-element.50), channel_id=1, source_target_pairs={{0,1},{1,0},{2,3},{3,2},{4,5},{5,4},{6,7},{7,6},{8,9},{9,8},{10,11... | collective-permute-start | bytes 1572872 | tf_op jit(solution)/shard_map/ppermute | solution.py:129
  382.5 157.0 %collective-permute-start.44 = (bf16[1024,1408]{1,0:T(8,128)(2,1)}, bf16[1024,1408]{1,0:T(8,128)(2,1)}, u32[]{:S(2)}, u32[]{:S(2)}) collective-permute-start(bf16[1024,1408]{1,0:T(8,128)(2,1)} %convolution_convert_fusion.1), channel_id=1, source_target_pairs={{0,2},{2,0},{4,6},{6,4},{8,10},{10,8},{12,14},{14,12},{16,18},{18,... | collective-permute-start | bytes 8650760 | tf_op jit(solution)/shard_map/ppermute | solution.py:53
  382.5 159.8 %collective-permute-start.39 = (bf16[1024,1408]{1,0:T(8,128)(2,1)}, bf16[1024,1408]{1,0:T(8,128)(2,1)}, u32[]{:S(2)}, u32[]{:S(2)}) collective-permute-start(bf16[1024,1408]{1,0:T(8,128)(2,1)} %convolution_convert_fusion.2), channel_id=1, source_target_pairs={{0,2},{2,0},{4,6},{6,4},{8,10},{10,8},{12,14},{14,12},{16,18},{18,... | collective-permute-start | bytes 8650760 | tf_op jit(solution)/shard_map/ppermute | solution.py:53
  383.1 159.9 %collective-permute-start.34 = (bf16[1024,1408]{1,0:T(8,128)(2,1)}, bf16[1024,1408]{1,0:T(8,128)(2,1)}, u32[]{:S(2)}, u32[]{:S(2)}) collective-permute-start(bf16[1024,1408]{1,0:T(8,128)(2,1)} %convolution_convert_fusion.3), channel_id=1, source_target_pairs={{0,2},{2,0},{4,6},{6,4},{8,10},{10,8},{12,14},{14,12},{16,18},{18,... | collective-permute-start | bytes 8650760 | tf_op jit(solution)/shard_map/ppermute | solution.py:53
  383.1 168.7 %collective-permute-start.29 = (bf16[1024,1408]{1,0:T(8,128)(2,1)}, bf16[1024,1408]{1,0:T(8,128)(2,1)}, u32[]{:S(2)}, u32[]{:S(2)}) collective-permute-start(bf16[1024,1408]{1,0:T(8,128)(2,1)} %convolution_convert_fusion.4), channel_id=1, source_target_pairs={{0,2},{2,0},{4,6},{6,4},{8,10},{10,8},{12,14},{14,12},{16,18},{18,... | collective-permute-start | bytes 8650760 | tf_op jit(solution)/shard_map/ppermute | solution.py:53
  418.2 25.4 %collective-permute-start.7 = (bf16[128,2048]{1,0:T(8,128)(2,1)}, bf16[128,2048]{1,0:T(8,128)(2,1)}, u32[]{:S(2)}, u32[]{:S(2)}) collective-permute-start(bf16[128,2048]{1,0:T(8,128)(2,1)} %slice.1148), channel_id=1, source_target_pairs={{0,1},{1,0},{2,3},{3,2},{4,5},{5,4},{6,7},{7,6},{8,9},{9,8},{10,11... | collective-permute-start | bytes 1572872 | tf_op jit(solution)/shard_map/ppermute | solution.py:129
  532.2 3.7 collective-permute-start.8
  535.9 14.0 %collective-permute-start.19 = (bf16[1024,1024]{1,0:T(8,128)(2,1)}, bf16[1024,1024]{1,0:T(8,128)(2,1)}, u32[]{:S(2)}, u32[]{:S(2)}) collective-permute-start(bf16[1024,1024]{1,0:T(8,128)(2,1)} %convolution_convert_fusion.6), channel_id=1, source_target_pairs={{0,2},{2,0},{4,6},{6,4},{8,10},{10,8},{12,14},{14,12},{16,18},{18,... | collective-permute-start | bytes 6291464 | tf_op jit(solution)/shard_map/ppermute | solution.py:53
  539.6 15.1 %collective-permute-start.14 = (bf16[1024,1024]{1,0:T(8,128)(2,1)}, bf16[1024,1024]{1,0:T(8,128)(2,1)}, u32[]{:S(2)}, u32[]{:S(2)}) collective-permute-start(bf16[1024,1024]{1,0:T(8,128)(2,1)} %convolution_convert_fusion.7), channel_id=1, source_target_pairs={{0,2},{2,0},{4,6},{6,4},{8,10},{10,8},{12,14},{14,12},{16,18},{18,... | collective-permute-start | bytes 6291464 | tf_op jit(solution)/shard_map/ppermute | solution.py:53
  542.4 15.2 %collective-permute-start.9 = (bf16[1024,1024]{1,0:T(8,128)(2,1)}, bf16[1024,1024]{1,0:T(8,128)(2,1)S(1)}, u32[]{:S(2)}, u32[]{:S(2)}) collective-permute-start(bf16[1024,1024]{1,0:T(8,128)(2,1)} %convolution_convert_fusion.8), channel_id=1, source_target_pairs={{0,2},{2,0},{4,6},{6,4},{8,10},{10,8},{12,14},{14,12},{16,18},{18,... | collective-permute-start | bytes 6291464 | tf_op jit(solution)/shard_map/ppermute | solution.py:53
  543.0 16.0 %collective-permute-start.24 = (bf16[1024,1024]{1,0:T(8,128)(2,1)}, bf16[1024,1024]{1,0:T(8,128)(2,1)S(1)}, u32[]{:S(2)}, u32[]{:S(2)}) collective-permute-start(bf16[1024,1024]{1,0:T(8,128)(2,1)} %convolution_convert_fusion.5), channel_id=1, source_target_pairs={{0,2},{2,0},{4,6},{6,4},{8,10},{10,8},{12,14},{14,12},{16,18},{18,... | collective-permute-start | bytes 6291464 | tf_op jit(solution)/shard_map/ppermute | solution.py:53
  549.9 227.4 %collective-permute-start.49 = (bf16[1024,2816]{1,0:T(8,128)(2,1)}, bf16[1024,2816]{1,0:T(8,128)(2,1)S(1)}, u32[]{:S(2)}, u32[]{:S(2)}) collective-permute-start(bf16[1024,2816]{1,0:T(8,128)(2,1)} %convolution_convert_fusion), channel_id=1, source_target_pairs={{0,2},{2,0},{4,6},{6,4},{8,10},{10,8},{12,14},{14,12},{16,18},{18,... | collective-permute-start | bytes 17301512 | tf_op jit(solution)/shard_map/ppermute | solution.py:53
  551.7 26.1 %collective-permute-start.20 = (bf16[512,1024]{1,0:T(8,128)(2,1)S(1)}, bf16[512,1024]{1,0:T(8,128)(2,1)S(1)}, u32[]{:S(2)}, u32[]{:S(2)}) collective-permute-start(bf16[512,1024]{1,0:T(8,128)(2,1)S(1)} %add_convert_fusion.2), channel_id=1, source_target_pairs={{0,4},{2,6},{4,0},{6,2},{8,12},{10,14},{12,8},{14,10},{16,20},{18,... | collective-permute-start | bytes 3145736 | tf_op jit(solution)/shard_map/ppermute | solution.py:53
  554.6 154.2 %collective-permute-start.45 = (bf16[512,1408]{1,0:T(8,128)(2,1)S(1)}, bf16[512,1408]{1,0:T(8,128)(2,1)S(1)}, u32[]{:S(2)}, u32[]{:S(2)}) collective-permute-start(bf16[512,1408]{1,0:T(8,128)(2,1)S(1)} %fusion.23), channel_id=1, source_target_pairs={{0,4},{2,6},{4,0},{6,2},{8,12},{10,14},{12,8},{14,10},{16,20},{18,... | collective-permute-start | bytes 4325384 | tf_op jit(solution)/shard_map/ppermute | solution.py:53
  557.6 159.7 %collective-permute-start.40 = (bf16[512,1408]{1,0:T(8,128)(2,1)S(1)}, bf16[512,1408]{1,0:T(8,128)(2,1)S(1)}, u32[]{:S(2)}, u32[]{:S(2)}) collective-permute-start(bf16[512,1408]{1,0:T(8,128)(2,1)S(1)} %fusion.22), channel_id=1, source_target_pairs={{0,4},{2,6},{4,0},{6,2},{8,12},{10,14},{12,8},{14,10},{16,20},{18,... | collective-permute-start | bytes 4325384 | tf_op jit(solution)/shard_map/ppermute | solution.py:53
  559.0 103.1 %collective-permute-start.15 = (bf16[512,1024]{1,0:T(8,128)(2,1)S(1)}, bf16[512,1024]{1,0:T(8,128)(2,1)S(1)}, u32[]{:S(2)}, u32[]{:S(2)}) collective-permute-start(bf16[512,1024]{1,0:T(8,128)(2,1)S(1)} %add_convert_fusion.3), channel_id=1, source_target_pairs={{0,4},{2,6},{4,0},{6,2},{8,12},{10,14},{12,8},{14,10},{16,20},{18,... | collective-permute-start | bytes 3145736 | tf_op jit(solution)/shard_map/ppermute | solution.py:53
  577.8 106.7 %collective-permute-start.10 = (bf16[512,1024]{1,0:T(8,128)(2,1)S(1)}, bf16[512,1024]{1,0:T(8,128)(2,1)S(1)}, u32[]{:S(2)}, u32[]{:S(2)}) collective-permute-start(bf16[512,1024]{1,0:T(8,128)(2,1)S(1)} %add_convert_fusion.4), channel_id=1, source_target_pairs={{0,4},{2,6},{4,0},{6,2},{8,12},{10,14},{12,8},{14,10},{16,20},{18,... | collective-permute-start | bytes 3145736 | tf_op jit(solution)/shard_map/ppermute | solution.py:53
  662.1 44.9 %collective-permute-start.25 = (bf16[512,1024]{1,0:T(8,128)(2,1)S(1)}, bf16[512,1024]{1,0:T(8,128)(2,1)S(1)}, u32[]{:S(2)}, u32[]{:S(2)}) collective-permute-start(bf16[512,1024]{1,0:T(8,128)(2,1)S(1)} %add_convert_fusion.1), channel_id=1, source_target_pairs={{0,4},{2,6},{4,0},{6,2},{8,12},{10,14},{12,8},{14,10},{16,20},{18,... | collective-permute-start | bytes 3145736 | tf_op jit(solution)/shard_map/ppermute | solution.py:53
  684.6 53.4 %collective-permute-start.35 = (bf16[512,1408]{1,0:T(8,128)(2,1)S(1)}, bf16[512,1408]{1,0:T(8,128)(2,1)S(1)}, u32[]{:S(2)}, u32[]{:S(2)}) collective-permute-start(bf16[512,1408]{1,0:T(8,128)(2,1)S(1)} %fusion.21), channel_id=1, source_target_pairs={{0,4},{2,6},{4,0},{6,2},{8,12},{10,14},{12,8},{14,10},{16,20},{18,... | collective-permute-start | bytes 4325384 | tf_op jit(solution)/shard_map/ppermute | solution.py:53
  707.0 61.3 %collective-permute-start.30 = (bf16[512,1408]{1,0:T(8,128)(2,1)S(1)}, bf16[512,1408]{1,0:T(8,128)(2,1)S(1)}, u32[]{:S(2)}, u32[]{:S(2)}) collective-permute-start(bf16[512,1408]{1,0:T(8,128)(2,1)S(1)} %fusion.20), channel_id=1, source_target_pairs={{0,4},{2,6},{4,0},{6,2},{8,12},{10,14},{12,8},{14,10},{16,20},{18,... | collective-permute-start | bytes 4325384 | tf_op jit(solution)/shard_map/ppermute | solution.py:53
  708.9 71.9 %collective-permute-start.23 = (bf16[128,1024]{1,0:T(8,128)(2,1)S(1)}, bf16[128,1024]{1,0:T(8,128)(2,1)S(1)}, u32[]{:S(2)}, u32[]{:S(2)}) collective-permute-start(bf16[128,1024]{1,0:T(8,128)(2,1)S(1)} %add_convert_fusion.6), channel_id=1, source_target_pairs={{0,24},{2,26},{4,28},{6,30},{8,0},{10,2},{12,4},{14,6},{16,8},{18,... | collective-permute-start | bytes 786440 | tf_op jit(solution)/shard_map/ppermute | solution.py:53
  717.3 66.1 %collective-permute-start.22 = (bf16[128,1024]{1,0:T(8,128)(2,1)S(1)}, bf16[128,1024]{1,0:T(8,128)(2,1)S(1)}, u32[]{:S(2)}, u32[]{:S(2)}) collective-permute-start(bf16[128,1024]{1,0:T(8,128)(2,1)S(1)} %add_convert_fusion.7), channel_id=1, source_target_pairs={{0,16},{2,18},{4,20},{6,22},{8,24},{10,26},{12,28},{14,30},{16,0},... | collective-permute-start | bytes 786440 | tf_op jit(solution)/shard_map/ppermute | solution.py:53
  737.9 45.6 %collective-permute-start.21 = (bf16[128,1024]{1,0:T(8,128)(2,1)S(1)}, bf16[128,1024]{1,0:T(8,128)(2,1)S(1)}, u32[]{:S(2)}, u32[]{:S(2)}) collective-permute-start(bf16[128,1024]{1,0:T(8,128)(2,1)S(1)} %add_convert_fusion.8), channel_id=1, source_target_pairs={{0,8},{2,10},{4,12},{6,14},{8,16},{10,18},{12,20},{14,22},{16,24},... | collective-permute-start | bytes 786440 | tf_op jit(solution)/shard_map/ppermute | solution.py:53
  768.3 18.9 %collective-permute-start.18 = (bf16[128,1024]{1,0:T(8,128)(2,1)S(1)}, bf16[128,1024]{1,0:T(8,128)(2,1)S(1)}, u32[]{:S(2)}, u32[]{:S(2)}) collective-permute-start(bf16[128,1024]{1,0:T(8,128)(2,1)S(1)} %add_convert_fusion.9), channel_id=1, source_target_pairs={{0,24},{2,26},{4,28},{6,30},{8,0},{10,2},{12,4},{14,6},{16,8},{18,... | collective-permute-start | bytes 786440 | tf_op jit(solution)/shard_map/ppermute | solution.py:53
  777.3 19.9 %collective-permute-start.17 = (bf16[128,1024]{1,0:T(8,128)(2,1)S(1)}, bf16[128,1024]{1,0:T(8,128)(2,1)S(1)}, u32[]{:S(2)}, u32[]{:S(2)}) collective-permute-start(bf16[128,1024]{1,0:T(8,128)(2,1)S(1)} %add_convert_fusion.10), channel_id=1, source_target_pairs={{0,16},{2,18},{4,20},{6,22},{8,24},{10,26},{12,28},{14,30},{16,0},... | collective-permute-start | bytes 786440 | tf_op jit(solution)/shard_map/ppermute | solution.py:53
  780.8 47.9 %copy-start.32 = (f32[128,1024]{1,0:T(8,128)S(1)}, f32[128,1024]{1,0:T(8,128)}, u32[]{:S(2)}) copy-start(f32[128,1024]{1,0:T(8,128)} %fusion.203) | copy-start | bytes 1572868
  780.8 186.1 %collective-permute-start.50 = (bf16[512,2816]{1,0:T(8,128)(2,1)}, bf16[512,2816]{1,0:T(8,128)(2,1)}, u32[]{:S(2)}, u32[]{:S(2)}) collective-permute-start(bf16[512,2816]{1,0:T(8,128)(2,1)} %add_convert_fusion), channel_id=1, source_target_pairs={{0,4},{2,6},{4,0},{6,2},{8,12},{10,14},{12,8},{14,10},{16,20},{18,... | collective-permute-start | bytes 8650760 | tf_op jit(solution)/shard_map/ppermute | solution.py:53
  783.4 71.3 %copy-start.33 = (f32[128,1024]{1,0:T(8,128)S(1)}, f32[128,1024]{1,0:T(8,128)}, u32[]{:S(2)}) copy-start(f32[128,1024]{1,0:T(8,128)} %fusion.205) | copy-start | bytes 1572868
  783.4 15.0 %collective-permute-start.16 = (bf16[128,1024]{1,0:T(8,128)(2,1)S(1)}, bf16[128,1024]{1,0:T(8,128)(2,1)S(1)}, u32[]{:S(2)}, u32[]{:S(2)}) collective-permute-start(bf16[128,1024]{1,0:T(8,128)(2,1)S(1)} %add_convert_fusion.11), channel_id=1, source_target_pairs={{0,8},{2,10},{4,12},{6,14},{8,16},{10,18},{12,20},{14,22},{16,24},... | collective-permute-start | bytes 786440 | tf_op jit(solution)/shard_map/ppermute | solution.py:53
  783.5 21.1 %collective-permute-start.13 = (bf16[128,1024]{1,0:T(8,128)(2,1)S(1)}, bf16[128,1024]{1,0:T(8,128)(2,1)S(1)}, u32[]{:S(2)}, u32[]{:S(2)}) collective-permute-start(bf16[128,1024]{1,0:T(8,128)(2,1)S(1)} %add_convert_fusion.12), channel_id=1, source_target_pairs={{0,24},{2,26},{4,28},{6,30},{8,0},{10,2},{12,4},{14,6},{16,8},{18,... | collective-permute-start | bytes 786440 | tf_op jit(solution)/shard_map/ppermute | solution.py:53
  787.2 37.6 %collective-permute-start.12 = (bf16[128,1024]{1,0:T(8,128)(2,1)S(1)}, bf16[128,1024]{1,0:T(8,128)(2,1)S(1)}, u32[]{:S(2)}, u32[]{:S(2)}) collective-permute-start(bf16[128,1024]{1,0:T(8,128)(2,1)S(1)} %add_convert_fusion.13), channel_id=1, source_target_pairs={{0,16},{2,18},{4,20},{6,22},{8,24},{10,26},{12,28},{14,30},{16,0},... | collective-permute-start | bytes 786440 | tf_op jit(solution)/shard_map/ppermute | solution.py:53
  797.2 27.9 %collective-permute-start.11 = (bf16[128,1024]{1,0:T(8,128)(2,1)S(1)}, bf16[128,1024]{1,0:T(8,128)(2,1)S(1)}, u32[]{:S(2)}, u32[]{:S(2)}) collective-permute-start(bf16[128,1024]{1,0:T(8,128)(2,1)S(1)} %add_convert_fusion.14), channel_id=1, source_target_pairs={{0,8},{2,10},{4,12},{6,14},{8,16},{10,18},{12,20},{14,22},{16,24},... | collective-permute-start | bytes 786440 | tf_op jit(solution)/shard_map/ppermute | solution.py:53
  798.4 31.4 %collective-permute-start.28 = (bf16[128,1024]{1,0:T(8,128)(2,1)S(1)}, bf16[128,1024]{1,0:T(8,128)(2,1)S(1)}, u32[]{:S(2)}, u32[]{:S(2)}) collective-permute-start(bf16[128,1024]{1,0:T(8,128)(2,1)S(1)} %fusion.88), channel_id=1, source_target_pairs={{0,24},{2,26},{4,28},{6,30},{8,0},{10,2},{12,4},{14,6},{16,8},{18,... | collective-permute-start | bytes 786440 | tf_op jit(solution)/shard_map/ppermute | solution.py:53
  804.6 37.3 %collective-permute-start.27 = (bf16[128,1024]{1,0:T(8,128)(2,1)S(1)}, bf16[128,1024]{1,0:T(8,128)(2,1)S(1)}, u32[]{:S(2)}, u32[]{:S(2)}) collective-permute-start(bf16[128,1024]{1,0:T(8,128)(2,1)S(1)} %fusion.87), channel_id=1, source_target_pairs={{0,16},{2,18},{4,20},{6,22},{8,24},{10,26},{12,28},{14,30},{16,0},... | collective-permute-start | bytes 786440 | tf_op jit(solution)/shard_map/ppermute | solution.py:53
  824.8 27.1 %collective-permute-start.26 = (bf16[128,1024]{1,0:T(8,128)(2,1)S(1)}, bf16[128,1024]{1,0:T(8,128)(2,1)S(1)}, u32[]{:S(2)}, u32[]{:S(2)}) collective-permute-start(bf16[128,1024]{1,0:T(8,128)(2,1)S(1)} %fusion.86), channel_id=1, source_target_pairs={{0,8},{2,10},{4,12},{6,14},{8,16},{10,18},{12,20},{14,22},{16,24},... | collective-permute-start | bytes 786440 | tf_op jit(solution)/shard_map/ppermute | solution.py:53
  825.1 29.8 %collective-permute-start.48 = (bf16[128,1408]{1,0:T(8,128)(2,1)S(1)}, bf16[128,1408]{1,0:T(8,128)(2,1)S(1)}, u32[]{:S(2)}, u32[]{:S(2)}) collective-permute-start(bf16[128,1408]{1,0:T(8,128)(2,1)S(1)} %fusion.56), channel_id=1, source_target_pairs={{0,24},{2,26},{4,28},{6,30},{8,0},{10,2},{12,4},{14,6},{16,8},{18,... | collective-permute-start | bytes 1081352 | tf_op jit(solution)/shard_map/ppermute | solution.py:53
  829.8 50.5 %collective-permute-start.47 = (bf16[128,1408]{1,0:T(8,128)(2,1)S(1)}, bf16[128,1408]{1,0:T(8,128)(2,1)S(1)}, u32[]{:S(2)}, u32[]{:S(2)}) collective-permute-start(bf16[128,1408]{1,0:T(8,128)(2,1)S(1)} %fusion.57), channel_id=1, source_target_pairs={{0,16},{2,18},{4,20},{6,22},{8,24},{10,26},{12,28},{14,30},{16,0},... | collective-permute-start | bytes 1081352 | tf_op jit(solution)/shard_map/ppermute | solution.py:53
  841.9 39.6 %collective-permute-start.46 = (bf16[128,1408]{1,0:T(8,128)(2,1)S(1)}, bf16[128,1408]{1,0:T(8,128)(2,1)}, u32[]{:S(2)}, u32[]{:S(2)}) collective-permute-start(bf16[128,1408]{1,0:T(8,128)(2,1)S(1)} %fusion.58), channel_id=1, source_target_pairs={{0,8},{2,10},{4,12},{6,14},{8,16},{10,18},{12,20},{14,22},{16,24},... | collective-permute-start | bytes 1081352 | tf_op jit(solution)/shard_map/ppermute | solution.py:53
  851.9 33.1 %collective-permute-start.43 = (bf16[128,1408]{1,0:T(8,128)(2,1)S(1)}, bf16[128,1408]{1,0:T(8,128)(2,1)}, u32[]{:S(2)}, u32[]{:S(2)}) collective-permute-start(bf16[128,1408]{1,0:T(8,128)(2,1)S(1)} %fusion.59), channel_id=1, source_target_pairs={{0,24},{2,26},{4,28},{6,30},{8,0},{10,2},{12,4},{14,6},{16,8},{18,... | collective-permute-start | bytes 1081352 | tf_op jit(solution)/shard_map/ppermute | solution.py:53
  854.9 56.5 %collective-permute-start.42 = (bf16[128,1408]{1,0:T(8,128)(2,1)}, bf16[128,1408]{1,0:T(8,128)(2,1)}, u32[]{:S(2)}, u32[]{:S(2)}) collective-permute-start(bf16[128,1408]{1,0:T(8,128)(2,1)} %fusion.60), channel_id=1, source_target_pairs={{0,16},{2,18},{4,20},{6,22},{8,24},{10,26},{12,28},{14,30},{16,0},... | collective-permute-start | bytes 1081352 | tf_op jit(solution)/shard_map/ppermute | solution.py:53
  881.1 32.7 %collective-permute-start.41 = (bf16[128,1408]{1,0:T(8,128)(2,1)}, bf16[128,1408]{1,0:T(8,128)(2,1)}, u32[]{:S(2)}, u32[]{:S(2)}) collective-permute-start(bf16[128,1408]{1,0:T(8,128)(2,1)} %fusion.61), channel_id=1, source_target_pairs={{0,8},{2,10},{4,12},{6,14},{8,16},{10,18},{12,20},{14,22},{16,24},... | collective-permute-start | bytes 1081352 | tf_op jit(solution)/shard_map/ppermute | solution.py:53
  881.5 35.9 %collective-permute-start.38 = (bf16[128,1408]{1,0:T(8,128)(2,1)}, bf16[128,1408]{1,0:T(8,128)(2,1)}, u32[]{:S(2)}, u32[]{:S(2)}) collective-permute-start(bf16[128,1408]{1,0:T(8,128)(2,1)} %fusion.62), channel_id=1, source_target_pairs={{0,24},{2,26},{4,28},{6,30},{8,0},{10,2},{12,4},{14,6},{16,8},{18,... | collective-permute-start | bytes 1081352 | tf_op jit(solution)/shard_map/ppermute | solution.py:53
  885.0 57.4 %collective-permute-start.37 = (bf16[128,1408]{1,0:T(8,128)(2,1)}, bf16[128,1408]{1,0:T(8,128)(2,1)}, u32[]{:S(2)}, u32[]{:S(2)}) collective-permute-start(bf16[128,1408]{1,0:T(8,128)(2,1)} %fusion.63), channel_id=1, source_target_pairs={{0,16},{2,18},{4,20},{6,22},{8,24},{10,26},{12,28},{14,30},{16,0},... | collective-permute-start | bytes 1081352 | tf_op jit(solution)/shard_map/ppermute | solution.py:53
  897.6 44.8 %copy-start.82 = (bf16[128,1408]{1,0:T(8,128)(2,1)S(1)}, bf16[128,1408]{1,0:T(8,128)(2,1)}, u32[]{:S(2)}) copy-start(bf16[128,1408]{1,0:T(8,128)(2,1)} %fusion.67) | copy-start | bytes 1081348
  897.6 45.1 %copy-start.19 = (bf16[256,2816]{1,0:T(8,128)(2,1)S(1)}, bf16[256,2816]{1,0:T(8,128)(2,1)}, u32[]{:S(2)}) copy-start(bf16[256,2816]{1,0:T(8,128)(2,1)} %copy-done.17) | copy-start | bytes 4325380
  911.4 33.3 %collective-permute-start.36 = (bf16[128,1408]{1,0:T(8,128)(2,1)}, bf16[128,1408]{1,0:T(8,128)(2,1)S(1)}, u32[]{:S(2)}, u32[]{:S(2)}) collective-permute-start(bf16[128,1408]{1,0:T(8,128)(2,1)} %fusion.64), channel_id=1, source_target_pairs={{0,8},{2,10},{4,12},{6,14},{8,16},{10,18},{12,20},{14,22},{16,24},... | collective-permute-start | bytes 1081352 | tf_op jit(solution)/shard_map/ppermute | solution.py:53
  913.8 30.9 %copy-start.16 = (bf16[256,2816]{1,0:T(8,128)(2,1)S(1)}, bf16[256,2816]{1,0:T(8,128)(2,1)}, u32[]{:S(2)}) copy-start(bf16[256,2816]{1,0:T(8,128)(2,1)} %copy-done.14) | copy-start | bytes 4325380
  913.8 32.7 %collective-permute-start.33 = (bf16[128,1408]{1,0:T(8,128)(2,1)S(1)}, bf16[128,1408]{1,0:T(8,128)(2,1)S(1)}, u32[]{:S(2)}, u32[]{:S(2)}) collective-permute-start(bf16[128,1408]{1,0:T(8,128)(2,1)S(1)} %copy-done.81), channel_id=1, source_target_pairs={{0,24},{2,26},{4,28},{6,30},{8,0},{10,2},{12,4},{14,6},{16,8},{18,... | collective-permute-start | bytes 1081352 | tf_op jit(solution)/shard_map/ppermute | solution.py:53
  917.4 47.9 %collective-permute-start.32 = (bf16[128,1408]{1,0:T(8,128)(2,1)S(1)}, bf16[128,1408]{1,0:T(8,128)(2,1)S(1)}, u32[]{:S(2)}, u32[]{:S(2)}) collective-permute-start(bf16[128,1408]{1,0:T(8,128)(2,1)S(1)} %copy-done.80), channel_id=1, source_target_pairs={{0,16},{2,18},{4,20},{6,22},{8,24},{10,26},{12,28},{14,30},{16,0},... | collective-permute-start | bytes 1081352 | tf_op jit(solution)/shard_map/ppermute | solution.py:53
  942.4 22.9 %collective-permute-start.31 = (bf16[128,1408]{1,0:T(8,128)(2,1)S(1)}, bf16[128,1408]{1,0:T(8,128)(2,1)S(1)}, u32[]{:S(2)}, u32[]{:S(2)}) collective-permute-start(bf16[128,1408]{1,0:T(8,128)(2,1)S(1)} %copy-done.82), channel_id=1, source_target_pairs={{0,8},{2,10},{4,12},{6,14},{8,16},{10,18},{12,20},{14,22},{16,24},... | collective-permute-start | bytes 1081352 | tf_op jit(solution)/shard_map/ppermute | solution.py:53
  968.4 18.0 %collective-permute-start.53 = (bf16[128,2816]{1,0:T(8,128)(2,1)S(1)}, bf16[128,2816]{1,0:T(8,128)(2,1)S(1)}, u32[]{:S(2)}, u32[]{:S(2)}) collective-permute-start(bf16[128,2816]{1,0:T(8,128)(2,1)S(1)} %fusion.17), channel_id=1, source_target_pairs={{0,24},{2,26},{4,28},{6,30},{8,0},{10,2},{12,4},{14,6},{16,8},{18,... | collective-permute-start | bytes 2162696 | tf_op jit(solution)/shard_map/ppermute | solution.py:53
  970.0 63.5 %collective-permute-start.52 = (bf16[128,2816]{1,0:T(8,128)(2,1)S(1)}, bf16[128,2816]{1,0:T(8,128)(2,1)S(1)}, u32[]{:S(2)}, u32[]{:S(2)}) collective-permute-start(bf16[128,2816]{1,0:T(8,128)(2,1)S(1)} %fusion.18), channel_id=1, source_target_pairs={{0,16},{2,18},{4,20},{6,22},{8,24},{10,26},{12,28},{14,30},{16,0},... | collective-permute-start | bytes 2162696 | tf_op jit(solution)/shard_map/ppermute | solution.py:53
  974.0 59.6 %collective-permute-start.51 = (bf16[128,2816]{1,0:T(8,128)(2,1)S(1)}, bf16[128,2816]{1,0:T(8,128)(2,1)S(1)}, u32[]{:S(2)}, u32[]{:S(2)}) collective-permute-start(bf16[128,2816]{1,0:T(8,128)(2,1)S(1)} %fusion.19), channel_id=1, source_target_pairs={{0,8},{2,10},{4,12},{6,14},{8,16},{10,18},{12,20},{14,22},{16,24},... | collective-permute-start | bytes 2162696 | tf_op jit(solution)/shard_map/ppermute | solution.py:53
  (80 other events, 493.9 us)
Sparse Core Ops, SparseCore 0:
  12.7 94.1 all-gather.7
  109.1 118.6 all-gather.5
  229.9 96.8 all-gather.9
  448.0 83.4 all-reduce.3
where the time goes:
time: 1050 us
  waiting for transfers between devices  631 us (60%)
  matrix products  166 us (16%)
  starting transfers between devices  121 us (12%)
  local copies, waits for them, and re-layouts  63.7 us (6%)
  other arithmetic  32.6 us (3%)
  Pallas kernels  16.3 us (2%)
  between operations  15.7 us (1%)
    ppermute x45, waiting for transfers between devices, shift(): return lax.ppermute(rows, 'fsdp', self.moves(**by))  315 us
    dot_general x61, matrix products, times(): lax.dot_general(left, right, (((1,), (0,)), ((), ())), preferred_element_...  128 us
    ppermute x45, starting transfers between devices, shift(): return lax.ppermute(rows, 'fsdp', self.moves(**by))  108 us
    psum x1, waiting for transfers between devices, shards(): terms = lax.psum(terms, 'fsdp')  81.7 us
    all_gather x1, waiting for transfers between devices, shards(): w_down = lax.all_gather(down_weight[0], 'fsdp', axis=1, tiled=True)  81.2 us
    all_gather x1, waiting for transfers between devices, shards(): packs = lax.all_gather(pack, 'fsdp', axis=0)  74.4 us
    all_gather x1, waiting for transfers between devices, shards(): lax.all_gather(jnp.swapaxes(gate_up_weight[0], 0, 1), 'fsdp', axis=1, til...  41.3 us
    ppermute x9, waiting for transfers between devices, other(): return lax.ppermute(rows, 'tp', [(0, 1), (1, 0)])  36.6 us
  transfers between devices with their start and end apart: 58, of which 25 were waited for; matrix products, arithmetic and copies ran while one was open for 20% of the time, Pallas kernels for 2%

commit v1 on v0

--- a/solution.py
+++ b/solution.py
@@ -52,6 +52,20 @@
     def shift(self, rows, **by):
         return lax.ppermute(rows, "fsdp", self.moves(**by))
 
+    def across(self, slow, step):
+        return slow ^ step if self.slow == 4 else (slow + step) % self.slow
+
+    def cross(self, rows, step, ends=True, inner=True):
+        moves = []
+        for s in range(self.slow):
+            if ends if s in (0, self.slow - 1) else inner:
+                moves += [
+                    (self.place(s, m, c), self.place(self.across(s, step), m, c))
+                    for m in range(self.mid)
+                    for c in range(self.cores)
+                ]
+        return lax.ppermute(rows, "fsdp", moves)
+
     def order(self):
         here = lax.axis_index("fsdp")
         core = here % self.cores
@@ -60,7 +74,7 @@
         step = jnp.arange(self.count, dtype=jnp.int32)
         core = (core + step // (self.mid * self.slow)) % self.cores
         mid = (mid + (step // self.slow) % self.mid) % self.mid
-        slow = (slow + step % self.slow) % self.slow
+        slow = self.across(slow, step % self.slow)
         return ((slow * self.mid + mid) * self.cores + core).astype(jnp.int32)
 
 
@@ -94,7 +108,7 @@
     )(order, rows)
 
 
-def scatter_product(grid, left, right):
+def scatter_product(grid, left, right, relay=False):
     block = left.shape[0] // grid.count
     per_mid = block * grid.slow
     per_core = per_mid * grid.mid
@@ -109,17 +123,30 @@
             part = part + got[m * per_mid : (m + 1) * per_mid].astype(F32)
         part = part.astype(BF16)
         from_mid.append(grid.shift(part, mid=m))
-    from_slow = []
-    for s in range(grid.slow):
-        span = slice(s * block, (s + 1) * block)
+
+    def part_of(span):
         part = times(left[span], right)
         for got in from_core + from_mid:
             part = part + got[span].astype(F32)
-        if s == 0:
-            total = part
-            continue
-        part = part.astype(BF16)
-        from_slow.append(grid.shift(part, slow=s))
+        return part
+
+    total = part_of(slice(0, block))
+    from_slow = []
+    if relay and grid.slow == 4:
+        mine = part_of(slice(block, 4 * block)).astype(BF16)
+        got = grid.cross(mine, 1, inner=False)
+        near, far, over = (slice(i * block, (i + 1) * block) for i in range(3))
+        from_slow.append(got[near])
+        sums = {
+            1: mine[near],
+            2: (mine[far].astype(F32) + got[over].astype(F32)).astype(BF16),
+            3: (mine[over].astype(F32) + got[far].astype(F32)).astype(BF16),
+        }
+        from_slow += [grid.cross(rows, s, ends=False) for s, rows in sums.items()]
+    else:
+        for s in range(1, grid.slow):
+            part = part_of(slice(s * block, (s + 1) * block)).astype(BF16)
+            from_slow.append(grid.cross(part, s))
     for got in from_slow:
         total = total + got.astype(F32)
     return total
@@ -279,9 +306,7 @@
     hidden = (gate * sigma * upper).astype(BF16)
     gate, upper, hidden = lax.optimization_barrier((gate, upper, hidden))
     sigma = jax.nn.sigmoid(gate)
-    down_grad = scatter_product(grid, down_cot_t, hidden)
-    resid_three = resid_two + collect(times(hidden, w_down))
-    block_output = resid_three.astype(BF16)
+    down_grad = scatter_product(grid, down_cot_t, hidden, relay=True)
 
     grad_three = cotangent.astype(F32)
     grad_hidden = times_transposed(down_cot, w_down)
@@ -291,7 +316,10 @@
     half = grad_gate.shape[1] // 2
     gate_grad, up_grad = (
         jnp.concatenate(
-            [scatter_product(grid, mlp_in_t, grad[:, :half]), scatter_product(grid, mlp_in_t, grad[:, half:])],
+            [
+                scatter_product(grid, mlp_in_t, grad[:, :half], relay=True),
+                scatter_product(grid, mlp_in_t, grad[:, half:], relay=True),
+            ],
             axis=1,
         )
         for grad in (grad_gate, grad_up)
@@ -300,6 +328,9 @@
     grad_norm_two, gain_two, shift_two = norm_backward(grad_mlp_in, normed_two, inv_two, gains[1])
     grad_two = grad_three + grad_norm_two
     attn_cot = pair(grad_two.astype(BF16))
+    attn_cot, hidden_late = lax.optimization_barrier((attn_cot, hidden))
+    resid_three = resid_two + collect(times(hidden_late, w_down))
+    block_output = resid_three.astype(BF16)
     grad_mixed = times(attn_cot, w_out_t).astype(BF16).reshape(mixed.shape)
     out_grad = scatter_product(grid, turned(attn_cot, order), mixed_flat)
     grad_queries, grad_keys, grad_values = attend_back(
@@ -320,6 +351,7 @@
     grad_norm_one, gain_one, shift_one = norm_backward(grad_attn_in, normed_one, inv_one, gains[0])
     input_grad = (grad_two + grad_norm_one).astype(BF16)
 
+    gate_up_grad = jnp.stack([gate_grad, up_grad], axis=1)[None]
     norm_terms = jnp.stack([gain_one, gain_two, shift_one, shift_two])
     norm_terms = jnp.swapaxes(norm_terms.reshape(4, count, block), 0, 1).reshape(count, 4 * block)
     bias_terms = jnp.transpose(bias_terms.reshape(3, heads, count, piece), (2, 0, 1, 3)).reshape(count, -1)
@@ -340,7 +372,7 @@
         jnp.stack([q_grad, k_grad, v_grad], axis=1)[None],
         bias_part[None],
         out_grad.T[None],
-        jnp.stack([gate_grad, up_grad], axis=1)[None],
+        gate_up_grad,
         down_grad.T[None],
     )
 

time: 1050 us -> 1010 us (0.962)
  starting transfers between devices: 121 us -> 81.7 us
    ppermute x0 -> x32, waiting for transfers between devices: none -> 150 us  [cross(): return lax.ppermute(rows, 'fsdp', moves)]
    ppermute x45 -> x18, waiting for transfers between devices: 315 us -> 165 us  [shift(): return lax.ppermute(rows, 'fsdp', self.moves(**by))]
    ppermute x45 -> x18, starting transfers between devices: 108 us -> 10.2 us  [shift(): return lax.ppermute(rows, 'fsdp', self.moves(**by))]
    ppermute x0 -> x32, starting transfers between devices: none -> 58.6 us  [cross(): return lax.ppermute(rows, 'fsdp', moves)]
    dot_general x61 -> x51, matrix products: 128 us -> 123 us  [times(): lax.dot_general(left, right, (((1,), (0,)), ((), ())), preferred_element_...]
    unnamed x186 -> x208, local copies, waits for them, and re-layouts: 30.4 us -> 28.7 us
  transfers between devices with their start and end apart: 58 -> 63, of which waited for: 25 -> 33; matrix products, arithmetic and copies ran while one was open for 20% -> 20% of each run, Pallas kernels for 2% -> 2%
where the time goes in v1:
time: 1010 us; the launch traced here: 1000 us
  waiting for transfers between devices  637 us (63%)
  matrix products  163 us (16%)
  starting transfers between devices  81.7 us (8%)
  local copies, waits for them, and re-layouts  59 us (6%)
  other arithmetic  30.5 us (3%)
  Pallas kernels  16.3 us (2%)
  between operations  16.1 us (2%)
    ppermute x18, waiting for transfers between devices, shift(): return lax.ppermute(rows, 'fsdp', self.moves(**by))  165 us
    ppermute x32, waiting for transfers between devices, cross(): return lax.ppermute(rows, 'fsdp', moves)  150 us
    dot_general x51, matrix products, times(): lax.dot_general(left, right, (((1,), (0,)), ((), ())), preferred_element_...  123 us
    psum x1, waiting for transfers between devices, shards(): terms = lax.psum(terms, 'fsdp')  84.7 us
    all_gather x1, waiting for transfers between devices, shards(): w_down = lax.all_gather(down_weight[0], 'fsdp', axis=1, tiled=True)  81.1 us
    all_gather x1, waiting for transfers between devices, shards(): packs = lax.all_gather(pack, 'fsdp', axis=0)  74.4 us
    ppermute x32, starting transfers between devices, cross(): return lax.ppermute(rows, 'fsdp', moves)  58.6 us
    all_gather x1, waiting for transfers between devices, shards(): lax.all_gather(jnp.swapaxes(gate_up_weight[0], 0, 1), 'fsdp', axis=1, til...  42 us
  transfers between devices with their start and end apart: 63, of which 33 were waited for; matrix products, arithmetic and copies ran while one was open for 20% of the time, Pallas kernels for 2%

profile of v1, /device:TPU:0, one launch (start us, length us, event | category | flops | bytes accessed | tf_op | source)
XLA Modules:
  0.0 1003.9 jit_solution(7686023690777792694)
XLA Ops:
  12.7 2.6 copy.95
  16.2 3.0 collective-permute-start
  20.8 11.1 %collective-permute-done = bf16[128,2048]{1,0:T(8,128)(2,1)S(1)} collective-permute-done((bf16[128,2048]{1,0:T(8,128)(2,1)S(1)}, bf16[128,2048]{1,0:T(8,128)(2,1)S(1)}, u32[]{:S(2)}, u32[]{:S(2)}) %collective-permute-start) | collective-permute-done | bytes 524320 | tf_op jit(solution)/shard_map/ppermute | solution.py:156
  32.6 74.4 %all-gather.8.cloned.1.call-done = bf16[8448,1024]{1,0:T(8,128)(2,1)} async-done(((bf16[528,1024]{1,0:T(8,128)(2,1)}), bf16[8448,1024]{1,0:T(8,128)(2,1)}) %all-gather.8.cloned.1.call-update) | async-done | bytes 17301520 | tf_op jit(solution)/shard_map/all_gather | solution.py:261
  109.9 11.5 %fusion.220 = (bf16[16,128,1024]{2,1,0:T(8,128)(2,1)}, bf16[16,128,1024]{2,1,0:T(8,128)(2,1)}, bf16[16,128,1024]{2,1,0:T(8,128)(2,1)}, bf16[16,128,1024]{2,1,0:T(8,128)(2,1)S(1)}) fusion(bf16[16,528,1024]{2,1,0:T(8,128)(2,1)} %bitcast.211), kind=kLoop, calls=%fused_computation.362 | loop fusion | bytes 33554432 | tf_op jit(solution)/shard_map/slice | solution.py:266
  125.9 4.6 convolution_add_fusion.16
  132.5 4.4 convolution_add_fusion.17
  151.0 11.6 %collective-permute-done.1 = bf16[128,2048]{1,0:T(8,128)(2,1)} collective-permute-done((bf16[128,2048]{1,0:T(8,128)(2,1)S(1)}, bf16[128,2048]{1,0:T(8,128)(2,1)}, u32[]{:S(2)}, u32[]{:S(2)}) %collective-permute-start.1) | collective-permute-done | bytes 524320 | tf_op jit(solution)/shard_map/ppermute | solution.py:156
  169.9 4.1 shard_map.172
  173.9 4.1 shard_map.169
  181.7 4.1 shard_map.171
  185.8 42.0 %all-gather.6.cloned.1.call-done = bf16[2,2048,2816]{2,1,0:T(8,128)(2,1)} async-done(((bf16[2,128,2816]{2,1,0:T(8,128)(2,1)}), bf16[2,2048,2816]{2,1,0:T(8,128)(2,1)}) %all-gather.6.cloned.1.call-update) | async-done | bytes 23068688 | tf_op jit(solution)/shard_map/all_gather | solution.py:262
  227.8 6.8 fusion.5
  234.6 11.2 %multiply_convert_fusion.3 = (bf16[256,2816]{1,0:T(8,128)(2,1)S(1)}, f32[256,2816]{1,0:T(8,128)}) fusion(f32[256,2816]{1,0:T(8,128)S(1)} %fusion.5, bf16[2,2048,2816]{2,1,0:T(8,128)(2,1)} %all-gather.6.cloned.1.call-done, bf16[128,2048]{1,0:T(8,128)(2,1)} %collective-permute-done.3, bf16[128,2048]{1,0:T(8,128)(2,1)} %add_convert_fusion.7), kind=kOutput, calls=%fused_computation.51 | convolution fusion | flops 2959212544 | bytes 19791872 | tf_op jit(solution)/shard_map/dot_general | solution.py:22
  245.8 81.1 %all-gather.10.cloned.1.call-done = bf16[1,2816,2048]{2,1,0:T(8,128)(2,1)} async-done(((bf16[1,2816,128]{2,1,0:T(8,128)(2,1)}), bf16[1,2816,2048]{2,1,0:T(8,128)(2,1)}) %all-gather.10.cloned.1.call-update) | async-done | bytes 11534352 | tf_op jit(solution)/shard_map/all_gather | solution.py:263
  326.9 10.2 %multiply_convert_fusion.1 = (bf16[256,2816]{1,0:T(8,128)(2,1)S(1)}, bf16[256,2816]{1,0:T(8,128)(2,1)S(1)}) fusion(f32[256,2816]{1,0:T(8,128)} %copy-done.96, f32[256,2816]{1,0:T(8,128)} %get-tuple-element.14, bf16[256,2048]{1,0:T(8,128)(2,1)} %copy-done.33, bf16[1,2816,2048]{2,1,0:T(8,128)(2,1)} %all-gather.10.cloned.1.call-done), kind=kOutput, calls=%fused_computation.48 | convolution fusion | flops 2962161664 | bytes 21233664 | tf_op jit(solution)/shard_map/dot_general | solution.py:26
  337.1 7.1 fusion.4
  344.2 6.7 fusion.30
  352.5 2.6 convolution_convert_fusion.1
  355.0 2.5 convolution_convert_fusion.2
  357.6 2.6 convolution_convert_fusion.3
  360.2 4.9 collective-permute-done.4
  366.1 2.6 fusion.218
  370.2 2.6 convolution_convert_fusion.4
  373.4 4.1 convolution_convert_fusion
  377.5 4.4 collective-permute-done.5
  386.7 3.8 multiply_convert_fusion
  399.2 2.6 fusion.227
  404.0 4.1 shard_map.170
  408.1 6.6 fusion
  425.9 3.2 convolution_convert_fusion.5
  435.3 4.1 collective-permute-done.7
  441.8 84.7 %all-reduce.4.cloned.1.call-done = f32[128,128]{1,0:T(8,128)} async-done(((f32[128,128]{1,0:T(8,128)}), f32[128,128]{1,0:T(8,128)}) %all-reduce.4.cloned.1.call-update) | async-done | bytes 65552 | tf_op jit(solution)/shard_map/psum | solution.py:362
  533.3 2.5 fusion.67
  557.0 16.2 %collective-permute-done.20 = bf16[512,1024]{1,0:T(8,128)(2,1)S(1)} collective-permute-done((bf16[512,1024]{1,0:T(8,128)(2,1)S(1)}, bf16[512,1024]{1,0:T(8,128)(2,1)S(1)}, u32[]{:S(2)}, u32[]{:S(2)}) %collective-permute-start.20) | collective-permute-done | bytes 1048608 | tf_op jit(solution)/shard_map/ppermute | solution.py:53
  579.3 78.2 %collective-permute-done.15 = bf16[512,1024]{1,0:T(8,128)(2,1)S(1)} collective-permute-done((bf16[512,1024]{1,0:T(8,128)(2,1)S(1)}, bf16[512,1024]{1,0:T(8,128)(2,1)S(1)}, u32[]{:S(2)}, u32[]{:S(2)}) %collective-permute-start.15) | collective-permute-done | bytes 1048608 | tf_op jit(solution)/shard_map/ppermute | solution.py:53
  664.5 15.5 %collective-permute-done.10 = bf16[512,1024]{1,0:T(8,128)(2,1)S(1)} collective-permute-done((bf16[512,1024]{1,0:T(8,128)(2,1)S(1)}, bf16[512,1024]{1,0:T(8,128)(2,1)S(1)}, u32[]{:S(2)}, u32[]{:S(2)}) %collective-permute-start.10) | collective-permute-done | bytes 1048608 | tf_op jit(solution)/shard_map/ppermute | solution.py:53
  683.9 18.5 %collective-permute-done.25 = bf16[512,1024]{1,0:T(8,128)(2,1)S(1)} collective-permute-done((bf16[512,1024]{1,0:T(8,128)(2,1)S(1)}, bf16[512,1024]{1,0:T(8,128)(2,1)S(1)}, u32[]{:S(2)}, u32[]{:S(2)}) %collective-permute-start.25) | collective-permute-done | bytes 1048608 | tf_op jit(solution)/shard_map/ppermute | solution.py:53
  706.8 4.6 collective-permute-start.23
  711.4 2.9 fusion.28
  720.5 3.7 add_convert_fusion
  724.1 9.2 collective-permute-done.36
  736.9 27.4 %collective-permute-done.30 = bf16[512,1408]{1,0:T(8,128)(2,1)S(1)} collective-permute-done((bf16[512,1408]{1,0:T(8,128)(2,1)S(1)}, bf16[512,1408]{1,0:T(8,128)(2,1)S(1)}, u32[]{:S(2)}, u32[]{:S(2)}) %collective-permute-start.30) | collective-permute-done | bytes 1441824 | tf_op jit(solution)/shard_map/ppermute | solution.py:53
  764.2 3.9 collective-permute-start.26
  775.2 4.9 collective-permute-start.49
  781.3 5.5 collective-permute-done.22
  788.8 4.1 collective-permute-done.18
  792.9 3.2 collective-permute-start.13
  797.5 23.0 %collective-permute-done.17 = bf16[128,1024]{1,0:T(8,128)(2,1)S(1)} collective-permute-done((bf16[128,1024]{1,0:T(8,128)(2,1)}, bf16[128,1024]{1,0:T(8,128)(2,1)S(1)}, u32[]{:S(2)}, u32[]{:S(2)}) %collective-permute-start.17) | collective-permute-done | bytes 262176 | tf_op jit(solution)/shard_map/ppermute | solution.py:67
  820.5 3.3 collective-permute-start.12
  828.5 4.4 collective-permute-done.13
  835.6 3.7 collective-permute-done.12
  843.0 4.3 collective-permute-start.31
  852.8 13.4 %collective-permute-done.43 = bf16[384,1408]{1,0:T(8,128)(2,1)S(1)} collective-permute-done((bf16[384,1408]{1,0:T(8,128)(2,1)}, bf16[384,1408]{1,0:T(8,128)(2,1)S(1)}, u32[]{:S(2)}, u32[]{:S(2)}) %collective-permute-start.43) | collective-permute-done | bytes 1081376 | tf_op jit(solution)/shard_map/ppermute | solution.py:67
  869.0 3.2 fusion.9
  873.1 16.2 %collective-permute-done.37 = bf16[384,1408]{1,0:T(8,128)(2,1)S(1)} collective-permute-done((bf16[384,1408]{1,0:T(8,128)(2,1)S(1)}, bf16[384,1408]{1,0:T(8,128)(2,1)S(1)}, u32[]{:S(2)}, u32[]{:S(2)}) %collective-permute-start.37) | collective-permute-done | bytes 1081376 | tf_op jit(solution)/shard_map/ppermute | solution.py:67
  889.2 4.5 collective-permute-start.55
  895.9 16.5 %collective-permute-done.31 = bf16[384,1408]{1,0:T(8,128)(2,1)S(1)} collective-permute-done((bf16[384,1408]{1,0:T(8,128)(2,1)S(1)}, bf16[384,1408]{1,0:T(8,128)(2,1)S(1)}, u32[]{:S(2)}, u32[]{:S(2)}) %collective-permute-start.31) | collective-permute-done | bytes 1081376 | tf_op jit(solution)/shard_map/ppermute | solution.py:67
  919.2 7.3 collective-permute-done.45
  930.4 11.5 %collective-permute-done.39 = bf16[128,1408]{1,0:T(8,128)(2,1)S(1)} collective-permute-done((bf16[128,1408]{1,0:T(8,128)(2,1)S(1)}, bf16[128,1408]{1,0:T(8,128)(2,1)S(1)}, u32[]{:S(2)}, u32[]{:S(2)}) %collective-permute-start.39) | collective-permute-done | bytes 360480 | tf_op jit(solution)/shard_map/ppermute | solution.py:67
  943.5 9.7 collective-permute-done.33
  959.8 3.8 copy.84
  963.6 7.1 collective-permute-done.56
  970.7 22.6 %collective-permute-done.57 = bf16[128,2816]{1,0:T(8,128)(2,1)S(1)} collective-permute-done((bf16[128,2816]{1,0:T(8,128)(2,1)S(1)}, bf16[128,2816]{1,0:T(8,128)(2,1)S(1)}, u32[]{:S(2)}, u32[]{:S(2)}) %collective-permute-start.57) | collective-permute-done | bytes 720928 | tf_op jit(solution)/shard_map/ppermute | solution.py:67
  (450 shorter events, 197.2 us)
Async XLA Ops:
  7.2 99.8 %all-gather.8.cloned.1.call-start = ((), (), s32[]{:S(2)}) async-start(), calls=%async_computation.2 | async-start | bytes 18382848 | tf_op jit(solution)/shard_map/all_gather | solution.py:261
  12.6 215.1 %all-gather.6.cloned.1.call-start = ((), (), s32[]{:S(2)}) async-start(), calls=%async_computation | async-start | bytes 24510464 | tf_op jit(solution)/shard_map/all_gather | solution.py:262
  15.4 311.5 %all-gather.10.cloned.1.call-start = ((), (), s32[]{:S(2)}) async-start(), calls=%async_computation.3 | async-start | bytes 12255232 | tf_op jit(solution)/shard_map/all_gather | solution.py:263
  16.1 510.4 %all-reduce.4.cloned.1.call-start = ((), (), s32[]{:S(2)}) async-start(), calls=%async_computation.1 | async-start | bytes 131072 | tf_op jit(solution)/shard_map/psum | solution.py:362
  16.2 15.8 %collective-permute-start = (bf16[128,2048]{1,0:T(8,128)(2,1)S(1)}, bf16[128,2048]{1,0:T(8,128)(2,1)S(1)}, u32[]{:S(2)}, u32[]{:S(2)}) collective-permute-start(bf16[128,2048]{1,0:T(8,128)(2,1)S(1)} %copy-done), channel_id=1, source_target_pairs={{0,1},{1,0},{2,3},{3,2},{4,5},{5,4},{6,7},{7,6},{8,9},{9,8},{10,11... | collective-permute-start | bytes 1572872 | tf_op jit(solution)/shard_map/ppermute | solution.py:156
  19.2 148.6 %collective-permute-start.2 = (bf16[128,2048]{1,0:T(8,128)(2,1)}, bf16[128,2048]{1,0:T(8,128)(2,1)}, u32[]{:S(2)}, u32[]{:S(2)}) collective-permute-start(bf16[128,2048]{1,0:T(8,128)(2,1)} %param.12), channel_id=1, source_target_pairs={{0,1},{1,0},{2,3},{3,2},{4,5},{5,4},{6,7},{7,6},{8,9},{9,8},{10,11... | collective-permute-start | bytes 1572872 | tf_op jit(solution)/shard_map/ppermute | solution.py:156
  148.1 14.4 %collective-permute-start.1 = (bf16[128,2048]{1,0:T(8,128)(2,1)S(1)}, bf16[128,2048]{1,0:T(8,128)(2,1)}, u32[]{:S(2)}, u32[]{:S(2)}) collective-permute-start(bf16[128,2048]{1,0:T(8,128)(2,1)S(1)} %slice.1152), channel_id=1, source_target_pairs={{0,1},{1,0},{2,3},{3,2},{4,5},{5,4},{6,7},{7,6},{8,9},{9,8},{10,11... | collective-permute-start | bytes 1572872 | tf_op jit(solution)/shard_map/ppermute | solution.py:156
  165.7 13.7 %collective-permute-start.3 = (bf16[128,2048]{1,0:T(8,128)(2,1)}, bf16[128,2048]{1,0:T(8,128)(2,1)}, u32[]{:S(2)}, u32[]{:S(2)}) collective-permute-start(bf16[128,2048]{1,0:T(8,128)(2,1)} %add_convert_fusion.7), channel_id=1, source_target_pairs={{0,1},{1,0},{2,3},{3,2},{4,5},{5,4},{6,7},{7,6},{8,9},{9,8},{10,11... | collective-permute-start | bytes 1572872 | tf_op jit(solution)/shard_map/ppermute | solution.py:156
  350.9 14.1 %collective-permute-start.4 = (bf16[128,2048]{1,0:T(8,128)(2,1)S(1)}, bf16[128,2048]{1,0:T(8,128)(2,1)S(1)}, u32[]{:S(2)}, u32[]{:S(2)}) collective-permute-start(bf16[128,2048]{1,0:T(8,128)(2,1)S(1)} %slice.1151), channel_id=1, source_target_pairs={{0,1},{1,0},{2,3},{3,2},{4,5},{5,4},{6,7},{7,6},{8,9},{9,8},{10,11... | collective-permute-start | bytes 1572872 | tf_op jit(solution)/shard_map/ppermute | solution.py:156
  368.7 13.2 %collective-permute-start.5 = (bf16[128,2048]{1,0:T(8,128)(2,1)S(1)}, bf16[128,2048]{1,0:T(8,128)(2,1)S(1)}, u32[]{:S(2)}, u32[]{:S(2)}) collective-permute-start(bf16[128,2048]{1,0:T(8,128)(2,1)S(1)} %get-tuple-element.54), channel_id=1, source_target_pairs={{0,1},{1,0},{2,3},{3,2},{4,5},{5,4},{6,7},{7,6},{8,9},{9,8},{10,11... | collective-permute-start | bytes 1572872 | tf_op jit(solution)/shard_map/ppermute | solution.py:156
  372.8 162.9 %collective-permute-start.47 = (bf16[1024,1408]{1,0:T(8,128)(2,1)}, bf16[1024,1408]{1,0:T(8,128)(2,1)}, u32[]{:S(2)}, u32[]{:S(2)}) collective-permute-start(bf16[1024,1408]{1,0:T(8,128)(2,1)} %convolution_convert_fusion.1), channel_id=1, source_target_pairs={{0,2},{2,0},{4,6},{6,4},{8,10},{10,8},{12,14},{14,12},{16,18},{18,... | collective-permute-start | bytes 8650760 | tf_op jit(solution)/shard_map/ppermute | solution.py:53
  372.8 164.9 %collective-permute-start.41 = (bf16[1024,1408]{1,0:T(8,128)(2,1)}, bf16[1024,1408]{1,0:T(8,128)(2,1)}, u32[]{:S(2)}, u32[]{:S(2)}) collective-permute-start(bf16[1024,1408]{1,0:T(8,128)(2,1)} %convolution_convert_fusion.2), channel_id=1, source_target_pairs={{0,2},{2,0},{4,6},{6,4},{8,10},{10,8},{12,14},{14,12},{16,18},{18,... | collective-permute-start | bytes 8650760 | tf_op jit(solution)/shard_map/ppermute | solution.py:53
  373.4 165.0 %collective-permute-start.35 = (bf16[1024,1408]{1,0:T(8,128)(2,1)}, bf16[1024,1408]{1,0:T(8,128)(2,1)}, u32[]{:S(2)}, u32[]{:S(2)}) collective-permute-start(bf16[1024,1408]{1,0:T(8,128)(2,1)} %convolution_convert_fusion.3), channel_id=1, source_target_pairs={{0,2},{2,0},{4,6},{6,4},{8,10},{10,8},{12,14},{14,12},{16,18},{18,... | collective-permute-start | bytes 8650760 | tf_op jit(solution)/shard_map/ppermute | solution.py:53
  415.5 111.9 %collective-permute-start.6 = (bf16[128,2048]{1,0:T(8,128)(2,1)}, bf16[128,2048]{1,0:T(8,128)(2,1)}, u32[]{:S(2)}, u32[]{:S(2)}) collective-permute-start(bf16[128,2048]{1,0:T(8,128)(2,1)} %slice.1150), channel_id=1, source_target_pairs={{0,1},{1,0},{2,3},{3,2},{4,5},{5,4},{6,7},{7,6},{8,9},{9,8},{10,11... | collective-permute-start | bytes 1572872 | tf_op jit(solution)/shard_map/ppermute | solution.py:156
  425.0 14.4 %collective-permute-start.7 = (bf16[128,2048]{1,0:T(8,128)(2,1)}, bf16[128,2048]{1,0:T(8,128)(2,1)}, u32[]{:S(2)}, u32[]{:S(2)}) collective-permute-start(bf16[128,2048]{1,0:T(8,128)(2,1)} %slice.1149), channel_id=1, source_target_pairs={{0,1},{1,0},{2,3},{3,2},{4,5},{5,4},{6,7},{7,6},{8,9},{9,8},{10,11... | collective-permute-start | bytes 1572872 | tf_op jit(solution)/shard_map/ppermute | solution.py:156
  439.4 101.7 %collective-permute-start.19 = (bf16[1024,1024]{1,0:T(8,128)(2,1)}, bf16[1024,1024]{1,0:T(8,128)(2,1)}, u32[]{:S(2)}, u32[]{:S(2)}) collective-permute-start(bf16[1024,1024]{1,0:T(8,128)(2,1)} %convolution_convert_fusion.6), channel_id=1, source_target_pairs={{0,2},{2,0},{4,6},{6,4},{8,10},{10,8},{12,14},{14,12},{16,18},{18,... | collective-permute-start | bytes 6291464 | tf_op jit(solution)/shard_map/ppermute | solution.py:53
  527.4 3.6 collective-permute-start.8
  531.0 16.2 %collective-permute-start.29 = (bf16[1024,1408]{1,0:T(8,128)(2,1)}, bf16[1024,1408]{1,0:T(8,128)(2,1)}, u32[]{:S(2)}, u32[]{:S(2)}) collective-permute-start(bf16[1024,1408]{1,0:T(8,128)(2,1)} %convolution_convert_fusion.4), channel_id=1, source_target_pairs={{0,2},{2,0},{4,6},{6,4},{8,10},{10,8},{12,14},{14,12},{16,18},{18,... | collective-permute-start | bytes 8650760 | tf_op jit(solution)/shard_map/ppermute | solution.py:53
  535.7 14.2 %collective-permute-start.14 = (bf16[1024,1024]{1,0:T(8,128)(2,1)}, bf16[1024,1024]{1,0:T(8,128)(2,1)}, u32[]{:S(2)}, u32[]{:S(2)}) collective-permute-start(bf16[1024,1024]{1,0:T(8,128)(2,1)} %convolution_convert_fusion.7), channel_id=1, source_target_pairs={{0,2},{2,0},{4,6},{6,4},{8,10},{10,8},{12,14},{14,12},{16,18},{18,... | collective-permute-start | bytes 6291464 | tf_op jit(solution)/shard_map/ppermute | solution.py:53
  537.7 15.2 %collective-permute-start.9 = (bf16[1024,1024]{1,0:T(8,128)(2,1)}, bf16[1024,1024]{1,0:T(8,128)(2,1)S(1)}, u32[]{:S(2)}, u32[]{:S(2)}) collective-permute-start(bf16[1024,1024]{1,0:T(8,128)(2,1)} %convolution_convert_fusion.8), channel_id=1, source_target_pairs={{0,2},{2,0},{4,6},{6,4},{8,10},{10,8},{12,14},{14,12},{16,18},{18,... | collective-permute-start | bytes 6291464 | tf_op jit(solution)/shard_map/ppermute | solution.py:53
  538.4 16.0 %collective-permute-start.24 = (bf16[1024,1024]{1,0:T(8,128)(2,1)}, bf16[1024,1024]{1,0:T(8,128)(2,1)S(1)}, u32[]{:S(2)}, u32[]{:S(2)}) collective-permute-start(bf16[1024,1024]{1,0:T(8,128)(2,1)} %convolution_convert_fusion.5), channel_id=1, source_target_pairs={{0,2},{2,0},{4,6},{6,4},{8,10},{10,8},{12,14},{14,12},{16,18},{18,... | collective-permute-start | bytes 6291464 | tf_op jit(solution)/shard_map/ppermute | solution.py:53
  541.1 178.5 %collective-permute-start.53 = (bf16[1024,2816]{1,0:T(8,128)(2,1)}, bf16[1024,2816]{1,0:T(8,128)(2,1)S(1)}, u32[]{:S(2)}, u32[]{:S(2)}) collective-permute-start(bf16[1024,2816]{1,0:T(8,128)(2,1)} %convolution_convert_fusion), channel_id=1, source_target_pairs={{0,2},{2,0},{4,6},{6,4},{8,10},{10,8},{12,14},{14,12},{16,18},{18,... | collective-permute-start | bytes 17301512 | tf_op jit(solution)/shard_map/ppermute | solution.py:53
  547.1 26.1 %collective-permute-start.20 = (bf16[512,1024]{1,0:T(8,128)(2,1)S(1)}, bf16[512,1024]{1,0:T(8,128)(2,1)S(1)}, u32[]{:S(2)}, u32[]{:S(2)}) collective-permute-start(bf16[512,1024]{1,0:T(8,128)(2,1)S(1)} %add_convert_fusion.2), channel_id=1, source_target_pairs={{0,4},{2,6},{4,0},{6,2},{8,12},{10,14},{12,8},{14,10},{16,20},{18,... | collective-permute-start | bytes 3145736 | tf_op jit(solution)/shard_map/ppermute | solution.py:53
  550.0 156.8 %collective-permute-start.48 = (bf16[512,1408]{1,0:T(8,128)(2,1)S(1)}, bf16[512,1408]{1,0:T(8,128)(2,1)S(1)}, u32[]{:S(2)}, u32[]{:S(2)}) collective-permute-start(bf16[512,1408]{1,0:T(8,128)(2,1)S(1)} %fusion.24), channel_id=1, source_target_pairs={{0,4},{2,6},{4,0},{6,2},{8,12},{10,14},{12,8},{14,10},{16,20},{18,... | collective-permute-start | bytes 4325384 | tf_op jit(solution)/shard_map/ppermute | solution.py:53
  552.9 129.9 %copy-start.40 = (bf16[1024,1024]{1,0:T(8,128)(2,1)}, bf16[1024,1024]{1,0:T(8,128)(2,1)S(1)}, u32[]{:S(2)}) copy-start(bf16[1024,1024]{1,0:T(8,128)(2,1)S(1)} %collective-permute-done.9) | copy-start | bytes 6291460
  553.0 163.0 %collective-permute-start.42 = (bf16[512,1408]{1,0:T(8,128)(2,1)S(1)}, bf16[512,1408]{1,0:T(8,128)(2,1)S(1)}, u32[]{:S(2)}, u32[]{:S(2)}) collective-permute-start(bf16[512,1408]{1,0:T(8,128)(2,1)S(1)} %fusion.23), channel_id=1, source_target_pairs={{0,4},{2,6},{4,0},{6,2},{8,12},{10,14},{12,8},{14,10},{16,20},{18,... | collective-permute-start | bytes 4325384 | tf_op jit(solution)/shard_map/ppermute | solution.py:53
  554.4 103.1 %collective-permute-start.15 = (bf16[512,1024]{1,0:T(8,128)(2,1)S(1)}, bf16[512,1024]{1,0:T(8,128)(2,1)S(1)}, u32[]{:S(2)}, u32[]{:S(2)}) collective-permute-start(bf16[512,1024]{1,0:T(8,128)(2,1)S(1)} %add_convert_fusion.3), channel_id=1, source_target_pairs={{0,4},{2,6},{4,0},{6,2},{8,12},{10,14},{12,8},{14,10},{16,20},{18,... | collective-permute-start | bytes 3145736 | tf_op jit(solution)/shard_map/ppermute | solution.py:53
  573.2 106.7 %collective-permute-start.10 = (bf16[512,1024]{1,0:T(8,128)(2,1)S(1)}, bf16[512,1024]{1,0:T(8,128)(2,1)S(1)}, u32[]{:S(2)}, u32[]{:S(2)}) collective-permute-start(bf16[512,1024]{1,0:T(8,128)(2,1)S(1)} %add_convert_fusion.4), channel_id=1, source_target_pairs={{0,4},{2,6},{4,0},{6,2},{8,12},{10,14},{12,8},{14,10},{16,20},{18,... | collective-permute-start | bytes 3145736 | tf_op jit(solution)/shard_map/ppermute | solution.py:53
  657.5 44.9 %collective-permute-start.25 = (bf16[512,1024]{1,0:T(8,128)(2,1)S(1)}, bf16[512,1024]{1,0:T(8,128)(2,1)S(1)}, u32[]{:S(2)}, u32[]{:S(2)}) collective-permute-start(bf16[512,1024]{1,0:T(8,128)(2,1)S(1)} %add_convert_fusion.1), channel_id=1, source_target_pairs={{0,4},{2,6},{4,0},{6,2},{8,12},{10,14},{12,8},{14,10},{16,20},{18,... | collective-permute-start | bytes 3145736 | tf_op jit(solution)/shard_map/ppermute | solution.py:53
  680.0 53.4 %collective-permute-start.36 = (bf16[512,1408]{1,0:T(8,128)(2,1)S(1)}, bf16[512,1408]{1,0:T(8,128)(2,1)S(1)}, u32[]{:S(2)}, u32[]{:S(2)}) collective-permute-start(bf16[512,1408]{1,0:T(8,128)(2,1)S(1)} %fusion.22), channel_id=1, source_target_pairs={{0,4},{2,6},{4,0},{6,2},{8,12},{10,14},{12,8},{14,10},{16,20},{18,... | collective-permute-start | bytes 4325384 | tf_op jit(solution)/shard_map/ppermute | solution.py:53
  702.4 61.8 %collective-permute-start.30 = (bf16[512,1408]{1,0:T(8,128)(2,1)S(1)}, bf16[512,1408]{1,0:T(8,128)(2,1)S(1)}, u32[]{:S(2)}, u32[]{:S(2)}) collective-permute-start(bf16[512,1408]{1,0:T(8,128)(2,1)S(1)} %fusion.21), channel_id=1, source_target_pairs={{0,4},{2,6},{4,0},{6,2},{8,12},{10,14},{12,8},{14,10},{16,20},{18,... | collective-permute-start | bytes 4325384 | tf_op jit(solution)/shard_map/ppermute | solution.py:53
  706.8 64.0 %collective-permute-start.23 = (bf16[128,1024]{1,0:T(8,128)(2,1)S(1)}, bf16[128,1024]{1,0:T(8,128)(2,1)S(1)}, u32[]{:S(2)}, u32[]{:S(2)}) collective-permute-start(bf16[128,1024]{1,0:T(8,128)(2,1)S(1)} %add_convert_fusion.19), channel_id=1, source_target_pairs={{0,24},{2,26},{4,28},{6,30},{8,16},{10,18},{12,20},{14,22},{16,8},... | collective-permute-start | bytes 786440 | tf_op jit(solution)/shard_map/ppermute | solution.py:67
  716.0 56.3 %collective-permute-start.28 = (bf16[128,1024]{1,0:T(8,128)(2,1)S(1)}, bf16[128,1024]{1,0:T(8,128)(2,1)S(1)}, u32[]{:S(2)}, u32[]{:S(2)}) collective-permute-start(bf16[128,1024]{1,0:T(8,128)(2,1)S(1)} %add_convert_fusion.16), channel_id=1, source_target_pairs={{0,24},{2,26},{4,28},{6,30},{8,16},{10,18},{12,20},{14,22},{16,8},... | collective-permute-start | bytes 786440 | tf_op jit(solution)/shard_map/ppermute | solution.py:67
  719.9 52.9 %collective-permute-start.27 = (bf16[128,1024]{1,0:T(8,128)(2,1)S(1)}, bf16[128,1024]{1,0:T(8,128)(2,1)S(1)}, u32[]{:S(2)}, u32[]{:S(2)}) collective-permute-start(bf16[128,1024]{1,0:T(8,128)(2,1)S(1)} %add_convert_fusion.17), channel_id=1, source_target_pairs={{0,16},{2,18},{4,20},{6,22},{8,24},{10,26},{12,28},{14,30},{16,0},... | collective-permute-start | bytes 786440 | tf_op jit(solution)/shard_map/ppermute | solution.py:67
  733.3 134.4 %collective-permute-start.54 = (bf16[512,2816]{1,0:T(8,128)(2,1)}, bf16[512,2816]{1,0:T(8,128)(2,1)}, u32[]{:S(2)}, u32[]{:S(2)}) collective-permute-start(bf16[512,2816]{1,0:T(8,128)(2,1)} %add_convert_fusion), channel_id=1, source_target_pairs={{0,4},{2,6},{4,0},{6,2},{8,12},{10,14},{12,8},{14,10},{16,20},{18,... | collective-permute-start | bytes 8650760 | tf_op jit(solution)/shard_map/ppermute | solution.py:53
  764.2 11.0 %collective-permute-start.26 = (bf16[128,1024]{1,0:T(8,128)(2,1)S(1)}, bf16[128,1024]{1,0:T(8,128)(2,1)S(1)}, u32[]{:S(2)}, u32[]{:S(2)}) collective-permute-start(bf16[128,1024]{1,0:T(8,128)(2,1)S(1)} %add_convert_fusion.18), channel_id=1, source_target_pairs={{0,8},{2,10},{4,12},{6,14},{8,0},{10,2},{12,4},{14,6},{16,24},{18,... | collective-permute-start | bytes 786440 | tf_op jit(solution)/shard_map/ppermute | solution.py:67
  770.8 16.1 %collective-permute-start.22 = (bf16[128,1024]{1,0:T(8,128)(2,1)}, bf16[128,1024]{1,0:T(8,128)(2,1)}, u32[]{:S(2)}, u32[]{:S(2)}) collective-permute-start(bf16[128,1024]{1,0:T(8,128)(2,1)} %add_convert_fusion.20), channel_id=1, source_target_pairs={{0,16},{2,18},{4,20},{6,22},{8,24},{10,26},{12,28},{14,30},{16,0},... | collective-permute-start | bytes 786440 | tf_op jit(solution)/shard_map/ppermute | solution.py:67
  772.3 14.6 %collective-permute-start.21 = (bf16[128,1024]{1,0:T(8,128)(2,1)}, bf16[128,1024]{1,0:T(8,128)(2,1)}, u32[]{:S(2)}, u32[]{:S(2)}) collective-permute-start(bf16[128,1024]{1,0:T(8,128)(2,1)} %add_convert_fusion.21), channel_id=1, source_target_pairs={{0,8},{2,10},{4,12},{6,14},{8,0},{10,2},{12,4},{14,6},{16,24},{18,... | collective-permute-start | bytes 786440 | tf_op jit(solution)/shard_map/ppermute | solution.py:67
  772.8 20.1 %collective-permute-start.18 = (bf16[128,1024]{1,0:T(8,128)(2,1)}, bf16[128,1024]{1,0:T(8,128)(2,1)}, u32[]{:S(2)}, u32[]{:S(2)}) collective-permute-start(bf16[128,1024]{1,0:T(8,128)(2,1)} %add_convert_fusion.22), channel_id=1, source_target_pairs={{0,24},{2,26},{4,28},{6,30},{8,16},{10,18},{12,20},{14,22},{16,8},... | collective-permute-start | bytes 786440 | tf_op jit(solution)/shard_map/ppermute | solution.py:67
  775.2 74.7 %collective-permute-start.49 = (bf16[384,1408]{1,0:T(8,128)(2,1)}, bf16[384,1408]{1,0:T(8,128)(2,1)}, u32[]{:S(2)}, u32[]{:S(2)}) collective-permute-start(bf16[384,1408]{1,0:T(8,128)(2,1)} %fusion.28), channel_id=1, source_target_pairs={{0,8},{2,10},{4,12},{6,14},{24,16},{26,18},{28,20},{30,22},{1,9},{... | collective-permute-start | bytes 3244040 | tf_op jit(solution)/shard_map/ppermute | solution.py:67
  786.8 33.7 %collective-permute-start.17 = (bf16[128,1024]{1,0:T(8,128)(2,1)}, bf16[128,1024]{1,0:T(8,128)(2,1)S(1)}, u32[]{:S(2)}, u32[]{:S(2)}) collective-permute-start(bf16[128,1024]{1,0:T(8,128)(2,1)} %add_convert_fusion.23), channel_id=1, source_target_pairs={{0,16},{2,18},{4,20},{6,22},{8,24},{10,26},{12,28},{14,30},{16,0},... | collective-permute-start | bytes 786440 | tf_op jit(solution)/shard_map/ppermute | solution.py:67
  786.8 39.3 %collective-permute-start.16 = (bf16[128,1024]{1,0:T(8,128)(2,1)}, bf16[128,1024]{1,0:T(8,128)(2,1)S(1)}, u32[]{:S(2)}, u32[]{:S(2)}) collective-permute-start(bf16[128,1024]{1,0:T(8,128)(2,1)} %add_convert_fusion.24), channel_id=1, source_target_pairs={{0,8},{2,10},{4,12},{6,14},{8,0},{10,2},{12,4},{14,6},{16,24},{18,... | collective-permute-start | bytes 786440 | tf_op jit(solution)/shard_map/ppermute | solution.py:67
  792.9 40.1 %collective-permute-start.13 = (bf16[128,1024]{1,0:T(8,128)(2,1)}, bf16[128,1024]{1,0:T(8,128)(2,1)S(1)}, u32[]{:S(2)}, u32[]{:S(2)}) collective-permute-start(bf16[128,1024]{1,0:T(8,128)(2,1)} %add_convert_fusion.25), channel_id=1, source_target_pairs={{0,24},{2,26},{4,28},{6,30},{8,16},{10,18},{12,20},{14,22},{16,8},... | collective-permute-start | bytes 786440 | tf_op jit(solution)/shard_map/ppermute | solution.py:67
  820.5 18.8 %collective-permute-start.12 = (bf16[128,1024]{1,0:T(8,128)(2,1)}, bf16[128,1024]{1,0:T(8,128)(2,1)S(1)}, u32[]{:S(2)}, u32[]{:S(2)}) collective-permute-start(bf16[128,1024]{1,0:T(8,128)(2,1)} %add_convert_fusion.26), channel_id=1, source_target_pairs={{0,16},{2,18},{4,20},{6,22},{8,24},{10,26},{12,28},{14,30},{16,0},... | collective-permute-start | bytes 786440 | tf_op jit(solution)/shard_map/ppermute | solution.py:67
  826.1 16.9 %collective-permute-start.11 = (bf16[128,1024]{1,0:T(8,128)(2,1)}, bf16[128,1024]{1,0:T(8,128)(2,1)S(1)}, u32[]{:S(2)}, u32[]{:S(2)}) collective-permute-start(bf16[128,1024]{1,0:T(8,128)(2,1)} %add_convert_fusion.27), channel_id=1, source_target_pairs={{0,8},{2,10},{4,12},{6,14},{8,0},{10,2},{12,4},{14,6},{16,24},{18,... | collective-permute-start | bytes 786440 | tf_op jit(solution)/shard_map/ppermute | solution.py:67
  832.9 33.3 %collective-permute-start.43 = (bf16[384,1408]{1,0:T(8,128)(2,1)}, bf16[384,1408]{1,0:T(8,128)(2,1)S(1)}, u32[]{:S(2)}, u32[]{:S(2)}) collective-permute-start(bf16[384,1408]{1,0:T(8,128)(2,1)} %copy-done.52), channel_id=1, source_target_pairs={{0,8},{2,10},{4,12},{6,14},{24,16},{26,18},{28,20},{30,22},{1,9},{... | collective-permute-start | bytes 3244040 | tf_op jit(solution)/shard_map/ppermute | solution.py:67
  839.4 49.9 %collective-permute-start.37 = (bf16[384,1408]{1,0:T(8,128)(2,1)S(1)}, bf16[384,1408]{1,0:T(8,128)(2,1)S(1)}, u32[]{:S(2)}, u32[]{:S(2)}) collective-permute-start(bf16[384,1408]{1,0:T(8,128)(2,1)S(1)} %copy-done.51), channel_id=1, source_target_pairs={{0,8},{2,10},{4,12},{6,14},{24,16},{26,18},{28,20},{30,22},{1,9},{... | collective-permute-start | bytes 3244040 | tf_op jit(solution)/shard_map/ppermute | solution.py:67
  843.0 69.4 %collective-permute-start.31 = (bf16[384,1408]{1,0:T(8,128)(2,1)S(1)}, bf16[384,1408]{1,0:T(8,128)(2,1)S(1)}, u32[]{:S(2)}, u32[]{:S(2)}) collective-permute-start(bf16[384,1408]{1,0:T(8,128)(2,1)S(1)} %copy-done.49), channel_id=1, source_target_pairs={{0,8},{2,10},{4,12},{6,14},{24,16},{26,18},{28,20},{30,22},{1,9},{... | collective-permute-start | bytes 3244040 | tf_op jit(solution)/shard_map/ppermute | solution.py:67
  849.9 22.3 %collective-permute-start.50 = (bf16[128,1408]{1,0:T(8,128)(2,1)S(1)}, bf16[128,1408]{1,0:T(8,128)(2,1)S(1)}, u32[]{:S(2)}, u32[]{:S(2)}) collective-permute-start(bf16[128,1408]{1,0:T(8,128)(2,1)S(1)} %copy-done.61), channel_id=1, source_target_pairs={{8,0},{10,2},{12,4},{14,6},{16,24},{18,26},{20,28},{22,30},{9,1},{... | collective-permute-start | bytes 1081352 | tf_op jit(solution)/shard_map/ppermute | solution.py:67
  866.2 27.8 %collective-permute-start.44 = (bf16[128,1408]{1,0:T(8,128)(2,1)S(1)}, bf16[128,1408]{1,0:T(8,128)(2,1)S(1)}, u32[]{:S(2)}, u32[]{:S(2)}) collective-permute-start(bf16[128,1408]{1,0:T(8,128)(2,1)S(1)} %copy-done.60), channel_id=1, source_target_pairs={{8,0},{10,2},{12,4},{14,6},{16,24},{18,26},{20,28},{22,30},{9,1},{... | collective-permute-start | bytes 1081352 | tf_op jit(solution)/shard_map/ppermute | solution.py:67
  867.7 27.5 %collective-permute-start.38 = (bf16[128,1408]{1,0:T(8,128)(2,1)S(1)}, bf16[128,1408]{1,0:T(8,128)(2,1)S(1)}, u32[]{:S(2)}, u32[]{:S(2)}) collective-permute-start(bf16[128,1408]{1,0:T(8,128)(2,1)S(1)} %copy-done.62), channel_id=1, source_target_pairs={{8,0},{10,2},{12,4},{14,6},{16,24},{18,26},{20,28},{22,30},{9,1},{... | collective-permute-start | bytes 1081352 | tf_op jit(solution)/shard_map/ppermute | solution.py:67
  872.2 41.5 %collective-permute-start.52 = (bf16[128,1408]{1,0:T(8,128)(2,1)S(1)}, bf16[128,1408]{1,0:T(8,128)(2,1)S(1)}, u32[]{:S(2)}, u32[]{:S(2)}) collective-permute-start(bf16[128,1408]{1,0:T(8,128)(2,1)S(1)} %get-tuple-element.73), channel_id=1, source_target_pairs={{8,16},{10,18},{12,20},{14,22},{16,8},{18,10},{20,12},{22,14},{9,1... | collective-permute-start | bytes 1081352 | tf_op jit(solution)/shard_map/ppermute | solution.py:67
  889.2 67.9 %collective-permute-start.55 = (bf16[384,2816]{1,0:T(8,128)(2,1)S(1)}, bf16[384,2816]{1,0:T(8,128)(2,1)S(1)}, u32[]{:S(2)}, u32[]{:S(2)}) collective-permute-start(bf16[384,2816]{1,0:T(8,128)(2,1)S(1)} %fusion.9), channel_id=1, source_target_pairs={{0,8},{2,10},{4,12},{6,14},{24,16},{26,18},{28,20},{30,22},{1,9},{... | collective-permute-start | bytes 6488072 | tf_op jit(solution)/shard_map/ppermute | solution.py:67
  893.9 20.7 %collective-permute-start.51 = (bf16[128,1408]{1,0:T(8,128)(2,1)S(1)}, bf16[128,1408]{1,0:T(8,128)(2,1)S(1)}, u32[]{:S(2)}, u32[]{:S(2)}) collective-permute-start(bf16[128,1408]{1,0:T(8,128)(2,1)S(1)} %get-tuple-element.72), channel_id=1, source_target_pairs={{8,24},{10,26},{12,28},{14,30},{16,0},{18,2},{20,4},{22,6},{9,25},... | collective-permute-start | bytes 1081352 | tf_op jit(solution)/shard_map/ppermute | solution.py:67
  895.3 22.5 %collective-permute-start.46 = (bf16[128,1408]{1,0:T(8,128)(2,1)S(1)}, bf16[128,1408]{1,0:T(8,128)(2,1)S(1)}, u32[]{:S(2)}, u32[]{:S(2)}) collective-permute-start(bf16[128,1408]{1,0:T(8,128)(2,1)S(1)} %get-tuple-element.71), channel_id=1, source_target_pairs={{8,16},{10,18},{12,20},{14,22},{16,8},{18,10},{20,12},{22,14},{9,1... | collective-permute-start | bytes 1081352 | tf_op jit(solution)/shard_map/ppermute | solution.py:67
  912.4 14.2 %collective-permute-start.45 = (bf16[128,1408]{1,0:T(8,128)(2,1)S(1)}, bf16[128,1408]{1,0:T(8,128)(2,1)S(1)}, u32[]{:S(2)}, u32[]{:S(2)}) collective-permute-start(bf16[128,1408]{1,0:T(8,128)(2,1)S(1)} %get-tuple-element.70), channel_id=1, source_target_pairs={{8,24},{10,26},{12,28},{14,30},{16,0},{18,2},{20,4},{22,6},{9,25},... | collective-permute-start | bytes 1081352 | tf_op jit(solution)/shard_map/ppermute | solution.py:67
  913.7 13.5 %collective-permute-start.40 = (bf16[128,1408]{1,0:T(8,128)(2,1)S(1)}, bf16[128,1408]{1,0:T(8,128)(2,1)S(1)}, u32[]{:S(2)}, u32[]{:S(2)}) collective-permute-start(bf16[128,1408]{1,0:T(8,128)(2,1)S(1)} %get-tuple-element.69), channel_id=1, source_target_pairs={{8,16},{10,18},{12,20},{14,22},{16,8},{18,10},{20,12},{22,14},{9,1... | collective-permute-start | bytes 1081352 | tf_op jit(solution)/shard_map/ppermute | solution.py:67
  914.6 27.3 %collective-permute-start.39 = (bf16[128,1408]{1,0:T(8,128)(2,1)S(1)}, bf16[128,1408]{1,0:T(8,128)(2,1)S(1)}, u32[]{:S(2)}, u32[]{:S(2)}) collective-permute-start(bf16[128,1408]{1,0:T(8,128)(2,1)S(1)} %get-tuple-element.68), channel_id=1, source_target_pairs={{8,24},{10,26},{12,28},{14,30},{16,0},{18,2},{20,4},{22,6},{9,25},... | collective-permute-start | bytes 1081352 | tf_op jit(solution)/shard_map/ppermute | solution.py:67
  917.8 25.7 %collective-permute-start.32 = (bf16[128,1408]{1,0:T(8,128)(2,1)S(1)}, bf16[128,1408]{1,0:T(8,128)(2,1)S(1)}, u32[]{:S(2)}, u32[]{:S(2)}) collective-permute-start(bf16[128,1408]{1,0:T(8,128)(2,1)S(1)} %copy-done.59), channel_id=1, source_target_pairs={{8,0},{10,2},{12,4},{14,6},{16,24},{18,26},{20,28},{22,30},{9,1},{... | collective-permute-start | bytes 1081352 | tf_op jit(solution)/shard_map/ppermute | solution.py:67
  926.6 17.0 %collective-permute-start.34 = (bf16[128,1408]{1,0:T(8,128)(2,1)S(1)}, bf16[128,1408]{1,0:T(8,128)(2,1)S(1)}, u32[]{:S(2)}, u32[]{:S(2)}) collective-permute-start(bf16[128,1408]{1,0:T(8,128)(2,1)S(1)} %get-tuple-element.67), channel_id=1, source_target_pairs={{8,16},{10,18},{12,20},{14,22},{16,8},{18,10},{20,12},{22,14},{9,1... | collective-permute-start | bytes 1081352 | tf_op jit(solution)/shard_map/ppermute | solution.py:67
  927.3 26.0 %collective-permute-start.33 = (bf16[128,1408]{1,0:T(8,128)(2,1)S(1)}, bf16[128,1408]{1,0:T(8,128)(2,1)S(1)}, u32[]{:S(2)}, u32[]{:S(2)}) collective-permute-start(bf16[128,1408]{1,0:T(8,128)(2,1)S(1)} %get-tuple-element.66), channel_id=1, source_target_pairs={{8,24},{10,26},{12,28},{14,30},{16,0},{18,2},{20,4},{22,6},{9,25},... | collective-permute-start | bytes 1081352 | tf_op jit(solution)/shard_map/ppermute | solution.py:67
  955.1 15.7 %collective-permute-start.56 = (bf16[128,2816]{1,0:T(8,128)(2,1)S(1)}, bf16[128,2816]{1,0:T(8,128)(2,1)S(1)}, u32[]{:S(2)}, u32[]{:S(2)}) collective-permute-start(bf16[128,2816]{1,0:T(8,128)(2,1)S(1)} %slice.835), channel_id=1, source_target_pairs={{8,0},{10,2},{12,4},{14,6},{16,24},{18,26},{20,28},{22,30},{9,1},{... | collective-permute-start | bytes 2162696 | tf_op jit(solution)/shard_map/ppermute | solution.py:67
  957.5 13.2 %collective-permute-start.58 = (bf16[128,2816]{1,0:T(8,128)(2,1)S(1)}, bf16[128,2816]{1,0:T(8,128)(2,1)S(1)}, u32[]{:S(2)}, u32[]{:S(2)}) collective-permute-start(bf16[128,2816]{1,0:T(8,128)(2,1)S(1)} %get-tuple-element.65), channel_id=1, source_target_pairs={{8,16},{10,18},{12,20},{14,22},{16,8},{18,10},{20,12},{22,14},{9,1... | collective-permute-start | bytes 2162696 | tf_op jit(solution)/shard_map/ppermute | solution.py:67
  958.2 35.1 %collective-permute-start.57 = (bf16[128,2816]{1,0:T(8,128)(2,1)S(1)}, bf16[128,2816]{1,0:T(8,128)(2,1)S(1)}, u32[]{:S(2)}, u32[]{:S(2)}) collective-permute-start(bf16[128,2816]{1,0:T(8,128)(2,1)S(1)} %get-tuple-element.64), channel_id=1, source_target_pairs={{8,24},{10,26},{12,28},{14,30},{16,0},{18,2},{20,4},{22,6},{9,25},... | collective-permute-start | bytes 2162696 | tf_op jit(solution)/shard_map/ppermute | solution.py:67
  (96 other events, 1153.9 us)
Sparse Core Ops, SparseCore 0:
  12.7 94.1 all-gather.7
  109.1 118.6 all-gather.5
  229.9 96.8 all-gather.9
  441.9 84.5 all-reduce.3

commit v2 on v1

--- a/solution.py
+++ b/solution.py
@@ -149,6 +149,20 @@
             from_slow.append(grid.cross(part, s))
     for got in from_slow:
         total = total + got.astype(F32)
+    return total
+
+
+def scatter_rows(grid, rows):
+    per_core = grid.mid * grid.slow
+    total = rows[:per_core]
+    for c in range(1, grid.cores):
+        total = total + grid.shift(rows[c * per_core : (c + 1) * per_core], core=c)
+    rows, total = total, total[: grid.slow]
+    for m in range(1, grid.mid):
+        total = total + grid.shift(rows[m * grid.slow : (m + 1) * grid.slow], mid=m)
+    rows, total = total, total[0]
+    for s in range(1, grid.slow):
+        total = total + grid.cross(rows[s], s)
     return total
 
 
@@ -355,15 +369,10 @@
     norm_terms = jnp.stack([gain_one, gain_two, shift_one, shift_two])
     norm_terms = jnp.swapaxes(norm_terms.reshape(4, count, block), 0, 1).reshape(count, 4 * block)
     bias_terms = jnp.transpose(bias_terms.reshape(3, heads, count, piece), (2, 0, 1, 3)).reshape(count, -1)
-    terms = jnp.concatenate([norm_terms, bias_terms], axis=1)
-    n_terms = terms.shape[1]
-    term_rows = 8 * (-(-n_terms // (8 * 128)))
-    terms = jnp.pad(terms, ((0, 0), (0, term_rows * 128 - n_terms))).reshape(count * term_rows, 128)
-    terms = lax.psum(terms, "fsdp")
-    terms = lax.dynamic_slice_in_dim(terms, lax.axis_index("fsdp") * term_rows, term_rows, 0).reshape(-1)
+    terms = scatter_rows(grid, jnp.concatenate([norm_terms, bias_terms], axis=1)[order])
     norm_part = terms[: 4 * block].reshape(4, block)
     norm_part = norm_part + other(norm_part)
-    bias_part = terms[4 * block : n_terms].reshape(3, heads, piece)
+    bias_part = terms[4 * block :].reshape(3, heads, piece)
     return (
         block_output,
         input_grad,

time: 1010 us -> 933 us (0.924)
  waiting for transfers between devices: 637 us -> 561 us
    psum x1 -> x0, waiting for transfers between devices: 84.7 us -> none  [shards(): terms = lax.psum(terms, 'fsdp')]
    ppermute x18 -> x20, waiting for transfers between devices: 165 us -> 167 us  [shift(): return lax.ppermute(rows, 'fsdp', self.moves(**by))]
    ppermute x32 -> x35, starting transfers between devices: 58.6 us -> 56.5 us  [cross(): return lax.ppermute(rows, 'fsdp', moves)]
    unnamed x208 -> x198, local copies, waits for them, and re-layouts: 28.7 us -> 27.6 us
    ppermute x32 -> x35, waiting for transfers between devices: 150 us -> 150 us  [cross(): return lax.ppermute(rows, 'fsdp', moves)]
  transfers between devices with their start and end apart: 63 -> 67, of which waited for: 33 -> 35; matrix products, arithmetic and copies ran while one was open for 20% -> 22% of each run, Pallas kernels for 2% -> 2%
where the time goes in v2:
time: 933 us; the launch traced here: 927 us
  waiting for transfers between devices  561 us (60%)
  matrix products  167 us (18%)
  starting transfers between devices  80.3 us (9%)
  local copies, waits for them, and re-layouts  55.9 us (6%)
  other arithmetic  30.6 us (3%)
  Pallas kernels  16.2 us (2%)
  between operations  16 us (2%)
    ppermute x20, waiting for transfers between devices, shift(): return lax.ppermute(rows, 'fsdp', self.moves(**by))  167 us
    ppermute x35, waiting for transfers between devices, cross(): return lax.ppermute(rows, 'fsdp', moves)  150 us
    dot_general x51, matrix products, times(): lax.dot_general(left, right, (((1,), (0,)), ((), ())), preferred_element_...  126 us
    all_gather x1, waiting for transfers between devices, shards(): w_down = lax.all_gather(down_weight[0], 'fsdp', axis=1, tiled=True)  81.1 us
    all_gather x1, waiting for transfers between devices, shards(): packs = lax.all_gather(pack, 'fsdp', axis=0)  74.4 us
    ppermute x35, starting transfers between devices, cross(): return lax.ppermute(rows, 'fsdp', moves)  56.5 us
    all_gather x1, waiting for transfers between devices, shards(): lax.all_gather(jnp.swapaxes(gate_up_weight[0], 0, 1), 'fsdp', axis=1, til...  44.7 us
    ppermute x9, waiting for transfers between devices, other(): return lax.ppermute(rows, 'tp', [(0, 1), (1, 0)])  42.6 us
  transfers between devices with their start and end apart: 67, of which 35 were waited for; matrix products, arithmetic and copies ran while one was open for 22% of the time, Pallas kernels for 2%

profile of v2, /device:TPU:0, one launch (start us, length us, event | category | flops | bytes accessed | tf_op | source)
XLA Modules:
  0.0 927.4 jit_solution(6128178513580349152)
XLA Ops:
  12.7 2.7 copy.95
  16.1 3.0 collective-permute-start
  22.0 10.0 %collective-permute-done = bf16[128,2048]{1,0:T(8,128)(2,1)S(1)} collective-permute-done((bf16[128,2048]{1,0:T(8,128)(2,1)S(1)}, bf16[128,2048]{1,0:T(8,128)(2,1)S(1)}, u32[]{:S(2)}, u32[]{:S(2)}) %collective-permute-start) | collective-permute-done | bytes 524320 | tf_op jit(solution)/shard_map/ppermute | solution.py:170
  32.6 74.4 %all-gather.8.cloned.1.call-done = bf16[8448,1024]{1,0:T(8,128)(2,1)} async-done(((bf16[528,1024]{1,0:T(8,128)(2,1)}), bf16[8448,1024]{1,0:T(8,128)(2,1)}) %all-gather.8.cloned.1.call-update) | async-done | bytes 17301520 | tf_op jit(solution)/shard_map/all_gather | solution.py:275
  109.9 11.5 %fusion.232 = (bf16[16,128,1024]{2,1,0:T(8,128)(2,1)}, bf16[16,128,1024]{2,1,0:T(8,128)(2,1)}, bf16[16,128,1024]{2,1,0:T(8,128)(2,1)}, bf16[16,128,1024]{2,1,0:T(8,128)(2,1)S(1)}) fusion(bf16[16,528,1024]{2,1,0:T(8,128)(2,1)} %bitcast.215), kind=kLoop, calls=%fused_computation.398 | loop fusion | bytes 33554432 | tf_op jit(solution)/shard_map/slice | solution.py:280
  126.0 4.6 convolution_add_fusion.16
  132.6 4.4 convolution_add_fusion.17
  150.1 11.1 %collective-permute-done.1 = bf16[128,2048]{1,0:T(8,128)(2,1)S(1)} collective-permute-done((bf16[128,2048]{1,0:T(8,128)(2,1)S(1)}, bf16[128,2048]{1,0:T(8,128)(2,1)S(1)}, u32[]{:S(2)}, u32[]{:S(2)}) %collective-permute-start.1) | collective-permute-done | bytes 524320 | tf_op jit(solution)/shard_map/ppermute | solution.py:170
  167.1 4.1 shard_map.172
  171.2 4.0 shard_map.169
  179.0 4.1 shard_map.171
  183.1 44.7 %all-gather.6.cloned.1.call-done = bf16[2,2048,2816]{2,1,0:T(8,128)(2,1)} async-done(((bf16[2,128,2816]{2,1,0:T(8,128)(2,1)}), bf16[2,2048,2816]{2,1,0:T(8,128)(2,1)}) %all-gather.6.cloned.1.call-update) | async-done | bytes 23068688 | tf_op jit(solution)/shard_map/all_gather | solution.py:276
  227.8 6.8 fusion.5
  234.6 11.2 %multiply_convert_fusion.3 = (bf16[256,2816]{1,0:T(8,128)(2,1)S(1)}, f32[256,2816]{1,0:T(8,128)}) fusion(f32[256,2816]{1,0:T(8,128)S(1)} %fusion.5, bf16[2,2048,2816]{2,1,0:T(8,128)(2,1)} %all-gather.6.cloned.1.call-done, bf16[128,2048]{1,0:T(8,128)(2,1)} %collective-permute-done.3, bf16[128,2048]{1,0:T(8,128)(2,1)} %add_convert_fusion.7), kind=kOutput, calls=%fused_computation.52 | convolution fusion | flops 2959212544 | bytes 19791872 | tf_op jit(solution)/shard_map/dot_general | solution.py:22
  245.8 81.1 %all-gather.10.cloned.1.call-done = bf16[1,2816,2048]{2,1,0:T(8,128)(2,1)} async-done(((bf16[1,2816,128]{2,1,0:T(8,128)(2,1)}), bf16[1,2816,2048]{2,1,0:T(8,128)(2,1)}) %all-gather.10.cloned.1.call-update) | async-done | bytes 11534352 | tf_op jit(solution)/shard_map/all_gather | solution.py:277
  326.9 10.2 %multiply_convert_fusion.1 = (bf16[256,2816]{1,0:T(8,128)(2,1)S(1)}, bf16[256,2816]{1,0:T(8,128)(2,1)S(1)}) fusion(f32[256,2816]{1,0:T(8,128)} %copy-done.91, f32[256,2816]{1,0:T(8,128)} %get-tuple-element.14, bf16[256,2048]{1,0:T(8,128)(2,1)} %copy-done.30, bf16[1,2816,2048]{2,1,0:T(8,128)(2,1)} %all-gather.10.cloned.1.call-done), kind=kOutput, calls=%fused_computation.49 | convolution fusion | flops 2962161664 | bytes 21233664 | tf_op jit(solution)/shard_map/dot_general | solution.py:26
  337.1 7.1 fusion.4
  344.1 6.6 fusion.30
  352.4 2.6 convolution_convert_fusion.1
  355.0 2.7 convolution_convert_fusion.2
  357.6 2.5 convolution_convert_fusion.3
  360.2 4.8 collective-permute-done.4
  366.1 2.6 fusion.230
  370.1 2.6 convolution_convert_fusion.4
  373.2 4.2 convolution_convert_fusion
  377.4 4.5 collective-permute-done.5
  386.6 3.8 multiply_convert_fusion
  396.1 4.1 shard_map.170
  400.1 3.6 fusion.239
  414.7 9.3 %fusion = f32[256,2048]{1,0:T(8,128)} fusion(bf16[256,2816]{1,0:T(8,128)(2,1)} %copy-done.9, bf16[1,2816,2048]{2,1,0:T(8,128)(2,1)} %all-gather.10.cloned.1.call-done), kind=kOutput, calls=%fused_computation.3 | convolution fusion | flops 2952790016 | bytes 15073280 | tf_op jit(solution)/shard_map/dot_general | solution.py:22
  446.6 8.3 collective-permute-done.6
  455.5 3.0 collective-permute-done.13
  466.8 2.4 fusion.23
  483.0 16.2 %collective-permute-done.25 = bf16[512,1024]{1,0:T(8,128)(2,1)S(1)} collective-permute-done((bf16[512,1024]{1,0:T(8,128)(2,1)S(1)}, bf16[512,1024]{1,0:T(8,128)(2,1)S(1)}, u32[]{:S(2)}, u32[]{:S(2)}) %collective-permute-start.25) | collective-permute-done | bytes 1048608 | tf_op jit(solution)/shard_map/ppermute | solution.py:53
  505.3 78.1 %collective-permute-done.20 = bf16[512,1024]{1,0:T(8,128)(2,1)S(1)} collective-permute-done((bf16[512,1024]{1,0:T(8,128)(2,1)S(1)}, bf16[512,1024]{1,0:T(8,128)(2,1)S(1)}, u32[]{:S(2)}, u32[]{:S(2)}) %collective-permute-start.20) | collective-permute-done | bytes 1048608 | tf_op jit(solution)/shard_map/ppermute | solution.py:53
  590.2 15.7 %collective-permute-done.15 = bf16[512,1024]{1,0:T(8,128)(2,1)S(1)} collective-permute-done((bf16[512,1024]{1,0:T(8,128)(2,1)S(1)}, bf16[512,1024]{1,0:T(8,128)(2,1)S(1)}, u32[]{:S(2)}, u32[]{:S(2)}) %collective-permute-start.15) | collective-permute-done | bytes 1048608 | tf_op jit(solution)/shard_map/ppermute | solution.py:53
  609.8 18.5 %collective-permute-done.30 = bf16[512,1024]{1,0:T(8,128)(2,1)S(1)} collective-permute-done((bf16[512,1024]{1,0:T(8,128)(2,1)S(1)}, bf16[512,1024]{1,0:T(8,128)(2,1)S(1)}, u32[]{:S(2)}, u32[]{:S(2)}) %collective-permute-start.30) | collective-permute-done | bytes 1048608 | tf_op jit(solution)/shard_map/ppermute | solution.py:53
  634.2 2.9 fusion.28
  638.9 2.5 collective-permute-start.33
  644.4 3.7 add_convert_fusion
  648.1 11.1 %collective-permute-done.41 = bf16[512,1408]{1,0:T(8,128)(2,1)S(1)} collective-permute-done((bf16[512,1408]{1,0:T(8,128)(2,1)S(1)}, bf16[512,1408]{1,0:T(8,128)(2,1)S(1)}, u32[]{:S(2)}, u32[]{:S(2)}) %collective-permute-start.41) | collective-permute-done | bytes 1441824 | tf_op jit(solution)/shard_map/ppermute | solution.py:53
  662.8 27.3 %collective-permute-done.35 = bf16[512,1408]{1,0:T(8,128)(2,1)S(1)} collective-permute-done((bf16[512,1408]{1,0:T(8,128)(2,1)S(1)}, bf16[512,1408]{1,0:T(8,128)(2,1)S(1)}, u32[]{:S(2)}, u32[]{:S(2)}) %collective-permute-start.35) | collective-permute-done | bytes 1441824 | tf_op jit(solution)/shard_map/ppermute | solution.py:53
  696.9 3.0 collective-permute-start.23
  699.8 4.1 collective-permute-start.54
  707.0 4.5 collective-permute-done.27
  712.8 4.2 collective-permute-done.23
  717.1 2.8 collective-permute-start.18
  721.5 22.9 %collective-permute-done.22 = bf16[128,1024]{1,0:T(8,128)(2,1)S(1)} collective-permute-done((bf16[128,1024]{1,0:T(8,128)(2,1)}, bf16[128,1024]{1,0:T(8,128)(2,1)S(1)}, u32[]{:S(2)}, u32[]{:S(2)}) %collective-permute-start.22) | collective-permute-done | bytes 262176 | tf_op jit(solution)/shard_map/ppermute | solution.py:67
  744.4 3.3 collective-permute-start.17
  752.4 4.7 collective-permute-done.18
  760.1 2.7 collective-permute-done.17
  762.8 2.4 collective-permute-start.42
  766.9 4.3 collective-permute-start.36
  776.7 13.4 %collective-permute-done.48 = bf16[384,1408]{1,0:T(8,128)(2,1)S(1)} collective-permute-done((bf16[384,1408]{1,0:T(8,128)(2,1)}, bf16[384,1408]{1,0:T(8,128)(2,1)S(1)}, u32[]{:S(2)}, u32[]{:S(2)}) %collective-permute-start.48) | collective-permute-done | bytes 1081376 | tf_op jit(solution)/shard_map/ppermute | solution.py:67
  792.9 3.2 fusion.9
  796.8 16.3 %collective-permute-done.42 = bf16[384,1408]{1,0:T(8,128)(2,1)S(1)} collective-permute-done((bf16[384,1408]{1,0:T(8,128)(2,1)S(1)}, bf16[384,1408]{1,0:T(8,128)(2,1)S(1)}, u32[]{:S(2)}, u32[]{:S(2)}) %collective-permute-start.42) | collective-permute-done | bytes 1081376 | tf_op jit(solution)/shard_map/ppermute | solution.py:67
  813.1 4.5 collective-permute-start.60
  819.8 16.5 %collective-permute-done.36 = bf16[384,1408]{1,0:T(8,128)(2,1)S(1)} collective-permute-done((bf16[384,1408]{1,0:T(8,128)(2,1)S(1)}, bf16[384,1408]{1,0:T(8,128)(2,1)S(1)}, u32[]{:S(2)}, u32[]{:S(2)}) %collective-permute-start.36) | collective-permute-done | bytes 1081376 | tf_op jit(solution)/shard_map/ppermute | solution.py:67
  843.1 7.4 collective-permute-done.50
  854.0 11.8 %collective-permute-done.44 = bf16[128,1408]{1,0:T(8,128)(2,1)S(1)} collective-permute-done((bf16[128,1408]{1,0:T(8,128)(2,1)S(1)}, bf16[128,1408]{1,0:T(8,128)(2,1)S(1)}, u32[]{:S(2)}, u32[]{:S(2)}) %collective-permute-start.44) | collective-permute-done | bytes 360480 | tf_op jit(solution)/shard_map/ppermute | solution.py:67
  867.5 9.4 %collective-permute-done.38 = bf16[128,1408]{1,0:T(8,128)(2,1)S(1)} collective-permute-done((bf16[128,1408]{1,0:T(8,128)(2,1)S(1)}, bf16[128,1408]{1,0:T(8,128)(2,1)S(1)}, u32[]{:S(2)}, u32[]{:S(2)}) %collective-permute-start.38) | collective-permute-done | bytes 360480 | tf_op jit(solution)/shard_map/ppermute | solution.py:67
  883.5 3.8 copy.84
  887.3 6.6 collective-permute-done.61
  893.9 22.9 %collective-permute-done.62 = bf16[128,2816]{1,0:T(8,128)(2,1)S(1)} collective-permute-done((bf16[128,2816]{1,0:T(8,128)(2,1)S(1)}, bf16[128,2816]{1,0:T(8,128)(2,1)S(1)}, u32[]{:S(2)}, u32[]{:S(2)}) %collective-permute-start.62) | collective-permute-done | bytes 720928 | tf_op jit(solution)/shard_map/ppermute | solution.py:67
  (453 shorter events, 198.6 us)
Async XLA Ops:
  7.2 99.8 %all-gather.8.cloned.1.call-start = ((), (), s32[]{:S(2)}) async-start(), calls=%async_computation.1 | async-start | bytes 18382848 | tf_op jit(solution)/shard_map/all_gather | solution.py:275
  12.6 215.2 %all-gather.6.cloned.1.call-start = ((), (), s32[]{:S(2)}) async-start(), calls=%async_computation | async-start | bytes 24510464 | tf_op jit(solution)/shard_map/all_gather | solution.py:276
  15.4 311.5 %all-gather.10.cloned.1.call-start = ((), (), s32[]{:S(2)}) async-start(), calls=%async_computation.2 | async-start | bytes 12255232 | tf_op jit(solution)/shard_map/all_gather | solution.py:277
  16.1 15.8 %collective-permute-start = (bf16[128,2048]{1,0:T(8,128)(2,1)S(1)}, bf16[128,2048]{1,0:T(8,128)(2,1)S(1)}, u32[]{:S(2)}, u32[]{:S(2)}) collective-permute-start(bf16[128,2048]{1,0:T(8,128)(2,1)S(1)} %copy-done), channel_id=1, source_target_pairs={{0,1},{1,0},{2,3},{3,2},{4,5},{5,4},{6,7},{7,6},{8,9},{9,8},{10,11... | collective-permute-start | bytes 1572872 | tf_op jit(solution)/shard_map/ppermute | solution.py:170
  19.1 145.9 %collective-permute-start.2 = (bf16[128,2048]{1,0:T(8,128)(2,1)}, bf16[128,2048]{1,0:T(8,128)(2,1)}, u32[]{:S(2)}, u32[]{:S(2)}) collective-permute-start(bf16[128,2048]{1,0:T(8,128)(2,1)} %param.12), channel_id=1, source_target_pairs={{0,1},{1,0},{2,3},{3,2},{4,5},{5,4},{6,7},{7,6},{8,9},{9,8},{10,11... | collective-permute-start | bytes 1572872 | tf_op jit(solution)/shard_map/ppermute | solution.py:170
  146.9 14.3 %collective-permute-start.1 = (bf16[128,2048]{1,0:T(8,128)(2,1)S(1)}, bf16[128,2048]{1,0:T(8,128)(2,1)S(1)}, u32[]{:S(2)}, u32[]{:S(2)}) collective-permute-start(bf16[128,2048]{1,0:T(8,128)(2,1)S(1)} %slice.1201), channel_id=1, source_target_pairs={{0,1},{1,0},{2,3},{3,2},{4,5},{5,4},{6,7},{7,6},{8,9},{9,8},{10,11... | collective-permute-start | bytes 1572872 | tf_op jit(solution)/shard_map/ppermute | solution.py:170
  162.9 13.8 %collective-permute-start.3 = (bf16[128,2048]{1,0:T(8,128)(2,1)}, bf16[128,2048]{1,0:T(8,128)(2,1)}, u32[]{:S(2)}, u32[]{:S(2)}) collective-permute-start(bf16[128,2048]{1,0:T(8,128)(2,1)} %add_convert_fusion.7), channel_id=1, source_target_pairs={{0,1},{1,0},{2,3},{3,2},{4,5},{5,4},{6,7},{7,6},{8,9},{9,8},{10,11... | collective-permute-start | bytes 1572872 | tf_op jit(solution)/shard_map/ppermute | solution.py:170
  350.8 14.1 %collective-permute-start.4 = (bf16[128,2048]{1,0:T(8,128)(2,1)S(1)}, bf16[128,2048]{1,0:T(8,128)(2,1)S(1)}, u32[]{:S(2)}, u32[]{:S(2)}) collective-permute-start(bf16[128,2048]{1,0:T(8,128)(2,1)S(1)} %slice.1200), channel_id=1, source_target_pairs={{0,1},{1,0},{2,3},{3,2},{4,5},{5,4},{6,7},{7,6},{8,9},{9,8},{10,11... | collective-permute-start | bytes 1572872 | tf_op jit(solution)/shard_map/ppermute | solution.py:170
  368.6 13.2 %collective-permute-start.5 = (bf16[128,2048]{1,0:T(8,128)(2,1)S(1)}, bf16[128,2048]{1,0:T(8,128)(2,1)S(1)}, u32[]{:S(2)}, u32[]{:S(2)}) collective-permute-start(bf16[128,2048]{1,0:T(8,128)(2,1)S(1)} %get-tuple-element.58), channel_id=1, source_target_pairs={{0,1},{1,0},{2,3},{3,2},{4,5},{5,4},{6,7},{7,6},{8,9},{9,8},{10,11... | collective-permute-start | bytes 1572872 | tf_op jit(solution)/shard_map/ppermute | solution.py:170
  372.7 88.2 %collective-permute-start.52 = (bf16[1024,1408]{1,0:T(8,128)(2,1)}, bf16[1024,1408]{1,0:T(8,128)(2,1)}, u32[]{:S(2)}, u32[]{:S(2)}) collective-permute-start(bf16[1024,1408]{1,0:T(8,128)(2,1)} %convolution_convert_fusion.1), channel_id=1, source_target_pairs={{0,2},{2,0},{4,6},{6,4},{8,10},{10,8},{12,14},{14,12},{16,18},{18,... | collective-permute-start | bytes 8650760 | tf_op jit(solution)/shard_map/ppermute | solution.py:53
  372.7 90.7 %collective-permute-start.46 = (bf16[1024,1408]{1,0:T(8,128)(2,1)}, bf16[1024,1408]{1,0:T(8,128)(2,1)}, u32[]{:S(2)}, u32[]{:S(2)}) collective-permute-start(bf16[1024,1408]{1,0:T(8,128)(2,1)} %convolution_convert_fusion.2), channel_id=1, source_target_pairs={{0,2},{2,0},{4,6},{6,4},{8,10},{10,8},{12,14},{14,12},{16,18},{18,... | collective-permute-start | bytes 8650760 | tf_op jit(solution)/shard_map/ppermute | solution.py:53
  373.2 90.8 %collective-permute-start.40 = (bf16[1024,1408]{1,0:T(8,128)(2,1)}, bf16[1024,1408]{1,0:T(8,128)(2,1)}, u32[]{:S(2)}, u32[]{:S(2)}) collective-permute-start(bf16[1024,1408]{1,0:T(8,128)(2,1)} %convolution_convert_fusion.3), channel_id=1, source_target_pairs={{0,2},{2,0},{4,6},{6,4},{8,10},{10,8},{12,14},{14,12},{16,18},{18,... | collective-permute-start | bytes 8650760 | tf_op jit(solution)/shard_map/ppermute | solution.py:53
  412.8 15.5 %collective-permute-start.7 = (bf16[128,2048]{1,0:T(8,128)(2,1)}, bf16[128,2048]{1,0:T(8,128)(2,1)}, u32[]{:S(2)}, u32[]{:S(2)}) collective-permute-start(bf16[128,2048]{1,0:T(8,128)(2,1)} %slice.1198), channel_id=1, source_target_pairs={{0,1},{1,0},{2,3},{3,2},{4,5},{5,4},{6,7},{7,6},{8,9},{9,8},{10,11... | collective-permute-start | bytes 1572872 | tf_op jit(solution)/shard_map/ppermute | solution.py:170
  433.1 3.8 collective-permute-start.9
  436.9 5.5 collective-permute-start.12
  438.4 4.5 collective-permute-start.11
  442.4 12.5 %collective-permute-start.6 = (bf16[128,2048]{1,0:T(8,128)(2,1)S(1)}, bf16[128,2048]{1,0:T(8,128)(2,1)S(1)}, u32[]{:S(2)}, u32[]{:S(2)}) collective-permute-start(bf16[128,2048]{1,0:T(8,128)(2,1)S(1)} %slice.1199), channel_id=1, source_target_pairs={{0,1},{1,0},{2,3},{3,2},{4,5},{5,4},{6,7},{7,6},{8,9},{9,8},{10,11... | collective-permute-start | bytes 1572872 | tf_op jit(solution)/shard_map/ppermute | solution.py:170
  446.6 20.2 %collective-permute-start.24 = (bf16[1024,1024]{1,0:T(8,128)(2,1)}, bf16[1024,1024]{1,0:T(8,128)(2,1)}, u32[]{:S(2)}, u32[]{:S(2)}) collective-permute-start(bf16[1024,1024]{1,0:T(8,128)(2,1)} %convolution_convert_fusion.6), channel_id=1, source_target_pairs={{0,2},{2,0},{4,6},{6,4},{8,10},{10,8},{12,14},{14,12},{16,18},{18,... | collective-permute-start | bytes 6291464 | tf_op jit(solution)/shard_map/ppermute | solution.py:53
  458.5 14.6 %collective-permute-start.34 = (bf16[1024,1408]{1,0:T(8,128)(2,1)}, bf16[1024,1408]{1,0:T(8,128)(2,1)}, u32[]{:S(2)}, u32[]{:S(2)}) collective-permute-start(bf16[1024,1408]{1,0:T(8,128)(2,1)} %convolution_convert_fusion.4), channel_id=1, source_target_pairs={{0,2},{2,0},{4,6},{6,4},{8,10},{10,8},{12,14},{14,12},{16,18},{18,... | collective-permute-start | bytes 8650760 | tf_op jit(solution)/shard_map/ppermute | solution.py:53
  460.9 15.1 %collective-permute-start.19 = (bf16[1024,1024]{1,0:T(8,128)(2,1)}, bf16[1024,1024]{1,0:T(8,128)(2,1)}, u32[]{:S(2)}, u32[]{:S(2)}) collective-permute-start(bf16[1024,1024]{1,0:T(8,128)(2,1)} %convolution_convert_fusion.7), channel_id=1, source_target_pairs={{0,2},{2,0},{4,6},{6,4},{8,10},{10,8},{12,14},{14,12},{16,18},{18,... | collective-permute-start | bytes 6291464 | tf_op jit(solution)/shard_map/ppermute | solution.py:53
  463.4 15.5 %collective-permute-start.14 = (bf16[1024,1024]{1,0:T(8,128)(2,1)}, bf16[1024,1024]{1,0:T(8,128)(2,1)S(1)}, u32[]{:S(2)}, u32[]{:S(2)}) collective-permute-start(bf16[1024,1024]{1,0:T(8,128)(2,1)} %convolution_convert_fusion.8), channel_id=1, source_target_pairs={{0,2},{2,0},{4,6},{6,4},{8,10},{10,8},{12,14},{14,12},{16,18},{18,... | collective-permute-start | bytes 6291464 | tf_op jit(solution)/shard_map/ppermute | solution.py:53
  464.0 16.4 %collective-permute-start.29 = (bf16[1024,1024]{1,0:T(8,128)(2,1)}, bf16[1024,1024]{1,0:T(8,128)(2,1)S(1)}, u32[]{:S(2)}, u32[]{:S(2)}) collective-permute-start(bf16[1024,1024]{1,0:T(8,128)(2,1)} %convolution_convert_fusion.5), channel_id=1, source_target_pairs={{0,2},{2,0},{4,6},{6,4},{8,10},{10,8},{12,14},{14,12},{16,18},{18,... | collective-permute-start | bytes 6291464 | tf_op jit(solution)/shard_map/ppermute | solution.py:53
  466.7 177.3 %collective-permute-start.58 = (bf16[1024,2816]{1,0:T(8,128)(2,1)}, bf16[1024,2816]{1,0:T(8,128)(2,1)S(1)}, u32[]{:S(2)}, u32[]{:S(2)}) collective-permute-start(bf16[1024,2816]{1,0:T(8,128)(2,1)} %convolution_convert_fusion), channel_id=1, source_target_pairs={{0,2},{2,0},{4,6},{6,4},{8,10},{10,8},{12,14},{14,12},{16,18},{18,... | collective-permute-start | bytes 17301512 | tf_op jit(solution)/shard_map/ppermute | solution.py:53
  473.1 26.1 %collective-permute-start.25 = (bf16[512,1024]{1,0:T(8,128)(2,1)S(1)}, bf16[512,1024]{1,0:T(8,128)(2,1)S(1)}, u32[]{:S(2)}, u32[]{:S(2)}) collective-permute-start(bf16[512,1024]{1,0:T(8,128)(2,1)S(1)} %add_convert_fusion.2), channel_id=1, source_target_pairs={{0,4},{2,6},{4,0},{6,2},{8,12},{10,14},{12,8},{14,10},{16,20},{18,... | collective-permute-start | bytes 3145736 | tf_op jit(solution)/shard_map/ppermute | solution.py:53
  476.0 156.8 %collective-permute-start.53 = (bf16[512,1408]{1,0:T(8,128)(2,1)S(1)}, bf16[512,1408]{1,0:T(8,128)(2,1)S(1)}, u32[]{:S(2)}, u32[]{:S(2)}) collective-permute-start(bf16[512,1408]{1,0:T(8,128)(2,1)S(1)} %fusion.24), channel_id=1, source_target_pairs={{0,4},{2,6},{4,0},{6,2},{8,12},{10,14},{12,8},{14,10},{16,20},{18,... | collective-permute-start | bytes 4325384 | tf_op jit(solution)/shard_map/ppermute | solution.py:53
  478.9 160.0 %collective-permute-start.47 = (bf16[512,1408]{1,0:T(8,128)(2,1)S(1)}, bf16[512,1408]{1,0:T(8,128)(2,1)S(1)}, u32[]{:S(2)}, u32[]{:S(2)}) collective-permute-start(bf16[512,1408]{1,0:T(8,128)(2,1)S(1)} %fusion.23), channel_id=1, source_target_pairs={{0,4},{2,6},{4,0},{6,2},{8,12},{10,14},{12,8},{14,10},{16,20},{18,... | collective-permute-start | bytes 4325384 | tf_op jit(solution)/shard_map/ppermute | solution.py:53
  480.3 103.1 %collective-permute-start.20 = (bf16[512,1024]{1,0:T(8,128)(2,1)S(1)}, bf16[512,1024]{1,0:T(8,128)(2,1)S(1)}, u32[]{:S(2)}, u32[]{:S(2)}) collective-permute-start(bf16[512,1024]{1,0:T(8,128)(2,1)S(1)} %add_convert_fusion.3), channel_id=1, source_target_pairs={{0,4},{2,6},{4,0},{6,2},{8,12},{10,14},{12,8},{14,10},{16,20},{18,... | collective-permute-start | bytes 3145736 | tf_op jit(solution)/shard_map/ppermute | solution.py:53
  499.2 106.7 %collective-permute-start.15 = (bf16[512,1024]{1,0:T(8,128)(2,1)S(1)}, bf16[512,1024]{1,0:T(8,128)(2,1)S(1)}, u32[]{:S(2)}, u32[]{:S(2)}) collective-permute-start(bf16[512,1024]{1,0:T(8,128)(2,1)S(1)} %add_convert_fusion.4), channel_id=1, source_target_pairs={{0,4},{2,6},{4,0},{6,2},{8,12},{10,14},{12,8},{14,10},{16,20},{18,... | collective-permute-start | bytes 3145736 | tf_op jit(solution)/shard_map/ppermute | solution.py:53
  583.4 44.9 %collective-permute-start.30 = (bf16[512,1024]{1,0:T(8,128)(2,1)S(1)}, bf16[512,1024]{1,0:T(8,128)(2,1)S(1)}, u32[]{:S(2)}, u32[]{:S(2)}) collective-permute-start(bf16[512,1024]{1,0:T(8,128)(2,1)S(1)} %add_convert_fusion.1), channel_id=1, source_target_pairs={{0,4},{2,6},{4,0},{6,2},{8,12},{10,14},{12,8},{14,10},{16,20},{18,... | collective-permute-start | bytes 3145736 | tf_op jit(solution)/shard_map/ppermute | solution.py:53
  605.9 53.4 %collective-permute-start.41 = (bf16[512,1408]{1,0:T(8,128)(2,1)S(1)}, bf16[512,1408]{1,0:T(8,128)(2,1)S(1)}, u32[]{:S(2)}, u32[]{:S(2)}) collective-permute-start(bf16[512,1408]{1,0:T(8,128)(2,1)S(1)} %fusion.22), channel_id=1, source_target_pairs={{0,4},{2,6},{4,0},{6,2},{8,12},{10,14},{12,8},{14,10},{16,20},{18,... | collective-permute-start | bytes 4325384 | tf_op jit(solution)/shard_map/ppermute | solution.py:53
  628.4 61.8 %collective-permute-start.35 = (bf16[512,1408]{1,0:T(8,128)(2,1)S(1)}, bf16[512,1408]{1,0:T(8,128)(2,1)S(1)}, u32[]{:S(2)}, u32[]{:S(2)}) collective-permute-start(bf16[512,1408]{1,0:T(8,128)(2,1)S(1)} %fusion.21), channel_id=1, source_target_pairs={{0,4},{2,6},{4,0},{6,2},{8,12},{10,14},{12,8},{14,10},{16,20},{18,... | collective-permute-start | bytes 4325384 | tf_op jit(solution)/shard_map/ppermute | solution.py:53
  632.8 62.7 %collective-permute-start.28 = (bf16[128,1024]{1,0:T(8,128)(2,1)S(1)}, bf16[128,1024]{1,0:T(8,128)(2,1)}, u32[]{:S(2)}, u32[]{:S(2)}) collective-permute-start(bf16[128,1024]{1,0:T(8,128)(2,1)S(1)} %add_convert_fusion.19), channel_id=1, source_target_pairs={{0,24},{2,26},{4,28},{6,30},{8,16},{10,18},{12,20},{14,22},{16,8},... | collective-permute-start | bytes 786440 | tf_op jit(solution)/shard_map/ppermute | solution.py:67
  638.9 56.9 %collective-permute-start.33 = (bf16[128,1024]{1,0:T(8,128)(2,1)S(1)}, bf16[128,1024]{1,0:T(8,128)(2,1)S(1)}, u32[]{:S(2)}, u32[]{:S(2)}) collective-permute-start(bf16[128,1024]{1,0:T(8,128)(2,1)S(1)} %add_convert_fusion.16), channel_id=1, source_target_pairs={{0,24},{2,26},{4,28},{6,30},{8,16},{10,18},{12,20},{14,22},{16,8},... | collective-permute-start | bytes 786440 | tf_op jit(solution)/shard_map/ppermute | solution.py:67
  644.3 52.6 %collective-permute-start.32 = (bf16[128,1024]{1,0:T(8,128)(2,1)S(1)}, bf16[128,1024]{1,0:T(8,128)(2,1)S(1)}, u32[]{:S(2)}, u32[]{:S(2)}) collective-permute-start(bf16[128,1024]{1,0:T(8,128)(2,1)S(1)} %add_convert_fusion.17), channel_id=1, source_target_pairs={{0,16},{2,18},{4,20},{6,22},{8,24},{10,26},{12,28},{14,30},{16,0},... | collective-permute-start | bytes 786440 | tf_op jit(solution)/shard_map/ppermute | solution.py:67
  659.3 132.3 %collective-permute-start.59 = (bf16[512,2816]{1,0:T(8,128)(2,1)}, bf16[512,2816]{1,0:T(8,128)(2,1)}, u32[]{:S(2)}, u32[]{:S(2)}) collective-permute-start(bf16[512,2816]{1,0:T(8,128)(2,1)} %add_convert_fusion), channel_id=1, source_target_pairs={{0,4},{2,6},{4,0},{6,2},{8,12},{10,14},{12,8},{14,10},{16,20},{18,... | collective-permute-start | bytes 8650760 | tf_op jit(solution)/shard_map/ppermute | solution.py:53
  690.2 9.7 %collective-permute-start.31 = (bf16[128,1024]{1,0:T(8,128)(2,1)S(1)}, bf16[128,1024]{1,0:T(8,128)(2,1)S(1)}, u32[]{:S(2)}, u32[]{:S(2)}) collective-permute-start(bf16[128,1024]{1,0:T(8,128)(2,1)S(1)} %add_convert_fusion.18), channel_id=1, source_target_pairs={{0,8},{2,10},{4,12},{6,14},{8,0},{10,2},{12,4},{14,6},{16,24},{18,... | collective-permute-start | bytes 786440 | tf_op jit(solution)/shard_map/ppermute | solution.py:67
  695.4 16.0 %collective-permute-start.27 = (bf16[128,1024]{1,0:T(8,128)(2,1)}, bf16[128,1024]{1,0:T(8,128)(2,1)}, u32[]{:S(2)}, u32[]{:S(2)}) collective-permute-start(bf16[128,1024]{1,0:T(8,128)(2,1)} %add_convert_fusion.20), channel_id=1, source_target_pairs={{0,16},{2,18},{4,20},{6,22},{8,24},{10,26},{12,28},{14,30},{16,0},... | collective-permute-start | bytes 786440 | tf_op jit(solution)/shard_map/ppermute | solution.py:67
  695.7 15.7 %collective-permute-start.26 = (bf16[128,1024]{1,0:T(8,128)(2,1)}, bf16[128,1024]{1,0:T(8,128)(2,1)}, u32[]{:S(2)}, u32[]{:S(2)}) collective-permute-start(bf16[128,1024]{1,0:T(8,128)(2,1)} %add_convert_fusion.21), channel_id=1, source_target_pairs={{0,8},{2,10},{4,12},{6,14},{8,0},{10,2},{12,4},{14,6},{16,24},{18,... | collective-permute-start | bytes 786440 | tf_op jit(solution)/shard_map/ppermute | solution.py:67
  696.9 20.2 %collective-permute-start.23 = (bf16[128,1024]{1,0:T(8,128)(2,1)}, bf16[128,1024]{1,0:T(8,128)(2,1)}, u32[]{:S(2)}, u32[]{:S(2)}) collective-permute-start(bf16[128,1024]{1,0:T(8,128)(2,1)} %add_convert_fusion.22), channel_id=1, source_target_pairs={{0,24},{2,26},{4,28},{6,30},{8,16},{10,18},{12,20},{14,22},{16,8},... | collective-permute-start | bytes 786440 | tf_op jit(solution)/shard_map/ppermute | solution.py:67
  699.8 73.9 %collective-permute-start.54 = (bf16[384,1408]{1,0:T(8,128)(2,1)}, bf16[384,1408]{1,0:T(8,128)(2,1)}, u32[]{:S(2)}, u32[]{:S(2)}) collective-permute-start(bf16[384,1408]{1,0:T(8,128)(2,1)} %fusion.28), channel_id=1, source_target_pairs={{0,8},{2,10},{4,12},{6,14},{24,16},{26,18},{28,20},{30,22},{1,9},{... | collective-permute-start | bytes 3244040 | tf_op jit(solution)/shard_map/ppermute | solution.py:67
  711.4 32.9 %collective-permute-start.22 = (bf16[128,1024]{1,0:T(8,128)(2,1)}, bf16[128,1024]{1,0:T(8,128)(2,1)S(1)}, u32[]{:S(2)}, u32[]{:S(2)}) collective-permute-start(bf16[128,1024]{1,0:T(8,128)(2,1)} %add_convert_fusion.23), channel_id=1, source_target_pairs={{0,16},{2,18},{4,20},{6,22},{8,24},{10,26},{12,28},{14,30},{16,0},... | collective-permute-start | bytes 786440 | tf_op jit(solution)/shard_map/ppermute | solution.py:67
  711.5 38.5 %collective-permute-start.21 = (bf16[128,1024]{1,0:T(8,128)(2,1)}, bf16[128,1024]{1,0:T(8,128)(2,1)S(1)}, u32[]{:S(2)}, u32[]{:S(2)}) collective-permute-start(bf16[128,1024]{1,0:T(8,128)(2,1)} %add_convert_fusion.24), channel_id=1, source_target_pairs={{0,8},{2,10},{4,12},{6,14},{8,0},{10,2},{12,4},{14,6},{16,24},{18,... | collective-permute-start | bytes 786440 | tf_op jit(solution)/shard_map/ppermute | solution.py:67
  717.1 40.1 %collective-permute-start.18 = (bf16[128,1024]{1,0:T(8,128)(2,1)}, bf16[128,1024]{1,0:T(8,128)(2,1)S(1)}, u32[]{:S(2)}, u32[]{:S(2)}) collective-permute-start(bf16[128,1024]{1,0:T(8,128)(2,1)} %add_convert_fusion.25), channel_id=1, source_target_pairs={{0,24},{2,26},{4,28},{6,30},{8,16},{10,18},{12,20},{14,22},{16,8},... | collective-permute-start | bytes 786440 | tf_op jit(solution)/shard_map/ppermute | solution.py:67
  744.4 18.4 %collective-permute-start.17 = (bf16[128,1024]{1,0:T(8,128)(2,1)}, bf16[128,1024]{1,0:T(8,128)(2,1)S(1)}, u32[]{:S(2)}, u32[]{:S(2)}) collective-permute-start(bf16[128,1024]{1,0:T(8,128)(2,1)} %add_convert_fusion.26), channel_id=1, source_target_pairs={{0,16},{2,18},{4,20},{6,22},{8,24},{10,26},{12,28},{14,30},{16,0},... | collective-permute-start | bytes 786440 | tf_op jit(solution)/shard_map/ppermute | solution.py:67
  750.0 16.9 %collective-permute-start.16 = (bf16[128,1024]{1,0:T(8,128)(2,1)}, bf16[128,1024]{1,0:T(8,128)(2,1)S(1)}, u32[]{:S(2)}, u32[]{:S(2)}) collective-permute-start(bf16[128,1024]{1,0:T(8,128)(2,1)} %add_convert_fusion.27), channel_id=1, source_target_pairs={{0,8},{2,10},{4,12},{6,14},{8,0},{10,2},{12,4},{14,6},{16,24},{18,... | collective-permute-start | bytes 786440 | tf_op jit(solution)/shard_map/ppermute | solution.py:67
  757.1 32.9 %collective-permute-start.48 = (bf16[384,1408]{1,0:T(8,128)(2,1)}, bf16[384,1408]{1,0:T(8,128)(2,1)S(1)}, u32[]{:S(2)}, u32[]{:S(2)}) collective-permute-start(bf16[384,1408]{1,0:T(8,128)(2,1)} %copy-done.46), channel_id=1, source_target_pairs={{0,8},{2,10},{4,12},{6,14},{24,16},{26,18},{28,20},{30,22},{1,9},{... | collective-permute-start | bytes 3244040 | tf_op jit(solution)/shard_map/ppermute | solution.py:67
  762.8 50.3 %collective-permute-start.42 = (bf16[384,1408]{1,0:T(8,128)(2,1)S(1)}, bf16[384,1408]{1,0:T(8,128)(2,1)S(1)}, u32[]{:S(2)}, u32[]{:S(2)}) collective-permute-start(bf16[384,1408]{1,0:T(8,128)(2,1)S(1)} %copy-done.45), channel_id=1, source_target_pairs={{0,8},{2,10},{4,12},{6,14},{24,16},{26,18},{28,20},{30,22},{1,9},{... | collective-permute-start | bytes 3244040 | tf_op jit(solution)/shard_map/ppermute | solution.py:67
  766.9 69.4 %collective-permute-start.36 = (bf16[384,1408]{1,0:T(8,128)(2,1)S(1)}, bf16[384,1408]{1,0:T(8,128)(2,1)S(1)}, u32[]{:S(2)}, u32[]{:S(2)}) collective-permute-start(bf16[384,1408]{1,0:T(8,128)(2,1)S(1)} %copy-done.43), channel_id=1, source_target_pairs={{0,8},{2,10},{4,12},{6,14},{24,16},{26,18},{28,20},{30,22},{1,9},{... | collective-permute-start | bytes 3244040 | tf_op jit(solution)/shard_map/ppermute | solution.py:67
  773.8 22.3 %collective-permute-start.55 = (bf16[128,1408]{1,0:T(8,128)(2,1)S(1)}, bf16[128,1408]{1,0:T(8,128)(2,1)S(1)}, u32[]{:S(2)}, u32[]{:S(2)}) collective-permute-start(bf16[128,1408]{1,0:T(8,128)(2,1)S(1)} %copy-done.55), channel_id=1, source_target_pairs={{8,0},{10,2},{12,4},{14,6},{16,24},{18,26},{20,28},{22,30},{9,1},{... | collective-permute-start | bytes 1081352 | tf_op jit(solution)/shard_map/ppermute | solution.py:67
  790.0 27.8 %collective-permute-start.49 = (bf16[128,1408]{1,0:T(8,128)(2,1)S(1)}, bf16[128,1408]{1,0:T(8,128)(2,1)S(1)}, u32[]{:S(2)}, u32[]{:S(2)}) collective-permute-start(bf16[128,1408]{1,0:T(8,128)(2,1)S(1)} %copy-done.54), channel_id=1, source_target_pairs={{8,0},{10,2},{12,4},{14,6},{16,24},{18,26},{20,28},{22,30},{9,1},{... | collective-permute-start | bytes 1081352 | tf_op jit(solution)/shard_map/ppermute | solution.py:67
  791.6 27.5 %collective-permute-start.43 = (bf16[128,1408]{1,0:T(8,128)(2,1)S(1)}, bf16[128,1408]{1,0:T(8,128)(2,1)S(1)}, u32[]{:S(2)}, u32[]{:S(2)}) collective-permute-start(bf16[128,1408]{1,0:T(8,128)(2,1)S(1)} %copy-done.56), channel_id=1, source_target_pairs={{8,0},{10,2},{12,4},{14,6},{16,24},{18,26},{20,28},{22,30},{9,1},{... | collective-permute-start | bytes 1081352 | tf_op jit(solution)/shard_map/ppermute | solution.py:67
  796.1 41.5 %collective-permute-start.57 = (bf16[128,1408]{1,0:T(8,128)(2,1)S(1)}, bf16[128,1408]{1,0:T(8,128)(2,1)S(1)}, u32[]{:S(2)}, u32[]{:S(2)}) collective-permute-start(bf16[128,1408]{1,0:T(8,128)(2,1)S(1)} %get-tuple-element.77), channel_id=1, source_target_pairs={{8,16},{10,18},{12,20},{14,22},{16,8},{18,10},{20,12},{22,14},{9,1... | collective-permute-start | bytes 1081352 | tf_op jit(solution)/shard_map/ppermute | solution.py:67
  813.1 67.7 %collective-permute-start.60 = (bf16[384,2816]{1,0:T(8,128)(2,1)S(1)}, bf16[384,2816]{1,0:T(8,128)(2,1)S(1)}, u32[]{:S(2)}, u32[]{:S(2)}) collective-permute-start(bf16[384,2816]{1,0:T(8,128)(2,1)S(1)} %fusion.9), channel_id=1, source_target_pairs={{0,8},{2,10},{4,12},{6,14},{24,16},{26,18},{28,20},{30,22},{1,9},{... | collective-permute-start | bytes 6488072 | tf_op jit(solution)/shard_map/ppermute | solution.py:67
  817.8 20.7 %collective-permute-start.56 = (bf16[128,1408]{1,0:T(8,128)(2,1)S(1)}, bf16[128,1408]{1,0:T(8,128)(2,1)S(1)}, u32[]{:S(2)}, u32[]{:S(2)}) collective-permute-start(bf16[128,1408]{1,0:T(8,128)(2,1)S(1)} %get-tuple-element.76), channel_id=1, source_target_pairs={{8,24},{10,26},{12,28},{14,30},{16,0},{18,2},{20,4},{22,6},{9,25},... | collective-permute-start | bytes 1081352 | tf_op jit(solution)/shard_map/ppermute | solution.py:67
  819.1 22.5 %collective-permute-start.51 = (bf16[128,1408]{1,0:T(8,128)(2,1)S(1)}, bf16[128,1408]{1,0:T(8,128)(2,1)S(1)}, u32[]{:S(2)}, u32[]{:S(2)}) collective-permute-start(bf16[128,1408]{1,0:T(8,128)(2,1)S(1)} %get-tuple-element.75), channel_id=1, source_target_pairs={{8,16},{10,18},{12,20},{14,22},{16,8},{18,10},{20,12},{22,14},{9,1... | collective-permute-start | bytes 1081352 | tf_op jit(solution)/shard_map/ppermute | solution.py:67
  836.3 14.2 %collective-permute-start.50 = (bf16[128,1408]{1,0:T(8,128)(2,1)S(1)}, bf16[128,1408]{1,0:T(8,128)(2,1)S(1)}, u32[]{:S(2)}, u32[]{:S(2)}) collective-permute-start(bf16[128,1408]{1,0:T(8,128)(2,1)S(1)} %get-tuple-element.74), channel_id=1, source_target_pairs={{8,24},{10,26},{12,28},{14,30},{16,0},{18,2},{20,4},{22,6},{9,25},... | collective-permute-start | bytes 1081352 | tf_op jit(solution)/shard_map/ppermute | solution.py:67
  837.6 13.5 %collective-permute-start.45 = (bf16[128,1408]{1,0:T(8,128)(2,1)S(1)}, bf16[128,1408]{1,0:T(8,128)(2,1)S(1)}, u32[]{:S(2)}, u32[]{:S(2)}) collective-permute-start(bf16[128,1408]{1,0:T(8,128)(2,1)S(1)} %get-tuple-element.73), channel_id=1, source_target_pairs={{8,16},{10,18},{12,20},{14,22},{16,8},{18,10},{20,12},{22,14},{9,1... | collective-permute-start | bytes 1081352 | tf_op jit(solution)/shard_map/ppermute | solution.py:67
  838.5 27.3 %collective-permute-start.44 = (bf16[128,1408]{1,0:T(8,128)(2,1)S(1)}, bf16[128,1408]{1,0:T(8,128)(2,1)S(1)}, u32[]{:S(2)}, u32[]{:S(2)}) collective-permute-start(bf16[128,1408]{1,0:T(8,128)(2,1)S(1)} %get-tuple-element.72), channel_id=1, source_target_pairs={{8,24},{10,26},{12,28},{14,30},{16,0},{18,2},{20,4},{22,6},{9,25},... | collective-permute-start | bytes 1081352 | tf_op jit(solution)/shard_map/ppermute | solution.py:67
  841.6 25.8 %collective-permute-start.37 = (bf16[128,1408]{1,0:T(8,128)(2,1)S(1)}, bf16[128,1408]{1,0:T(8,128)(2,1)S(1)}, u32[]{:S(2)}, u32[]{:S(2)}) collective-permute-start(bf16[128,1408]{1,0:T(8,128)(2,1)S(1)} %copy-done.53), channel_id=1, source_target_pairs={{8,0},{10,2},{12,4},{14,6},{16,24},{18,26},{20,28},{22,30},{9,1},{... | collective-permute-start | bytes 1081352 | tf_op jit(solution)/shard_map/ppermute | solution.py:67
  850.4 17.0 %collective-permute-start.39 = (bf16[128,1408]{1,0:T(8,128)(2,1)S(1)}, bf16[128,1408]{1,0:T(8,128)(2,1)S(1)}, u32[]{:S(2)}, u32[]{:S(2)}) collective-permute-start(bf16[128,1408]{1,0:T(8,128)(2,1)S(1)} %get-tuple-element.71), channel_id=1, source_target_pairs={{8,16},{10,18},{12,20},{14,22},{16,8},{18,10},{20,12},{22,14},{9,1... | collective-permute-start | bytes 1081352 | tf_op jit(solution)/shard_map/ppermute | solution.py:67
  851.1 25.7 %collective-permute-start.38 = (bf16[128,1408]{1,0:T(8,128)(2,1)S(1)}, bf16[128,1408]{1,0:T(8,128)(2,1)S(1)}, u32[]{:S(2)}, u32[]{:S(2)}) collective-permute-start(bf16[128,1408]{1,0:T(8,128)(2,1)S(1)} %get-tuple-element.70), channel_id=1, source_target_pairs={{8,24},{10,26},{12,28},{14,30},{16,0},{18,2},{20,4},{22,6},{9,25},... | collective-permute-start | bytes 1081352 | tf_op jit(solution)/shard_map/ppermute | solution.py:67
  878.6 15.3 %collective-permute-start.61 = (bf16[128,2816]{1,0:T(8,128)(2,1)S(1)}, bf16[128,2816]{1,0:T(8,128)(2,1)S(1)}, u32[]{:S(2)}, u32[]{:S(2)}) collective-permute-start(bf16[128,2816]{1,0:T(8,128)(2,1)S(1)} %slice.876), channel_id=1, source_target_pairs={{8,0},{10,2},{12,4},{14,6},{16,24},{18,26},{20,28},{22,30},{9,1},{... | collective-permute-start | bytes 2162696 | tf_op jit(solution)/shard_map/ppermute | solution.py:67
  881.2 12.8 %collective-permute-start.63 = (bf16[128,2816]{1,0:T(8,128)(2,1)S(1)}, bf16[128,2816]{1,0:T(8,128)(2,1)S(1)}, u32[]{:S(2)}, u32[]{:S(2)}) collective-permute-start(bf16[128,2816]{1,0:T(8,128)(2,1)S(1)} %get-tuple-element.69), channel_id=1, source_target_pairs={{8,16},{10,18},{12,20},{14,22},{16,8},{18,10},{20,12},{22,14},{9,1... | collective-permute-start | bytes 2162696 | tf_op jit(solution)/shard_map/ppermute | solution.py:67
  881.9 34.9 %collective-permute-start.62 = (bf16[128,2816]{1,0:T(8,128)(2,1)S(1)}, bf16[128,2816]{1,0:T(8,128)(2,1)S(1)}, u32[]{:S(2)}, u32[]{:S(2)}) collective-permute-start(bf16[128,2816]{1,0:T(8,128)(2,1)S(1)} %get-tuple-element.68), channel_id=1, source_target_pairs={{8,24},{10,26},{12,28},{14,30},{16,0},{18,2},{20,4},{22,6},{9,25},... | collective-permute-start | bytes 2162696 | tf_op jit(solution)/shard_map/ppermute | solution.py:67
  (95 other events, 1202.8 us)
Sparse Core Ops, SparseCore 0:
  12.7 94.1 all-gather.7
  109.1 118.6 all-gather.5
  229.9 96.8 all-gather.9

commit v3 on v2

--- a/solution.py
+++ b/solution.py
@@ -273,8 +273,8 @@
         [qkv_weight[0, :, 0], qkv_weight[0, :, 1], qkv_weight[0, :, 2], out_weight[0].T, small], axis=0
     )
     packs = lax.all_gather(pack, "fsdp", axis=0)
-    gate_up_all = lax.all_gather(jnp.swapaxes(gate_up_weight[0], 0, 1), "fsdp", axis=1, tiled=True)
-    w_down = lax.all_gather(down_weight[0], "fsdp", axis=1, tiled=True)
+    mlp_pack = jnp.stack([gate_up_weight[0, :, 0], gate_up_weight[0, :, 1], down_weight[0].T])
+    mlp_all = lax.all_gather(mlp_pack, "fsdp", axis=1, tiled=True)
 
     w_q, w_k, w_v, w_out_t = (
         packs[:, i * block : (i + 1) * block].reshape(width, wide) for i in range(4)
@@ -286,8 +286,7 @@
     bias = jnp.transpose(bias, (1, 2, 0, 3)).reshape(3, heads * HEAD).astype(F32)
     gains = gains.astype(F32)
     shifts = shifts.astype(F32)
-    w_gate = gate_up_all[0]
-    w_up = gate_up_all[1]
+    w_gate, w_up, w_down_t = mlp_all[0], mlp_all[1], mlp_all[2]
 
     position = (jnp.arange(length, dtype=jnp.int32) + turn * mine) % length
     cosine, sine = rope_tables(position)
@@ -323,7 +322,7 @@
     down_grad = scatter_product(grid, down_cot_t, hidden, relay=True)
 
     grad_three = cotangent.astype(F32)
-    grad_hidden = times_transposed(down_cot, w_down)
+    grad_hidden = times(down_cot, w_down_t)
     grad_gate = (grad_hidden * upper * sigma * (1.0 + gate * (1.0 - sigma))).astype(BF16)
     grad_up = (grad_hidden * gate * sigma).astype(BF16)
     mlp_in_t = turned(mlp_in, order)
@@ -343,7 +342,7 @@
     grad_two = grad_three + grad_norm_two
     attn_cot = pair(grad_two.astype(BF16))
     attn_cot, hidden_late = lax.optimization_barrier((attn_cot, hidden))
-    resid_three = resid_two + collect(times(hidden_late, w_down))
+    resid_three = resid_two + collect(times_transposed(hidden_late, w_down_t))
     block_output = resid_three.astype(BF16)
     grad_mixed = times(attn_cot, w_out_t).astype(BF16).reshape(mixed.shape)
     out_grad = scatter_product(grid, turned(attn_cot, order), mixed_flat)
@@ -359,7 +358,9 @@
     q_grad = scatter_product(grid, attn_in_t, grad_proj[0])
     k_grad = scatter_product(grid, attn_in_t, grad_proj[1])
     grad_attn_in = collect(
-        times_transposed(grad_proj[0], w_q) + times_transposed(grad_proj[1], w_k) + times_transposed(grad_proj[2], w_v)
+        times_transposed(grad_proj[0], w_q)
+        + times_transposed(grad_proj[1], w_k)
+        + times_transposed(grad_proj[2], w_v),
     )
     _, normed_one, inv_one = norm_forward(resid, gains[0], shifts[0])
     grad_norm_one, gain_one, shift_one = norm_backward(grad_attn_in, normed_one, inv_one, gains[0])

time: 933 us -> 910 us (0.975)
  waiting for transfers between devices: 561 us -> 530 us
    all_gather x2 -> x1, waiting for transfers between devices: 126 us -> 107 us  [shards(): mlp_all = lax.all_gather(mlp_pack, 'fsdp', axis=1, tiled=True)]
    unnamed x198 -> x199, local copies, waits for them, and re-layouts: 27.6 us -> 31.1 us
  transfers between devices with their start and end apart: 67 -> 66, of which waited for: 35 -> 35; matrix products, arithmetic and copies ran while one was open for 22% -> 22% of each run, Pallas kernels for 2% -> 2%
where the time goes in v3:
time: 910 us; the launch traced here: 903 us
  waiting for transfers between devices  530 us (58%)
  matrix products  163 us (18%)
  starting transfers between devices  82 us (9%)
  local copies, waits for them, and re-layouts  61.4 us (7%)
  other arithmetic  34 us (4%)
  Pallas kernels  16.5 us (2%)
  between operations  16.3 us (2%)
    ppermute x20, waiting for transfers between devices, shift(): return lax.ppermute(rows, 'fsdp', self.moves(**by))  166 us
    ppermute x35, waiting for transfers between devices, cross(): return lax.ppermute(rows, 'fsdp', moves)  150 us
    dot_general x51, matrix products, times(): lax.dot_general(left, right, (((1,), (0,)), ((), ())), preferred_element_...  122 us
    all_gather x1, waiting for transfers between devices, shards(): mlp_all = lax.all_gather(mlp_pack, 'fsdp', axis=1, tiled=True)  107 us
    all_gather x1, waiting for transfers between devices, shards(): packs = lax.all_gather(pack, 'fsdp', axis=0)  65.5 us
    ppermute x35, starting transfers between devices, cross(): return lax.ppermute(rows, 'fsdp', moves)  57.7 us
    ppermute x9, waiting for transfers between devices, other(): return lax.ppermute(rows, 'tp', [(0, 1), (1, 0)])  41.3 us
    unnamed x199, local copies, waits for them, and re-layouts  31.1 us
  transfers between devices with their start and end apart: 66, of which 35 were waited for; matrix products, arithmetic and copies ran while one was open for 22% of the time, Pallas kernels for 2%

profile of v3, /device:TPU:0, one launch (start us, length us, event | category | flops | bytes accessed | tf_op | source)
XLA Modules:
  0.0 902.8 jit_solution(15462254329438001472)
XLA Ops:
  12.8 2.9 fusion.231
  15.7 3.8 copy.96
  21.4 2.9 pad_maximum_fusion
  25.3 2.8 collective-permute-start
  30.9 10.0 %collective-permute-done = bf16[128,2048]{1,0:T(8,128)(2,1)S(1)} collective-permute-done((bf16[128,2048]{1,0:T(8,128)(2,1)S(1)}, bf16[128,2048]{1,0:T(8,128)(2,1)S(1)}, u32[]{:S(2)}, u32[]{:S(2)}) %collective-permute-start) | collective-permute-done | bytes 524320 | tf_op jit(solution)/shard_map/ppermute | solution.py:170
  41.6 65.5 %all-gather.6.cloned.1.call-done = bf16[8448,1024]{1,0:T(8,128)(2,1)} async-done(((bf16[528,1024]{1,0:T(8,128)(2,1)}), bf16[8448,1024]{1,0:T(8,128)(2,1)}) %all-gather.6.cloned.1.call-update) | async-done | bytes 17301520 | tf_op jit(solution)/shard_map/all_gather | solution.py:275
  110.0 11.7 %fusion.230 = (bf16[16,128,1024]{2,1,0:T(8,128)(2,1)}, bf16[16,128,1024]{2,1,0:T(8,128)(2,1)}, bf16[16,128,1024]{2,1,0:T(8,128)(2,1)}, bf16[16,128,1024]{2,1,0:T(8,128)(2,1)S(1)}) fusion(bf16[16,528,1024]{2,1,0:T(8,128)(2,1)} %bitcast.216), kind=kLoop, calls=%fused_computation.397 | loop fusion | bytes 33554432 | tf_op jit(solution)/shard_map/slice | solution.py:280
  126.3 4.4 convolution_add_fusion.16
  132.6 4.4 convolution_add_fusion.17
  150.5 10.6 %collective-permute-done.1 = bf16[128,2048]{1,0:T(8,128)(2,1)S(1)} collective-permute-done((bf16[128,2048]{1,0:T(8,128)(2,1)S(1)}, bf16[128,2048]{1,0:T(8,128)(2,1)S(1)}, u32[]{:S(2)}, u32[]{:S(2)}) %collective-permute-start.1) | collective-permute-done | bytes 524320 | tf_op jit(solution)/shard_map/ppermute | solution.py:170
  167.6 4.2 shard_map.172
  171.7 4.2 shard_map.169
  179.1 4.1 shard_map.171
  183.2 106.8 %all-gather.4.cloned.1.call-done = bf16[3,2048,2816]{1,2,0:T(8,128)(2,1)} async-done(((bf16[3,128,2816]{1,2,0:T(8,128)(2,1)}), bf16[3,2048,2816]{1,2,0:T(8,128)(2,1)}) %all-gather.4.cloned.1.call-update) | async-done | bytes 34603024 | tf_op jit(solution)/shard_map/all_gather | solution.py:277
  290.0 6.8 fusion.3
  296.8 9.7 %multiply_convert_fusion.3 = (bf16[256,2816]{1,0:T(8,128)(2,1)S(1)}, f32[256,2816]{1,0:T(8,128)}) fusion(f32[256,2816]{1,0:T(8,128)S(1)} %fusion.3, bf16[3,2048,2816]{1,2,0:T(8,128)(2,1)} %all-gather.4.cloned.1.call-done, bf16[128,2048]{1,0:T(8,128)(2,1)} %collective-permute-done.3, bf16[128,2048]{1,0:T(8,128)(2,1)} %add_convert_fusion.7), kind=kOutput, calls=%fused_computation.51 | convolution fusion | flops 2959212544 | bytes 19791872 | tf_op jit(solution)/shard_map/dot_general | solution.py:22
  306.4 8.1 multiply_convert_fusion.1
  314.5 7.0 fusion.2
  321.6 6.5 fusion.28
  329.7 2.6 convolution_convert_fusion.1
  332.3 2.5 convolution_convert_fusion.2
  334.8 2.6 convolution_convert_fusion.3
  337.4 4.9 collective-permute-done.4
  343.4 2.6 fusion.228
  347.4 2.7 convolution_convert_fusion.4
  350.7 4.1 convolution_convert_fusion
  354.8 4.4 collective-permute-done.5
  361.9 3.9 multiply_convert_fusion
  371.5 4.0 shard_map.170
  375.5 3.6 fusion.238
  390.1 9.3 %fusion = f32[256,2048]{1,0:T(8,128)} fusion(bf16[256,2816]{1,0:T(8,128)(2,1)} %copy-done.9, bf16[3,2048,2816]{1,2,0:T(8,128)(2,1)} %all-gather.4.cloned.1.call-done), kind=kOutput, calls=%fused_computation.4 | convolution fusion | flops 2952790016 | bytes 15073280 | tf_op jit(solution)/shard_map/dot_general | solution.py:26
  422.0 8.0 collective-permute-done.6
  430.6 3.0 collective-permute-done.13
  458.1 16.2 %collective-permute-done.25 = bf16[512,1024]{1,0:T(8,128)(2,1)S(1)} collective-permute-done((bf16[512,1024]{1,0:T(8,128)(2,1)S(1)}, bf16[512,1024]{1,0:T(8,128)(2,1)S(1)}, u32[]{:S(2)}, u32[]{:S(2)}) %collective-permute-start.25) | collective-permute-done | bytes 1048608 | tf_op jit(solution)/shard_map/ppermute | solution.py:53
  480.6 77.9 %collective-permute-done.20 = bf16[512,1024]{1,0:T(8,128)(2,1)S(1)} collective-permute-done((bf16[512,1024]{1,0:T(8,128)(2,1)S(1)}, bf16[512,1024]{1,0:T(8,128)(2,1)S(1)}, u32[]{:S(2)}, u32[]{:S(2)}) %collective-permute-start.20) | collective-permute-done | bytes 1048608 | tf_op jit(solution)/shard_map/ppermute | solution.py:53
  565.6 15.4 %collective-permute-done.15 = bf16[512,1024]{1,0:T(8,128)(2,1)S(1)} collective-permute-done((bf16[512,1024]{1,0:T(8,128)(2,1)S(1)}, bf16[512,1024]{1,0:T(8,128)(2,1)S(1)}, u32[]{:S(2)}, u32[]{:S(2)}) %collective-permute-start.15) | collective-permute-done | bytes 1048608 | tf_op jit(solution)/shard_map/ppermute | solution.py:53
  585.2 18.3 %collective-permute-done.30 = bf16[512,1024]{1,0:T(8,128)(2,1)S(1)} collective-permute-done((bf16[512,1024]{1,0:T(8,128)(2,1)S(1)}, bf16[512,1024]{1,0:T(8,128)(2,1)S(1)}, u32[]{:S(2)}, u32[]{:S(2)}) %collective-permute-start.30) | collective-permute-done | bytes 1048608 | tf_op jit(solution)/shard_map/ppermute | solution.py:53
  609.5 2.8 fusion.26
  614.1 2.5 collective-permute-start.33
  619.7 3.7 add_convert_fusion
  623.4 11.0 %collective-permute-done.41 = bf16[512,1408]{1,0:T(8,128)(2,1)S(1)} collective-permute-done((bf16[512,1408]{1,0:T(8,128)(2,1)S(1)}, bf16[512,1408]{1,0:T(8,128)(2,1)S(1)}, u32[]{:S(2)}, u32[]{:S(2)}) %collective-permute-start.41) | collective-permute-done | bytes 1441824 | tf_op jit(solution)/shard_map/ppermute | solution.py:53
  638.2 27.1 %collective-permute-done.35 = bf16[512,1408]{1,0:T(8,128)(2,1)S(1)} collective-permute-done((bf16[512,1408]{1,0:T(8,128)(2,1)S(1)}, bf16[512,1408]{1,0:T(8,128)(2,1)S(1)}, u32[]{:S(2)}, u32[]{:S(2)}) %collective-permute-start.35) | collective-permute-done | bytes 1441824 | tf_op jit(solution)/shard_map/ppermute | solution.py:53
  670.6 3.3 collective-permute-start.23
  674.6 4.4 collective-permute-start.54
  682.2 3.4 collective-permute-done.27
  687.5 3.7 collective-permute-done.23
  691.2 3.8 collective-permute-start.18
  696.6 22.9 %collective-permute-done.22 = bf16[128,1024]{1,0:T(8,128)(2,1)S(1)} collective-permute-done((bf16[128,1024]{1,0:T(8,128)(2,1)}, bf16[128,1024]{1,0:T(8,128)(2,1)S(1)}, u32[]{:S(2)}, u32[]{:S(2)}) %collective-permute-start.22) | collective-permute-done | bytes 262176 | tf_op jit(solution)/shard_map/ppermute | solution.py:67
  719.4 3.3 collective-permute-start.17
  727.4 3.8 collective-permute-done.18
  734.2 3.5 collective-permute-done.17
  739.3 2.6 collective-permute-done.16
  741.9 4.3 collective-permute-start.36
  751.7 13.4 %collective-permute-done.48 = bf16[384,1408]{1,0:T(8,128)(2,1)S(1)} collective-permute-done((bf16[384,1408]{1,0:T(8,128)(2,1)}, bf16[384,1408]{1,0:T(8,128)(2,1)S(1)}, u32[]{:S(2)}, u32[]{:S(2)}) %collective-permute-start.48) | collective-permute-done | bytes 1081376 | tf_op jit(solution)/shard_map/ppermute | solution.py:67
  767.9 3.2 fusion.7
  771.8 16.3 %collective-permute-done.42 = bf16[384,1408]{1,0:T(8,128)(2,1)S(1)} collective-permute-done((bf16[384,1408]{1,0:T(8,128)(2,1)S(1)}, bf16[384,1408]{1,0:T(8,128)(2,1)S(1)}, u32[]{:S(2)}, u32[]{:S(2)}) %collective-permute-start.42) | collective-permute-done | bytes 1081376 | tf_op jit(solution)/shard_map/ppermute | solution.py:67
  788.2 4.5 collective-permute-start.60
  794.9 16.5 %collective-permute-done.36 = bf16[384,1408]{1,0:T(8,128)(2,1)S(1)} collective-permute-done((bf16[384,1408]{1,0:T(8,128)(2,1)S(1)}, bf16[384,1408]{1,0:T(8,128)(2,1)S(1)}, u32[]{:S(2)}, u32[]{:S(2)}) %collective-permute-start.36) | collective-permute-done | bytes 1081376 | tf_op jit(solution)/shard_map/ppermute | solution.py:67
  818.1 7.4 collective-permute-done.50
  829.1 11.8 %collective-permute-done.44 = bf16[128,1408]{1,0:T(8,128)(2,1)S(1)} collective-permute-done((bf16[128,1408]{1,0:T(8,128)(2,1)S(1)}, bf16[128,1408]{1,0:T(8,128)(2,1)S(1)}, u32[]{:S(2)}, u32[]{:S(2)}) %collective-permute-start.44) | collective-permute-done | bytes 360480 | tf_op jit(solution)/shard_map/ppermute | solution.py:67
  842.5 9.4 %collective-permute-done.38 = bf16[128,1408]{1,0:T(8,128)(2,1)S(1)} collective-permute-done((bf16[128,1408]{1,0:T(8,128)(2,1)S(1)}, bf16[128,1408]{1,0:T(8,128)(2,1)S(1)}, u32[]{:S(2)}, u32[]{:S(2)}) %collective-permute-start.38) | collective-permute-done | bytes 360480 | tf_op jit(solution)/shard_map/ppermute | solution.py:67
  858.5 3.8 copy.88
  862.3 6.6 collective-permute-done.61
  869.0 22.9 %collective-permute-done.62 = bf16[128,2816]{1,0:T(8,128)(2,1)S(1)} collective-permute-done((bf16[128,2816]{1,0:T(8,128)(2,1)S(1)}, bf16[128,2816]{1,0:T(8,128)(2,1)S(1)}, u32[]{:S(2)}, u32[]{:S(2)}) %collective-permute-start.62) | collective-permute-done | bytes 720928 | tf_op jit(solution)/shard_map/ppermute | solution.py:67
  (453 shorter events, 202.5 us)
Async XLA Ops:
  7.2 99.9 %all-gather.6.cloned.1.call-start = ((), (), s32[]{:S(2)}) async-start(), calls=%async_computation.1 | async-start | bytes 18382848 | tf_op jit(solution)/shard_map/all_gather | solution.py:275
  12.7 277.2 %all-gather.4.cloned.1.call-start = ((), (), s32[]{:S(2)}) async-start(), calls=%async_computation | async-start | bytes 36765696 | tf_op jit(solution)/shard_map/all_gather | solution.py:277
  25.3 15.6 %collective-permute-start = (bf16[128,2048]{1,0:T(8,128)(2,1)S(1)}, bf16[128,2048]{1,0:T(8,128)(2,1)S(1)}, u32[]{:S(2)}, u32[]{:S(2)}) collective-permute-start(bf16[128,2048]{1,0:T(8,128)(2,1)S(1)} %copy-done), channel_id=1, source_target_pairs={{0,1},{1,0},{2,3},{3,2},{4,5},{5,4},{6,7},{7,6},{8,9},{9,8},{10,11... | collective-permute-start | bytes 1572872 | tf_op jit(solution)/shard_map/ppermute | solution.py:170
  28.1 137.4 %collective-permute-start.2 = (bf16[128,2048]{1,0:T(8,128)(2,1)}, bf16[128,2048]{1,0:T(8,128)(2,1)}, u32[]{:S(2)}, u32[]{:S(2)}) collective-permute-start(bf16[128,2048]{1,0:T(8,128)(2,1)} %param.12), channel_id=1, source_target_pairs={{0,1},{1,0},{2,3},{3,2},{4,5},{5,4},{6,7},{7,6},{8,9},{9,8},{10,11... | collective-permute-start | bytes 1572872 | tf_op jit(solution)/shard_map/ppermute | solution.py:170
  147.3 13.9 %collective-permute-start.1 = (bf16[128,2048]{1,0:T(8,128)(2,1)S(1)}, bf16[128,2048]{1,0:T(8,128)(2,1)S(1)}, u32[]{:S(2)}, u32[]{:S(2)}) collective-permute-start(bf16[128,2048]{1,0:T(8,128)(2,1)S(1)} %slice.1217), channel_id=1, source_target_pairs={{0,1},{1,0},{2,3},{3,2},{4,5},{5,4},{6,7},{7,6},{8,9},{9,8},{10,11... | collective-permute-start | bytes 1572872 | tf_op jit(solution)/shard_map/ppermute | solution.py:170
  163.4 13.4 %collective-permute-start.3 = (bf16[128,2048]{1,0:T(8,128)(2,1)}, bf16[128,2048]{1,0:T(8,128)(2,1)}, u32[]{:S(2)}, u32[]{:S(2)}) collective-permute-start(bf16[128,2048]{1,0:T(8,128)(2,1)} %add_convert_fusion.7), channel_id=1, source_target_pairs={{0,1},{1,0},{2,3},{3,2},{4,5},{5,4},{6,7},{7,6},{8,9},{9,8},{10,11... | collective-permute-start | bytes 1572872 | tf_op jit(solution)/shard_map/ppermute | solution.py:170
  328.2 14.2 %collective-permute-start.4 = (bf16[128,2048]{1,0:T(8,128)(2,1)S(1)}, bf16[128,2048]{1,0:T(8,128)(2,1)S(1)}, u32[]{:S(2)}, u32[]{:S(2)}) collective-permute-start(bf16[128,2048]{1,0:T(8,128)(2,1)S(1)} %slice.1216), channel_id=1, source_target_pairs={{0,1},{1,0},{2,3},{3,2},{4,5},{5,4},{6,7},{7,6},{8,9},{9,8},{10,11... | collective-permute-start | bytes 1572872 | tf_op jit(solution)/shard_map/ppermute | solution.py:170
  345.9 13.2 %collective-permute-start.5 = (bf16[128,2048]{1,0:T(8,128)(2,1)S(1)}, bf16[128,2048]{1,0:T(8,128)(2,1)S(1)}, u32[]{:S(2)}, u32[]{:S(2)}) collective-permute-start(bf16[128,2048]{1,0:T(8,128)(2,1)S(1)} %get-tuple-element.58), channel_id=1, source_target_pairs={{0,1},{1,0},{2,3},{3,2},{4,5},{5,4},{6,7},{7,6},{8,9},{9,8},{10,11... | collective-permute-start | bytes 1572872 | tf_op jit(solution)/shard_map/ppermute | solution.py:170
  350.1 85.8 %collective-permute-start.52 = (bf16[1024,1408]{1,0:T(8,128)(2,1)}, bf16[1024,1408]{1,0:T(8,128)(2,1)}, u32[]{:S(2)}, u32[]{:S(2)}) collective-permute-start(bf16[1024,1408]{1,0:T(8,128)(2,1)} %convolution_convert_fusion.1), channel_id=1, source_target_pairs={{0,2},{2,0},{4,6},{6,4},{8,10},{10,8},{12,14},{14,12},{16,18},{18,... | collective-permute-start | bytes 8650760 | tf_op jit(solution)/shard_map/ppermute | solution.py:53
  350.1 88.4 %collective-permute-start.46 = (bf16[1024,1408]{1,0:T(8,128)(2,1)}, bf16[1024,1408]{1,0:T(8,128)(2,1)}, u32[]{:S(2)}, u32[]{:S(2)}) collective-permute-start(bf16[1024,1408]{1,0:T(8,128)(2,1)} %convolution_convert_fusion.2), channel_id=1, source_target_pairs={{0,2},{2,0},{4,6},{6,4},{8,10},{10,8},{12,14},{14,12},{16,18},{18,... | collective-permute-start | bytes 8650760 | tf_op jit(solution)/shard_map/ppermute | solution.py:53
  350.6 88.4 %collective-permute-start.40 = (bf16[1024,1408]{1,0:T(8,128)(2,1)}, bf16[1024,1408]{1,0:T(8,128)(2,1)}, u32[]{:S(2)}, u32[]{:S(2)}) collective-permute-start(bf16[1024,1408]{1,0:T(8,128)(2,1)} %convolution_convert_fusion.3), channel_id=1, source_target_pairs={{0,2},{2,0},{4,6},{6,4},{8,10},{10,8},{12,14},{14,12},{16,18},{18,... | collective-permute-start | bytes 8650760 | tf_op jit(solution)/shard_map/ppermute | solution.py:53
  388.2 15.4 %collective-permute-start.7 = (bf16[128,2048]{1,0:T(8,128)(2,1)}, bf16[128,2048]{1,0:T(8,128)(2,1)}, u32[]{:S(2)}, u32[]{:S(2)}) collective-permute-start(bf16[128,2048]{1,0:T(8,128)(2,1)} %slice.1214), channel_id=1, source_target_pairs={{0,1},{1,0},{2,3},{3,2},{4,5},{5,4},{6,7},{7,6},{8,9},{9,8},{10,11... | collective-permute-start | bytes 1572872 | tf_op jit(solution)/shard_map/ppermute | solution.py:170
  408.5 3.8 collective-permute-start.9
  412.3 5.5 collective-permute-start.12
  412.9 5.5 collective-permute-start.11
  417.8 12.2 %collective-permute-start.6 = (bf16[128,2048]{1,0:T(8,128)(2,1)S(1)}, bf16[128,2048]{1,0:T(8,128)(2,1)S(1)}, u32[]{:S(2)}, u32[]{:S(2)}) collective-permute-start(bf16[128,2048]{1,0:T(8,128)(2,1)S(1)} %slice.1215), channel_id=1, source_target_pairs={{0,1},{1,0},{2,3},{3,2},{4,5},{5,4},{6,7},{7,6},{8,9},{9,8},{10,11... | collective-permute-start | bytes 1572872 | tf_op jit(solution)/shard_map/ppermute | solution.py:170
  418.4 3.6 collective-permute-start.10
  422.0 19.9 %collective-permute-start.24 = (bf16[1024,1024]{1,0:T(8,128)(2,1)}, bf16[1024,1024]{1,0:T(8,128)(2,1)}, u32[]{:S(2)}, u32[]{:S(2)}) collective-permute-start(bf16[1024,1024]{1,0:T(8,128)(2,1)} %convolution_convert_fusion.6), channel_id=1, source_target_pairs={{0,2},{2,0},{4,6},{6,4},{8,10},{10,8},{12,14},{14,12},{16,18},{18,... | collective-permute-start | bytes 6291464 | tf_op jit(solution)/shard_map/ppermute | solution.py:53
  433.6 14.6 %collective-permute-start.34 = (bf16[1024,1408]{1,0:T(8,128)(2,1)}, bf16[1024,1408]{1,0:T(8,128)(2,1)}, u32[]{:S(2)}, u32[]{:S(2)}) collective-permute-start(bf16[1024,1408]{1,0:T(8,128)(2,1)} %convolution_convert_fusion.4), channel_id=1, source_target_pairs={{0,2},{2,0},{4,6},{6,4},{8,10},{10,8},{12,14},{14,12},{16,18},{18,... | collective-permute-start | bytes 8650760 | tf_op jit(solution)/shard_map/ppermute | solution.py:53
  436.0 15.3 %collective-permute-start.19 = (bf16[1024,1024]{1,0:T(8,128)(2,1)}, bf16[1024,1024]{1,0:T(8,128)(2,1)}, u32[]{:S(2)}, u32[]{:S(2)}) collective-permute-start(bf16[1024,1024]{1,0:T(8,128)(2,1)} %convolution_convert_fusion.7), channel_id=1, source_target_pairs={{0,2},{2,0},{4,6},{6,4},{8,10},{10,8},{12,14},{14,12},{16,18},{18,... | collective-permute-start | bytes 6291464 | tf_op jit(solution)/shard_map/ppermute | solution.py:53
  438.5 15.5 %collective-permute-start.14 = (bf16[1024,1024]{1,0:T(8,128)(2,1)}, bf16[1024,1024]{1,0:T(8,128)(2,1)S(1)}, u32[]{:S(2)}, u32[]{:S(2)}) collective-permute-start(bf16[1024,1024]{1,0:T(8,128)(2,1)} %convolution_convert_fusion.8), channel_id=1, source_target_pairs={{0,2},{2,0},{4,6},{6,4},{8,10},{10,8},{12,14},{14,12},{16,18},{18,... | collective-permute-start | bytes 6291464 | tf_op jit(solution)/shard_map/ppermute | solution.py:53
  439.1 16.6 %collective-permute-start.29 = (bf16[1024,1024]{1,0:T(8,128)(2,1)}, bf16[1024,1024]{1,0:T(8,128)(2,1)S(1)}, u32[]{:S(2)}, u32[]{:S(2)}) collective-permute-start(bf16[1024,1024]{1,0:T(8,128)(2,1)} %convolution_convert_fusion.5), channel_id=1, source_target_pairs={{0,2},{2,0},{4,6},{6,4},{8,10},{10,8},{12,14},{14,12},{16,18},{18,... | collective-permute-start | bytes 6291464 | tf_op jit(solution)/shard_map/ppermute | solution.py:53
  441.8 177.4 %collective-permute-start.58 = (bf16[1024,2816]{1,0:T(8,128)(2,1)}, bf16[1024,2816]{1,0:T(8,128)(2,1)S(1)}, u32[]{:S(2)}, u32[]{:S(2)}) collective-permute-start(bf16[1024,2816]{1,0:T(8,128)(2,1)} %convolution_convert_fusion), channel_id=1, source_target_pairs={{0,2},{2,0},{4,6},{6,4},{8,10},{10,8},{12,14},{14,12},{16,18},{18,... | collective-permute-start | bytes 17301512 | tf_op jit(solution)/shard_map/ppermute | solution.py:53
  448.1 26.1 %collective-permute-start.25 = (bf16[512,1024]{1,0:T(8,128)(2,1)S(1)}, bf16[512,1024]{1,0:T(8,128)(2,1)S(1)}, u32[]{:S(2)}, u32[]{:S(2)}) collective-permute-start(bf16[512,1024]{1,0:T(8,128)(2,1)S(1)} %add_convert_fusion.2), channel_id=1, source_target_pairs={{0,4},{2,6},{4,0},{6,2},{8,12},{10,14},{12,8},{14,10},{16,20},{18,... | collective-permute-start | bytes 3145736 | tf_op jit(solution)/shard_map/ppermute | solution.py:53
  451.3 156.8 %collective-permute-start.53 = (bf16[512,1408]{1,0:T(8,128)(2,1)S(1)}, bf16[512,1408]{1,0:T(8,128)(2,1)S(1)}, u32[]{:S(2)}, u32[]{:S(2)}) collective-permute-start(bf16[512,1408]{1,0:T(8,128)(2,1)S(1)} %fusion.22), channel_id=1, source_target_pairs={{0,4},{2,6},{4,0},{6,2},{8,12},{10,14},{12,8},{14,10},{16,20},{18,... | collective-permute-start | bytes 4325384 | tf_op jit(solution)/shard_map/ppermute | solution.py:53
  454.0 160.1 %collective-permute-start.47 = (bf16[512,1408]{1,0:T(8,128)(2,1)S(1)}, bf16[512,1408]{1,0:T(8,128)(2,1)S(1)}, u32[]{:S(2)}, u32[]{:S(2)}) collective-permute-start(bf16[512,1408]{1,0:T(8,128)(2,1)S(1)} %fusion.21), channel_id=1, source_target_pairs={{0,4},{2,6},{4,0},{6,2},{8,12},{10,14},{12,8},{14,10},{16,20},{18,... | collective-permute-start | bytes 4325384 | tf_op jit(solution)/shard_map/ppermute | solution.py:53
  455.7 102.9 %collective-permute-start.20 = (bf16[512,1024]{1,0:T(8,128)(2,1)S(1)}, bf16[512,1024]{1,0:T(8,128)(2,1)S(1)}, u32[]{:S(2)}, u32[]{:S(2)}) collective-permute-start(bf16[512,1024]{1,0:T(8,128)(2,1)S(1)} %add_convert_fusion.3), channel_id=1, source_target_pairs={{0,4},{2,6},{4,0},{6,2},{8,12},{10,14},{12,8},{14,10},{16,20},{18,... | collective-permute-start | bytes 3145736 | tf_op jit(solution)/shard_map/ppermute | solution.py:53
  474.2 106.7 %collective-permute-start.15 = (bf16[512,1024]{1,0:T(8,128)(2,1)S(1)}, bf16[512,1024]{1,0:T(8,128)(2,1)S(1)}, u32[]{:S(2)}, u32[]{:S(2)}) collective-permute-start(bf16[512,1024]{1,0:T(8,128)(2,1)S(1)} %add_convert_fusion.4), channel_id=1, source_target_pairs={{0,4},{2,6},{4,0},{6,2},{8,12},{10,14},{12,8},{14,10},{16,20},{18,... | collective-permute-start | bytes 3145736 | tf_op jit(solution)/shard_map/ppermute | solution.py:53
  558.5 44.9 %collective-permute-start.30 = (bf16[512,1024]{1,0:T(8,128)(2,1)S(1)}, bf16[512,1024]{1,0:T(8,128)(2,1)S(1)}, u32[]{:S(2)}, u32[]{:S(2)}) collective-permute-start(bf16[512,1024]{1,0:T(8,128)(2,1)S(1)} %add_convert_fusion.1), channel_id=1, source_target_pairs={{0,4},{2,6},{4,0},{6,2},{8,12},{10,14},{12,8},{14,10},{16,20},{18,... | collective-permute-start | bytes 3145736 | tf_op jit(solution)/shard_map/ppermute | solution.py:53
  581.0 53.4 %collective-permute-start.41 = (bf16[512,1408]{1,0:T(8,128)(2,1)S(1)}, bf16[512,1408]{1,0:T(8,128)(2,1)S(1)}, u32[]{:S(2)}, u32[]{:S(2)}) collective-permute-start(bf16[512,1408]{1,0:T(8,128)(2,1)S(1)} %fusion.20), channel_id=1, source_target_pairs={{0,4},{2,6},{4,0},{6,2},{8,12},{10,14},{12,8},{14,10},{16,20},{18,... | collective-permute-start | bytes 4325384 | tf_op jit(solution)/shard_map/ppermute | solution.py:53
  603.5 61.8 %collective-permute-start.35 = (bf16[512,1408]{1,0:T(8,128)(2,1)S(1)}, bf16[512,1408]{1,0:T(8,128)(2,1)S(1)}, u32[]{:S(2)}, u32[]{:S(2)}) collective-permute-start(bf16[512,1408]{1,0:T(8,128)(2,1)S(1)} %fusion.19), channel_id=1, source_target_pairs={{0,4},{2,6},{4,0},{6,2},{8,12},{10,14},{12,8},{14,10},{16,20},{18,... | collective-permute-start | bytes 4325384 | tf_op jit(solution)/shard_map/ppermute | solution.py:53
  608.1 61.5 %collective-permute-start.28 = (bf16[128,1024]{1,0:T(8,128)(2,1)S(1)}, bf16[128,1024]{1,0:T(8,128)(2,1)S(1)}, u32[]{:S(2)}, u32[]{:S(2)}) collective-permute-start(bf16[128,1024]{1,0:T(8,128)(2,1)S(1)} %add_convert_fusion.19), channel_id=1, source_target_pairs={{0,24},{2,26},{4,28},{6,30},{8,16},{10,18},{12,20},{14,22},{16,8},... | collective-permute-start | bytes 786440 | tf_op jit(solution)/shard_map/ppermute | solution.py:67
  614.1 55.8 %collective-permute-start.33 = (bf16[128,1024]{1,0:T(8,128)(2,1)S(1)}, bf16[128,1024]{1,0:T(8,128)(2,1)S(1)}, u32[]{:S(2)}, u32[]{:S(2)}) collective-permute-start(bf16[128,1024]{1,0:T(8,128)(2,1)S(1)} %add_convert_fusion.16), channel_id=1, source_target_pairs={{0,24},{2,26},{4,28},{6,30},{8,16},{10,18},{12,20},{14,22},{16,8},... | collective-permute-start | bytes 786440 | tf_op jit(solution)/shard_map/ppermute | solution.py:67
  619.5 51.1 %collective-permute-start.32 = (bf16[128,1024]{1,0:T(8,128)(2,1)S(1)}, bf16[128,1024]{1,0:T(8,128)(2,1)S(1)}, u32[]{:S(2)}, u32[]{:S(2)}) collective-permute-start(bf16[128,1024]{1,0:T(8,128)(2,1)S(1)} %add_convert_fusion.17), channel_id=1, source_target_pairs={{0,16},{2,18},{4,20},{6,22},{8,24},{10,26},{12,28},{14,30},{16,0},... | collective-permute-start | bytes 786440 | tf_op jit(solution)/shard_map/ppermute | solution.py:67
  634.4 132.2 %collective-permute-start.59 = (bf16[512,2816]{1,0:T(8,128)(2,1)}, bf16[512,2816]{1,0:T(8,128)(2,1)}, u32[]{:S(2)}, u32[]{:S(2)}) collective-permute-start(bf16[512,2816]{1,0:T(8,128)(2,1)} %add_convert_fusion), channel_id=1, source_target_pairs={{0,4},{2,6},{4,0},{6,2},{8,12},{10,14},{12,8},{14,10},{16,20},{18,... | collective-permute-start | bytes 8650760 | tf_op jit(solution)/shard_map/ppermute | solution.py:53
  665.3 9.4 %collective-permute-start.31 = (bf16[128,1024]{1,0:T(8,128)(2,1)S(1)}, bf16[128,1024]{1,0:T(8,128)(2,1)S(1)}, u32[]{:S(2)}, u32[]{:S(2)}) collective-permute-start(bf16[128,1024]{1,0:T(8,128)(2,1)S(1)} %add_convert_fusion.18), channel_id=1, source_target_pairs={{0,8},{2,10},{4,12},{6,14},{8,0},{10,2},{12,4},{14,6},{16,24},{18,... | collective-permute-start | bytes 786440 | tf_op jit(solution)/shard_map/ppermute | solution.py:67
  669.6 16.1 %collective-permute-start.27 = (bf16[128,1024]{1,0:T(8,128)(2,1)}, bf16[128,1024]{1,0:T(8,128)(2,1)}, u32[]{:S(2)}, u32[]{:S(2)}) collective-permute-start(bf16[128,1024]{1,0:T(8,128)(2,1)} %add_convert_fusion.20), channel_id=1, source_target_pairs={{0,16},{2,18},{4,20},{6,22},{8,24},{10,26},{12,28},{14,30},{16,0},... | collective-permute-start | bytes 786440 | tf_op jit(solution)/shard_map/ppermute | solution.py:67
  669.8 15.8 %collective-permute-start.26 = (bf16[128,1024]{1,0:T(8,128)(2,1)}, bf16[128,1024]{1,0:T(8,128)(2,1)}, u32[]{:S(2)}, u32[]{:S(2)}) collective-permute-start(bf16[128,1024]{1,0:T(8,128)(2,1)} %add_convert_fusion.21), channel_id=1, source_target_pairs={{0,8},{2,10},{4,12},{6,14},{8,0},{10,2},{12,4},{14,6},{16,24},{18,... | collective-permute-start | bytes 786440 | tf_op jit(solution)/shard_map/ppermute | solution.py:67
  670.6 20.6 %collective-permute-start.23 = (bf16[128,1024]{1,0:T(8,128)(2,1)}, bf16[128,1024]{1,0:T(8,128)(2,1)}, u32[]{:S(2)}, u32[]{:S(2)}) collective-permute-start(bf16[128,1024]{1,0:T(8,128)(2,1)} %add_convert_fusion.22), channel_id=1, source_target_pairs={{0,24},{2,26},{4,28},{6,30},{8,16},{10,18},{12,20},{14,22},{16,8},... | collective-permute-start | bytes 786440 | tf_op jit(solution)/shard_map/ppermute | solution.py:67
  674.6 74.2 %collective-permute-start.54 = (bf16[384,1408]{1,0:T(8,128)(2,1)}, bf16[384,1408]{1,0:T(8,128)(2,1)}, u32[]{:S(2)}, u32[]{:S(2)}) collective-permute-start(bf16[384,1408]{1,0:T(8,128)(2,1)} %fusion.26), channel_id=1, source_target_pairs={{0,8},{2,10},{4,12},{6,14},{24,16},{26,18},{28,20},{30,22},{1,9},{... | collective-permute-start | bytes 3244040 | tf_op jit(solution)/shard_map/ppermute | solution.py:67
  685.6 33.8 %collective-permute-start.22 = (bf16[128,1024]{1,0:T(8,128)(2,1)}, bf16[128,1024]{1,0:T(8,128)(2,1)S(1)}, u32[]{:S(2)}, u32[]{:S(2)}) collective-permute-start(bf16[128,1024]{1,0:T(8,128)(2,1)} %add_convert_fusion.23), channel_id=1, source_target_pairs={{0,16},{2,18},{4,20},{6,22},{8,24},{10,26},{12,28},{14,30},{16,0},... | collective-permute-start | bytes 786440 | tf_op jit(solution)/shard_map/ppermute | solution.py:67
  685.6 39.4 %collective-permute-start.21 = (bf16[128,1024]{1,0:T(8,128)(2,1)}, bf16[128,1024]{1,0:T(8,128)(2,1)S(1)}, u32[]{:S(2)}, u32[]{:S(2)}) collective-permute-start(bf16[128,1024]{1,0:T(8,128)(2,1)} %add_convert_fusion.24), channel_id=1, source_target_pairs={{0,8},{2,10},{4,12},{6,14},{8,0},{10,2},{12,4},{14,6},{16,24},{18,... | collective-permute-start | bytes 786440 | tf_op jit(solution)/shard_map/ppermute | solution.py:67
  691.2 40.1 %collective-permute-start.18 = (bf16[128,1024]{1,0:T(8,128)(2,1)}, bf16[128,1024]{1,0:T(8,128)(2,1)S(1)}, u32[]{:S(2)}, u32[]{:S(2)}) collective-permute-start(bf16[128,1024]{1,0:T(8,128)(2,1)} %add_convert_fusion.25), channel_id=1, source_target_pairs={{0,24},{2,26},{4,28},{6,30},{8,16},{10,18},{12,20},{14,22},{16,8},... | collective-permute-start | bytes 786440 | tf_op jit(solution)/shard_map/ppermute | solution.py:67
  719.4 18.3 %collective-permute-start.17 = (bf16[128,1024]{1,0:T(8,128)(2,1)}, bf16[128,1024]{1,0:T(8,128)(2,1)S(1)}, u32[]{:S(2)}, u32[]{:S(2)}) collective-permute-start(bf16[128,1024]{1,0:T(8,128)(2,1)} %add_convert_fusion.26), channel_id=1, source_target_pairs={{0,16},{2,18},{4,20},{6,22},{8,24},{10,26},{12,28},{14,30},{16,0},... | collective-permute-start | bytes 786440 | tf_op jit(solution)/shard_map/ppermute | solution.py:67
  725.1 16.9 %collective-permute-start.16 = (bf16[128,1024]{1,0:T(8,128)(2,1)}, bf16[128,1024]{1,0:T(8,128)(2,1)S(1)}, u32[]{:S(2)}, u32[]{:S(2)}) collective-permute-start(bf16[128,1024]{1,0:T(8,128)(2,1)} %add_convert_fusion.27), channel_id=1, source_target_pairs={{0,8},{2,10},{4,12},{6,14},{8,0},{10,2},{12,4},{14,6},{16,24},{18,... | collective-permute-start | bytes 786440 | tf_op jit(solution)/shard_map/ppermute | solution.py:67
  731.2 33.8 %collective-permute-start.48 = (bf16[384,1408]{1,0:T(8,128)(2,1)}, bf16[384,1408]{1,0:T(8,128)(2,1)S(1)}, u32[]{:S(2)}, u32[]{:S(2)}) collective-permute-start(bf16[384,1408]{1,0:T(8,128)(2,1)} %copy-done.46), channel_id=1, source_target_pairs={{0,8},{2,10},{4,12},{6,14},{24,16},{26,18},{28,20},{30,22},{1,9},{... | collective-permute-start | bytes 3244040 | tf_op jit(solution)/shard_map/ppermute | solution.py:67
  737.7 50.5 %collective-permute-start.42 = (bf16[384,1408]{1,0:T(8,128)(2,1)S(1)}, bf16[384,1408]{1,0:T(8,128)(2,1)S(1)}, u32[]{:S(2)}, u32[]{:S(2)}) collective-permute-start(bf16[384,1408]{1,0:T(8,128)(2,1)S(1)} %copy-done.45), channel_id=1, source_target_pairs={{0,8},{2,10},{4,12},{6,14},{24,16},{26,18},{28,20},{30,22},{1,9},{... | collective-permute-start | bytes 3244040 | tf_op jit(solution)/shard_map/ppermute | solution.py:67
  741.9 69.4 %collective-permute-start.36 = (bf16[384,1408]{1,0:T(8,128)(2,1)S(1)}, bf16[384,1408]{1,0:T(8,128)(2,1)S(1)}, u32[]{:S(2)}, u32[]{:S(2)}) collective-permute-start(bf16[384,1408]{1,0:T(8,128)(2,1)S(1)} %copy-done.43), channel_id=1, source_target_pairs={{0,8},{2,10},{4,12},{6,14},{24,16},{26,18},{28,20},{30,22},{1,9},{... | collective-permute-start | bytes 3244040 | tf_op jit(solution)/shard_map/ppermute | solution.py:67
  748.8 22.3 %collective-permute-start.55 = (bf16[128,1408]{1,0:T(8,128)(2,1)S(1)}, bf16[128,1408]{1,0:T(8,128)(2,1)S(1)}, u32[]{:S(2)}, u32[]{:S(2)}) collective-permute-start(bf16[128,1408]{1,0:T(8,128)(2,1)S(1)} %copy-done.54), channel_id=1, source_target_pairs={{8,0},{10,2},{12,4},{14,6},{16,24},{18,26},{20,28},{22,30},{9,1},{... | collective-permute-start | bytes 1081352 | tf_op jit(solution)/shard_map/ppermute | solution.py:67
  765.1 27.8 %collective-permute-start.49 = (bf16[128,1408]{1,0:T(8,128)(2,1)S(1)}, bf16[128,1408]{1,0:T(8,128)(2,1)S(1)}, u32[]{:S(2)}, u32[]{:S(2)}) collective-permute-start(bf16[128,1408]{1,0:T(8,128)(2,1)S(1)} %copy-done.53), channel_id=1, source_target_pairs={{8,0},{10,2},{12,4},{14,6},{16,24},{18,26},{20,28},{22,30},{9,1},{... | collective-permute-start | bytes 1081352 | tf_op jit(solution)/shard_map/ppermute | solution.py:67
  766.6 27.5 %collective-permute-start.43 = (bf16[128,1408]{1,0:T(8,128)(2,1)S(1)}, bf16[128,1408]{1,0:T(8,128)(2,1)S(1)}, u32[]{:S(2)}, u32[]{:S(2)}) collective-permute-start(bf16[128,1408]{1,0:T(8,128)(2,1)S(1)} %copy-done.55), channel_id=1, source_target_pairs={{8,0},{10,2},{12,4},{14,6},{16,24},{18,26},{20,28},{22,30},{9,1},{... | collective-permute-start | bytes 1081352 | tf_op jit(solution)/shard_map/ppermute | solution.py:67
  771.1 41.5 %collective-permute-start.57 = (bf16[128,1408]{1,0:T(8,128)(2,1)S(1)}, bf16[128,1408]{1,0:T(8,128)(2,1)S(1)}, u32[]{:S(2)}, u32[]{:S(2)}) collective-permute-start(bf16[128,1408]{1,0:T(8,128)(2,1)S(1)} %get-tuple-element.77), channel_id=1, source_target_pairs={{8,16},{10,18},{12,20},{14,22},{16,8},{18,10},{20,12},{22,14},{9,1... | collective-permute-start | bytes 1081352 | tf_op jit(solution)/shard_map/ppermute | solution.py:67
  788.2 67.7 %collective-permute-start.60 = (bf16[384,2816]{1,0:T(8,128)(2,1)S(1)}, bf16[384,2816]{1,0:T(8,128)(2,1)S(1)}, u32[]{:S(2)}, u32[]{:S(2)}) collective-permute-start(bf16[384,2816]{1,0:T(8,128)(2,1)S(1)} %fusion.7), channel_id=1, source_target_pairs={{0,8},{2,10},{4,12},{6,14},{24,16},{26,18},{28,20},{30,22},{1,9},{... | collective-permute-start | bytes 6488072 | tf_op jit(solution)/shard_map/ppermute | solution.py:67
  792.9 20.7 %collective-permute-start.56 = (bf16[128,1408]{1,0:T(8,128)(2,1)S(1)}, bf16[128,1408]{1,0:T(8,128)(2,1)S(1)}, u32[]{:S(2)}, u32[]{:S(2)}) collective-permute-start(bf16[128,1408]{1,0:T(8,128)(2,1)S(1)} %get-tuple-element.76), channel_id=1, source_target_pairs={{8,24},{10,26},{12,28},{14,30},{16,0},{18,2},{20,4},{22,6},{9,25},... | collective-permute-start | bytes 1081352 | tf_op jit(solution)/shard_map/ppermute | solution.py:67
  794.2 22.5 %collective-permute-start.51 = (bf16[128,1408]{1,0:T(8,128)(2,1)S(1)}, bf16[128,1408]{1,0:T(8,128)(2,1)S(1)}, u32[]{:S(2)}, u32[]{:S(2)}) collective-permute-start(bf16[128,1408]{1,0:T(8,128)(2,1)S(1)} %get-tuple-element.75), channel_id=1, source_target_pairs={{8,16},{10,18},{12,20},{14,22},{16,8},{18,10},{20,12},{22,14},{9,1... | collective-permute-start | bytes 1081352 | tf_op jit(solution)/shard_map/ppermute | solution.py:67
  811.3 14.2 %collective-permute-start.50 = (bf16[128,1408]{1,0:T(8,128)(2,1)S(1)}, bf16[128,1408]{1,0:T(8,128)(2,1)S(1)}, u32[]{:S(2)}, u32[]{:S(2)}) collective-permute-start(bf16[128,1408]{1,0:T(8,128)(2,1)S(1)} %get-tuple-element.74), channel_id=1, source_target_pairs={{8,24},{10,26},{12,28},{14,30},{16,0},{18,2},{20,4},{22,6},{9,25},... | collective-permute-start | bytes 1081352 | tf_op jit(solution)/shard_map/ppermute | solution.py:67
  812.6 13.5 %collective-permute-start.45 = (bf16[128,1408]{1,0:T(8,128)(2,1)S(1)}, bf16[128,1408]{1,0:T(8,128)(2,1)S(1)}, u32[]{:S(2)}, u32[]{:S(2)}) collective-permute-start(bf16[128,1408]{1,0:T(8,128)(2,1)S(1)} %get-tuple-element.73), channel_id=1, source_target_pairs={{8,16},{10,18},{12,20},{14,22},{16,8},{18,10},{20,12},{22,14},{9,1... | collective-permute-start | bytes 1081352 | tf_op jit(solution)/shard_map/ppermute | solution.py:67
  813.5 27.3 %collective-permute-start.44 = (bf16[128,1408]{1,0:T(8,128)(2,1)S(1)}, bf16[128,1408]{1,0:T(8,128)(2,1)S(1)}, u32[]{:S(2)}, u32[]{:S(2)}) collective-permute-start(bf16[128,1408]{1,0:T(8,128)(2,1)S(1)} %get-tuple-element.72), channel_id=1, source_target_pairs={{8,24},{10,26},{12,28},{14,30},{16,0},{18,2},{20,4},{22,6},{9,25},... | collective-permute-start | bytes 1081352 | tf_op jit(solution)/shard_map/ppermute | solution.py:67
  816.7 25.8 %collective-permute-start.37 = (bf16[128,1408]{1,0:T(8,128)(2,1)S(1)}, bf16[128,1408]{1,0:T(8,128)(2,1)S(1)}, u32[]{:S(2)}, u32[]{:S(2)}) collective-permute-start(bf16[128,1408]{1,0:T(8,128)(2,1)S(1)} %copy-done.52), channel_id=1, source_target_pairs={{8,0},{10,2},{12,4},{14,6},{16,24},{18,26},{20,28},{22,30},{9,1},{... | collective-permute-start | bytes 1081352 | tf_op jit(solution)/shard_map/ppermute | solution.py:67
  825.5 17.0 %collective-permute-start.39 = (bf16[128,1408]{1,0:T(8,128)(2,1)S(1)}, bf16[128,1408]{1,0:T(8,128)(2,1)S(1)}, u32[]{:S(2)}, u32[]{:S(2)}) collective-permute-start(bf16[128,1408]{1,0:T(8,128)(2,1)S(1)} %get-tuple-element.71), channel_id=1, source_target_pairs={{8,16},{10,18},{12,20},{14,22},{16,8},{18,10},{20,12},{22,14},{9,1... | collective-permute-start | bytes 1081352 | tf_op jit(solution)/shard_map/ppermute | solution.py:67
  826.2 25.7 %collective-permute-start.38 = (bf16[128,1408]{1,0:T(8,128)(2,1)S(1)}, bf16[128,1408]{1,0:T(8,128)(2,1)S(1)}, u32[]{:S(2)}, u32[]{:S(2)}) collective-permute-start(bf16[128,1408]{1,0:T(8,128)(2,1)S(1)} %get-tuple-element.70), channel_id=1, source_target_pairs={{8,24},{10,26},{12,28},{14,30},{16,0},{18,2},{20,4},{22,6},{9,25},... | collective-permute-start | bytes 1081352 | tf_op jit(solution)/shard_map/ppermute | solution.py:67
  853.7 15.3 %collective-permute-start.61 = (bf16[128,2816]{1,0:T(8,128)(2,1)S(1)}, bf16[128,2816]{1,0:T(8,128)(2,1)S(1)}, u32[]{:S(2)}, u32[]{:S(2)}) collective-permute-start(bf16[128,2816]{1,0:T(8,128)(2,1)S(1)} %slice.889), channel_id=1, source_target_pairs={{8,0},{10,2},{12,4},{14,6},{16,24},{18,26},{20,28},{22,30},{9,1},{... | collective-permute-start | bytes 2162696 | tf_op jit(solution)/shard_map/ppermute | solution.py:67
  856.2 12.8 %collective-permute-start.63 = (bf16[128,2816]{1,0:T(8,128)(2,1)S(1)}, bf16[128,2816]{1,0:T(8,128)(2,1)S(1)}, u32[]{:S(2)}, u32[]{:S(2)}) collective-permute-start(bf16[128,2816]{1,0:T(8,128)(2,1)S(1)} %get-tuple-element.69), channel_id=1, source_target_pairs={{8,16},{10,18},{12,20},{14,22},{16,8},{18,10},{20,12},{22,14},{9,1... | collective-permute-start | bytes 2162696 | tf_op jit(solution)/shard_map/ppermute | solution.py:67
  856.9 34.9 %collective-permute-start.62 = (bf16[128,2816]{1,0:T(8,128)(2,1)S(1)}, bf16[128,2816]{1,0:T(8,128)(2,1)S(1)}, u32[]{:S(2)}, u32[]{:S(2)}) collective-permute-start(bf16[128,2816]{1,0:T(8,128)(2,1)S(1)} %get-tuple-element.68), channel_id=1, source_target_pairs={{8,24},{10,26},{12,28},{14,30},{16,0},{18,2},{20,4},{22,6},{9,25},... | collective-permute-start | bytes 2162696 | tf_op jit(solution)/shard_map/ppermute | solution.py:67
  (94 other events, 1118.4 us)
Sparse Core Ops, SparseCore 0:
  12.8 94.1 all-gather.5
  109.2 180.7 all-gather.3

commit v4 on v3

--- a/solution.py
+++ b/solution.py
@@ -368,20 +368,22 @@
 
     gate_up_grad = jnp.stack([gate_grad, up_grad], axis=1)[None]
     norm_terms = jnp.stack([gain_one, gain_two, shift_one, shift_two])
+    norm_terms = norm_terms + other(norm_terms)
     norm_terms = jnp.swapaxes(norm_terms.reshape(4, count, block), 0, 1).reshape(count, 4 * block)
     bias_terms = jnp.transpose(bias_terms.reshape(3, heads, count, piece), (2, 0, 1, 3)).reshape(count, -1)
     terms = scatter_rows(grid, jnp.concatenate([norm_terms, bias_terms], axis=1)[order])
     norm_part = terms[: 4 * block].reshape(4, block)
-    norm_part = norm_part + other(norm_part)
+    out_weight_grad = out_grad.T[None]
+    qkv_weight_grad = jnp.stack([q_grad, k_grad, v_grad], axis=1)[None]
     bias_part = terms[4 * block :].reshape(3, heads, piece)
     return (
         block_output,
         input_grad,
         norm_part[None, 0:2],
         norm_part[None, 2:4],
-        jnp.stack([q_grad, k_grad, v_grad], axis=1)[None],
+        qkv_weight_grad,
         bias_part[None],
-        out_grad.T[None],
+        out_weight_grad,
         gate_up_grad,
         down_grad.T[None],
     )

time: 910 us -> 908 us (level)
  transfers between devices with their start and end apart: 66 -> 66, of which waited for: 35 -> 34; matrix products, arithmetic and copies ran while one was open for 22% -> 22% of each run, Pallas kernels for 2% -> 2%
where the time goes in v4:
time: 908 us; the launch traced here: 901 us
  waiting for transfers between devices  530 us (58%)
  matrix products  159 us (18%)
  starting transfers between devices  81.5 us (9%)
  local copies, waits for them, and re-layouts  63.2 us (7%)
  other arithmetic  34.6 us (4%)
  Pallas kernels  16.5 us (2%)
  between operations  16.3 us (2%)
    ppermute x20, waiting for transfers between devices, shift(): return lax.ppermute(rows, 'fsdp', self.moves(**by))  167 us
    ppermute x35, waiting for transfers between devices, cross(): return lax.ppermute(rows, 'fsdp', moves)  152 us
    dot_general x51, matrix products, times(): lax.dot_general(left, right, (((1,), (0,)), ((), ())), preferred_element_...  123 us
    all_gather x1, waiting for transfers between devices, shards(): mlp_all = lax.all_gather(mlp_pack, 'fsdp', axis=1, tiled=True)  107 us
    all_gather x1, waiting for transfers between devices, shards(): packs = lax.all_gather(pack, 'fsdp', axis=0)  65.5 us
    ppermute x35, starting transfers between devices, cross(): return lax.ppermute(rows, 'fsdp', moves)  56.7 us
    ppermute x9, waiting for transfers between devices, other(): return lax.ppermute(rows, 'tp', [(0, 1), (1, 0)])  39.3 us
    unnamed x199, local copies, waits for them, and re-layouts  32 us
  transfers between devices with their start and end apart: 66, of which 34 were waited for; matrix products, arithmetic and copies ran while one was open for 22% of the time, Pallas kernels for 2%

profile of v4, /device:TPU:0, one launch (start us, length us, event | category | flops | bytes accessed | tf_op | source)
XLA Modules:
  0.0 900.8 jit_solution(7248636207032708209)
XLA Ops:
  12.8 2.9 fusion.231
  15.7 3.8 copy.96
  21.4 2.9 pad_maximum_fusion
  25.3 2.8 collective-permute-start
  30.9 10.0 %collective-permute-done = bf16[128,2048]{1,0:T(8,128)(2,1)S(1)} collective-permute-done((bf16[128,2048]{1,0:T(8,128)(2,1)S(1)}, bf16[128,2048]{1,0:T(8,128)(2,1)S(1)}, u32[]{:S(2)}, u32[]{:S(2)}) %collective-permute-start) | collective-permute-done | bytes 524320 | tf_op jit(solution)/shard_map/ppermute | solution.py:170
  41.6 65.5 %all-gather.6.cloned.1.call-done = bf16[8448,1024]{1,0:T(8,128)(2,1)} async-done(((bf16[528,1024]{1,0:T(8,128)(2,1)}), bf16[8448,1024]{1,0:T(8,128)(2,1)}) %all-gather.6.cloned.1.call-update) | async-done | bytes 17301520 | tf_op jit(solution)/shard_map/all_gather | solution.py:275
  110.0 11.7 %fusion.230 = (bf16[16,128,1024]{2,1,0:T(8,128)(2,1)}, bf16[16,128,1024]{2,1,0:T(8,128)(2,1)}, bf16[16,128,1024]{2,1,0:T(8,128)(2,1)}, bf16[16,128,1024]{2,1,0:T(8,128)(2,1)S(1)}) fusion(bf16[16,528,1024]{2,1,0:T(8,128)(2,1)} %bitcast.214), kind=kLoop, calls=%fused_computation.396 | loop fusion | bytes 33554432 | tf_op jit(solution)/shard_map/slice | solution.py:280
  126.3 4.4 convolution_add_fusion.16
  132.6 4.4 convolution_add_fusion.17
  150.5 10.6 %collective-permute-done.1 = bf16[128,2048]{1,0:T(8,128)(2,1)S(1)} collective-permute-done((bf16[128,2048]{1,0:T(8,128)(2,1)S(1)}, bf16[128,2048]{1,0:T(8,128)(2,1)S(1)}, u32[]{:S(2)}, u32[]{:S(2)}) %collective-permute-start.1) | collective-permute-done | bytes 524320 | tf_op jit(solution)/shard_map/ppermute | solution.py:170
  167.5 4.2 shard_map.172
  171.7 4.2 shard_map.169
  179.1 4.1 shard_map.171
  183.2 106.8 %all-gather.4.cloned.1.call-done = bf16[3,2048,2816]{1,2,0:T(8,128)(2,1)} async-done(((bf16[3,128,2816]{1,2,0:T(8,128)(2,1)}), bf16[3,2048,2816]{1,2,0:T(8,128)(2,1)}) %all-gather.4.cloned.1.call-update) | async-done | bytes 34603024 | tf_op jit(solution)/shard_map/all_gather | solution.py:277
  290.0 6.8 fusion.3
  296.8 9.7 %multiply_convert_fusion.3 = (bf16[256,2816]{1,0:T(8,128)(2,1)S(1)}, f32[256,2816]{1,0:T(8,128)}) fusion(f32[256,2816]{1,0:T(8,128)S(1)} %fusion.3, bf16[3,2048,2816]{1,2,0:T(8,128)(2,1)} %all-gather.4.cloned.1.call-done, bf16[128,2048]{1,0:T(8,128)(2,1)} %collective-permute-done.3, bf16[128,2048]{1,0:T(8,128)(2,1)} %add_convert_fusion.7), kind=kOutput, calls=%fused_computation.51 | convolution fusion | flops 2959212544 | bytes 19791872 | tf_op jit(solution)/shard_map/dot_general | solution.py:22
  306.4 8.1 multiply_convert_fusion.1
  314.5 7.0 fusion.2
  321.6 6.5 fusion.28
  329.7 2.6 convolution_convert_fusion.1
  332.3 2.5 convolution_convert_fusion.2
  334.8 2.6 convolution_convert_fusion.3
  337.4 4.9 collective-permute-done.4
  343.4 2.6 fusion.228
  347.4 2.7 convolution_convert_fusion.4
  350.7 4.1 convolution_convert_fusion
  354.8 4.4 collective-permute-done.5
  361.9 3.9 multiply_convert_fusion
  371.5 4.0 shard_map.170
  375.6 6.6 fusion
  400.1 3.1 convolution_convert_fusion.5
  403.3 6.1 collective-permute-done.7
  412.1 2.9 collective-permute-done.8
  428.3 2.6 collective-permute-done.11
  456.4 16.2 %collective-permute-done.25 = bf16[512,1024]{1,0:T(8,128)(2,1)S(1)} collective-permute-done((bf16[512,1024]{1,0:T(8,128)(2,1)S(1)}, bf16[512,1024]{1,0:T(8,128)(2,1)S(1)}, u32[]{:S(2)}, u32[]{:S(2)}) %collective-permute-start.25) | collective-permute-done | bytes 1048608 | tf_op jit(solution)/shard_map/ppermute | solution.py:53
  479.0 77.9 %collective-permute-done.20 = bf16[512,1024]{1,0:T(8,128)(2,1)S(1)} collective-permute-done((bf16[512,1024]{1,0:T(8,128)(2,1)S(1)}, bf16[512,1024]{1,0:T(8,128)(2,1)S(1)}, u32[]{:S(2)}, u32[]{:S(2)}) %collective-permute-start.20) | collective-permute-done | bytes 1048608 | tf_op jit(solution)/shard_map/ppermute | solution.py:53
  563.9 15.5 %collective-permute-done.15 = bf16[512,1024]{1,0:T(8,128)(2,1)S(1)} collective-permute-done((bf16[512,1024]{1,0:T(8,128)(2,1)S(1)}, bf16[512,1024]{1,0:T(8,128)(2,1)S(1)}, u32[]{:S(2)}, u32[]{:S(2)}) %collective-permute-start.15) | collective-permute-done | bytes 1048608 | tf_op jit(solution)/shard_map/ppermute | solution.py:53
  583.6 18.2 %collective-permute-done.30 = bf16[512,1024]{1,0:T(8,128)(2,1)S(1)} collective-permute-done((bf16[512,1024]{1,0:T(8,128)(2,1)S(1)}, bf16[512,1024]{1,0:T(8,128)(2,1)S(1)}, u32[]{:S(2)}, u32[]{:S(2)}) %collective-permute-start.30) | collective-permute-done | bytes 1048608 | tf_op jit(solution)/shard_map/ppermute | solution.py:53
  606.5 3.0 collective-permute-start.28
  609.5 2.8 fusion.26
  617.9 3.6 add_convert_fusion
  621.5 11.2 %collective-permute-done.41 = bf16[512,1408]{1,0:T(8,128)(2,1)S(1)} collective-permute-done((bf16[512,1408]{1,0:T(8,128)(2,1)S(1)}, bf16[512,1408]{1,0:T(8,128)(2,1)S(1)}, u32[]{:S(2)}, u32[]{:S(2)}) %collective-permute-start.41) | collective-permute-done | bytes 1441824 | tf_op jit(solution)/shard_map/ppermute | solution.py:53
  636.5 27.1 %collective-permute-done.35 = bf16[512,1408]{1,0:T(8,128)(2,1)S(1)} collective-permute-done((bf16[512,1408]{1,0:T(8,128)(2,1)S(1)}, bf16[512,1408]{1,0:T(8,128)(2,1)S(1)}, u32[]{:S(2)}, u32[]{:S(2)}) %collective-permute-start.35) | collective-permute-done | bytes 1441824 | tf_op jit(solution)/shard_map/ppermute | solution.py:53
  668.2 2.5 collective-permute-start.27
  672.6 3.1 collective-permute-start.54
  678.8 5.7 collective-permute-done.27
  684.5 3.8 collective-permute-start.21
  690.4 2.9 collective-permute-start.18
  694.8 23.0 %collective-permute-done.22 = bf16[128,1024]{1,0:T(8,128)(2,1)S(1)} collective-permute-done((bf16[128,1024]{1,0:T(8,128)(2,1)}, bf16[128,1024]{1,0:T(8,128)(2,1)S(1)}, u32[]{:S(2)}, u32[]{:S(2)}) %collective-permute-start.22) | collective-permute-done | bytes 262176 | tf_op jit(solution)/shard_map/ppermute | solution.py:67
  717.8 3.3 collective-permute-start.17
  725.8 4.6 collective-permute-done.18
  733.1 3.6 collective-permute-done.17
  740.3 4.3 collective-permute-start.36
  750.1 13.4 %collective-permute-done.48 = bf16[384,1408]{1,0:T(8,128)(2,1)S(1)} collective-permute-done((bf16[384,1408]{1,0:T(8,128)(2,1)}, bf16[384,1408]{1,0:T(8,128)(2,1)S(1)}, u32[]{:S(2)}, u32[]{:S(2)}) %collective-permute-start.48) | collective-permute-done | bytes 1081376 | tf_op jit(solution)/shard_map/ppermute | solution.py:67
  766.5 3.2 fusion.7
  770.4 16.1 %collective-permute-done.42 = bf16[384,1408]{1,0:T(8,128)(2,1)S(1)} collective-permute-done((bf16[384,1408]{1,0:T(8,128)(2,1)S(1)}, bf16[384,1408]{1,0:T(8,128)(2,1)S(1)}, u32[]{:S(2)}, u32[]{:S(2)}) %collective-permute-start.42) | collective-permute-done | bytes 1081376 | tf_op jit(solution)/shard_map/ppermute | solution.py:67
  786.5 4.5 collective-permute-start.60
  793.2 16.5 %collective-permute-done.36 = bf16[384,1408]{1,0:T(8,128)(2,1)S(1)} collective-permute-done((bf16[384,1408]{1,0:T(8,128)(2,1)S(1)}, bf16[384,1408]{1,0:T(8,128)(2,1)S(1)}, u32[]{:S(2)}, u32[]{:S(2)}) %collective-permute-start.36) | collective-permute-done | bytes 1081376 | tf_op jit(solution)/shard_map/ppermute | solution.py:67
  816.5 7.4 collective-permute-done.50
  827.5 11.8 %collective-permute-done.44 = bf16[128,1408]{1,0:T(8,128)(2,1)S(1)} collective-permute-done((bf16[128,1408]{1,0:T(8,128)(2,1)S(1)}, bf16[128,1408]{1,0:T(8,128)(2,1)S(1)}, u32[]{:S(2)}, u32[]{:S(2)}) %collective-permute-start.44) | collective-permute-done | bytes 360480 | tf_op jit(solution)/shard_map/ppermute | solution.py:67
  840.9 9.4 %collective-permute-done.38 = bf16[128,1408]{1,0:T(8,128)(2,1)S(1)} collective-permute-done((bf16[128,1408]{1,0:T(8,128)(2,1)S(1)}, bf16[128,1408]{1,0:T(8,128)(2,1)S(1)}, u32[]{:S(2)}, u32[]{:S(2)}) %collective-permute-start.38) | collective-permute-done | bytes 360480 | tf_op jit(solution)/shard_map/ppermute | solution.py:67
  856.7 3.8 copy.88
  860.5 6.8 collective-permute-done.61
  867.3 22.5 %collective-permute-done.62 = bf16[128,2816]{1,0:T(8,128)(2,1)S(1)} collective-permute-done((bf16[128,2816]{1,0:T(8,128)(2,1)S(1)}, bf16[128,2816]{1,0:T(8,128)(2,1)S(1)}, u32[]{:S(2)}, u32[]{:S(2)}) %collective-permute-start.62) | collective-permute-done | bytes 720928 | tf_op jit(solution)/shard_map/ppermute | solution.py:67
  (452 shorter events, 205.0 us)
Async XLA Ops:
  7.2 99.9 %all-gather.6.cloned.1.call-start = ((), (), s32[]{:S(2)}) async-start(), calls=%async_computation.1 | async-start | bytes 18382848 | tf_op jit(solution)/shard_map/all_gather | solution.py:275
  12.7 277.2 %all-gather.4.cloned.1.call-start = ((), (), s32[]{:S(2)}) async-start(), calls=%async_computation | async-start | bytes 36765696 | tf_op jit(solution)/shard_map/all_gather | solution.py:277
  25.3 15.6 %collective-permute-start = (bf16[128,2048]{1,0:T(8,128)(2,1)S(1)}, bf16[128,2048]{1,0:T(8,128)(2,1)S(1)}, u32[]{:S(2)}, u32[]{:S(2)}) collective-permute-start(bf16[128,2048]{1,0:T(8,128)(2,1)S(1)} %copy-done), channel_id=1, source_target_pairs={{0,1},{1,0},{2,3},{3,2},{4,5},{5,4},{6,7},{7,6},{8,9},{9,8},{10,11... | collective-permute-start | bytes 1572872 | tf_op jit(solution)/shard_map/ppermute | solution.py:170
  28.1 137.3 %collective-permute-start.2 = (bf16[128,2048]{1,0:T(8,128)(2,1)}, bf16[128,2048]{1,0:T(8,128)(2,1)}, u32[]{:S(2)}, u32[]{:S(2)}) collective-permute-start(bf16[128,2048]{1,0:T(8,128)(2,1)} %param.12), channel_id=1, source_target_pairs={{0,1},{1,0},{2,3},{3,2},{4,5},{5,4},{6,7},{7,6},{8,9},{9,8},{10,11... | collective-permute-start | bytes 1572872 | tf_op jit(solution)/shard_map/ppermute | solution.py:170
  147.3 13.9 %collective-permute-start.1 = (bf16[128,2048]{1,0:T(8,128)(2,1)S(1)}, bf16[128,2048]{1,0:T(8,128)(2,1)S(1)}, u32[]{:S(2)}, u32[]{:S(2)}) collective-permute-start(bf16[128,2048]{1,0:T(8,128)(2,1)S(1)} %slice.1225), channel_id=1, source_target_pairs={{0,1},{1,0},{2,3},{3,2},{4,5},{5,4},{6,7},{7,6},{8,9},{9,8},{10,11... | collective-permute-start | bytes 1572872 | tf_op jit(solution)/shard_map/ppermute | solution.py:170
  163.4 13.4 %collective-permute-start.3 = (bf16[128,2048]{1,0:T(8,128)(2,1)}, bf16[128,2048]{1,0:T(8,128)(2,1)}, u32[]{:S(2)}, u32[]{:S(2)}) collective-permute-start(bf16[128,2048]{1,0:T(8,128)(2,1)} %add_convert_fusion.7), channel_id=1, source_target_pairs={{0,1},{1,0},{2,3},{3,2},{4,5},{5,4},{6,7},{7,6},{8,9},{9,8},{10,11... | collective-permute-start | bytes 1572872 | tf_op jit(solution)/shard_map/ppermute | solution.py:170
  328.2 14.2 %collective-permute-start.4 = (bf16[128,2048]{1,0:T(8,128)(2,1)S(1)}, bf16[128,2048]{1,0:T(8,128)(2,1)S(1)}, u32[]{:S(2)}, u32[]{:S(2)}) collective-permute-start(bf16[128,2048]{1,0:T(8,128)(2,1)S(1)} %slice.1224), channel_id=1, source_target_pairs={{0,1},{1,0},{2,3},{3,2},{4,5},{5,4},{6,7},{7,6},{8,9},{9,8},{10,11... | collective-permute-start | bytes 1572872 | tf_op jit(solution)/shard_map/ppermute | solution.py:170
  345.9 13.2 %collective-permute-start.5 = (bf16[128,2048]{1,0:T(8,128)(2,1)S(1)}, bf16[128,2048]{1,0:T(8,128)(2,1)S(1)}, u32[]{:S(2)}, u32[]{:S(2)}) collective-permute-start(bf16[128,2048]{1,0:T(8,128)(2,1)S(1)} %get-tuple-element.58), channel_id=1, source_target_pairs={{0,1},{1,0},{2,3},{3,2},{4,5},{5,4},{6,7},{7,6},{8,9},{9,8},{10,11... | collective-permute-start | bytes 1572872 | tf_op jit(solution)/shard_map/ppermute | solution.py:170
  350.1 83.2 %collective-permute-start.52 = (bf16[1024,1408]{1,0:T(8,128)(2,1)}, bf16[1024,1408]{1,0:T(8,128)(2,1)}, u32[]{:S(2)}, u32[]{:S(2)}) collective-permute-start(bf16[1024,1408]{1,0:T(8,128)(2,1)} %convolution_convert_fusion.1), channel_id=1, source_target_pairs={{0,2},{2,0},{4,6},{6,4},{8,10},{10,8},{12,14},{14,12},{16,18},{18,... | collective-permute-start | bytes 8650760 | tf_op jit(solution)/shard_map/ppermute | solution.py:53
  350.1 86.5 %collective-permute-start.46 = (bf16[1024,1408]{1,0:T(8,128)(2,1)}, bf16[1024,1408]{1,0:T(8,128)(2,1)}, u32[]{:S(2)}, u32[]{:S(2)}) collective-permute-start(bf16[1024,1408]{1,0:T(8,128)(2,1)} %convolution_convert_fusion.2), channel_id=1, source_target_pairs={{0,2},{2,0},{4,6},{6,4},{8,10},{10,8},{12,14},{14,12},{16,18},{18,... | collective-permute-start | bytes 8650760 | tf_op jit(solution)/shard_map/ppermute | solution.py:53
  350.6 86.6 %collective-permute-start.40 = (bf16[1024,1408]{1,0:T(8,128)(2,1)}, bf16[1024,1408]{1,0:T(8,128)(2,1)}, u32[]{:S(2)}, u32[]{:S(2)}) collective-permute-start(bf16[1024,1408]{1,0:T(8,128)(2,1)} %convolution_convert_fusion.3), channel_id=1, source_target_pairs={{0,2},{2,0},{4,6},{6,4},{8,10},{10,8},{12,14},{14,12},{16,18},{18,... | collective-permute-start | bytes 8650760 | tf_op jit(solution)/shard_map/ppermute | solution.py:53
  383.1 39.3 %collective-permute-start.6 = (bf16[128,2048]{1,0:T(8,128)(2,1)}, bf16[128,2048]{1,0:T(8,128)(2,1)}, u32[]{:S(2)}, u32[]{:S(2)}) collective-permute-start(bf16[128,2048]{1,0:T(8,128)(2,1)} %slice.1223), channel_id=1, source_target_pairs={{0,1},{1,0},{2,3},{3,2},{4,5},{5,4},{6,7},{7,6},{8,9},{9,8},{10,11... | collective-permute-start | bytes 1572872 | tf_op jit(solution)/shard_map/ppermute | solution.py:170
  396.9 12.4 %collective-permute-start.7 = (bf16[128,2048]{1,0:T(8,128)(2,1)}, bf16[128,2048]{1,0:T(8,128)(2,1)}, u32[]{:S(2)}, u32[]{:S(2)}) collective-permute-start(bf16[128,2048]{1,0:T(8,128)(2,1)} %slice.1222), channel_id=1, source_target_pairs={{0,1},{1,0},{2,3},{3,2},{4,5},{5,4},{6,7},{7,6},{8,9},{9,8},{10,11... | collective-permute-start | bytes 1572872 | tf_op jit(solution)/shard_map/ppermute | solution.py:170
  411.0 4.0 collective-permute-start.8
  418.0 3.8 collective-permute-start.10
  421.8 5.5 collective-permute-start.13
  422.4 4.9 collective-permute-start.12
  427.3 12.7 %collective-permute-start.24 = (bf16[1024,1024]{1,0:T(8,128)(2,1)}, bf16[1024,1024]{1,0:T(8,128)(2,1)}, u32[]{:S(2)}, u32[]{:S(2)}) collective-permute-start(bf16[1024,1024]{1,0:T(8,128)(2,1)} %convolution_convert_fusion.6), channel_id=1, source_target_pairs={{0,2},{2,0},{4,6},{6,4},{8,10},{10,8},{12,14},{14,12},{16,18},{18,... | collective-permute-start | bytes 6291464 | tf_op jit(solution)/shard_map/ppermute | solution.py:53
  430.9 15.6 %collective-permute-start.34 = (bf16[1024,1408]{1,0:T(8,128)(2,1)}, bf16[1024,1408]{1,0:T(8,128)(2,1)}, u32[]{:S(2)}, u32[]{:S(2)}) collective-permute-start(bf16[1024,1408]{1,0:T(8,128)(2,1)} %convolution_convert_fusion.4), channel_id=1, source_target_pairs={{0,2},{2,0},{4,6},{6,4},{8,10},{10,8},{12,14},{14,12},{16,18},{18,... | collective-permute-start | bytes 8650760 | tf_op jit(solution)/shard_map/ppermute | solution.py:53
  433.3 16.4 %collective-permute-start.19 = (bf16[1024,1024]{1,0:T(8,128)(2,1)}, bf16[1024,1024]{1,0:T(8,128)(2,1)}, u32[]{:S(2)}, u32[]{:S(2)}) collective-permute-start(bf16[1024,1024]{1,0:T(8,128)(2,1)} %convolution_convert_fusion.7), channel_id=1, source_target_pairs={{0,2},{2,0},{4,6},{6,4},{8,10},{10,8},{12,14},{14,12},{16,18},{18,... | collective-permute-start | bytes 6291464 | tf_op jit(solution)/shard_map/ppermute | solution.py:53
  436.7 15.7 %collective-permute-start.14 = (bf16[1024,1024]{1,0:T(8,128)(2,1)}, bf16[1024,1024]{1,0:T(8,128)(2,1)S(1)}, u32[]{:S(2)}, u32[]{:S(2)}) collective-permute-start(bf16[1024,1024]{1,0:T(8,128)(2,1)} %convolution_convert_fusion.8), channel_id=1, source_target_pairs={{0,2},{2,0},{4,6},{6,4},{8,10},{10,8},{12,14},{14,12},{16,18},{18,... | collective-permute-start | bytes 6291464 | tf_op jit(solution)/shard_map/ppermute | solution.py:53
  437.3 16.8 %collective-permute-start.29 = (bf16[1024,1024]{1,0:T(8,128)(2,1)}, bf16[1024,1024]{1,0:T(8,128)(2,1)S(1)}, u32[]{:S(2)}, u32[]{:S(2)}) collective-permute-start(bf16[1024,1024]{1,0:T(8,128)(2,1)} %convolution_convert_fusion.5), channel_id=1, source_target_pairs={{0,2},{2,0},{4,6},{6,4},{8,10},{10,8},{12,14},{14,12},{16,18},{18,... | collective-permute-start | bytes 6291464 | tf_op jit(solution)/shard_map/ppermute | solution.py:53
  440.0 177.6 %collective-permute-start.58 = (bf16[1024,2816]{1,0:T(8,128)(2,1)}, bf16[1024,2816]{1,0:T(8,128)(2,1)S(1)}, u32[]{:S(2)}, u32[]{:S(2)}) collective-permute-start(bf16[1024,2816]{1,0:T(8,128)(2,1)} %convolution_convert_fusion), channel_id=1, source_target_pairs={{0,2},{2,0},{4,6},{6,4},{8,10},{10,8},{12,14},{14,12},{16,18},{18,... | collective-permute-start | bytes 17301512 | tf_op jit(solution)/shard_map/ppermute | solution.py:53
  446.5 26.1 %collective-permute-start.25 = (bf16[512,1024]{1,0:T(8,128)(2,1)S(1)}, bf16[512,1024]{1,0:T(8,128)(2,1)S(1)}, u32[]{:S(2)}, u32[]{:S(2)}) collective-permute-start(bf16[512,1024]{1,0:T(8,128)(2,1)S(1)} %add_convert_fusion.2), channel_id=1, source_target_pairs={{0,4},{2,6},{4,0},{6,2},{8,12},{10,14},{12,8},{14,10},{16,20},{18,... | collective-permute-start | bytes 3145736 | tf_op jit(solution)/shard_map/ppermute | solution.py:53
  449.7 156.8 %collective-permute-start.53 = (bf16[512,1408]{1,0:T(8,128)(2,1)S(1)}, bf16[512,1408]{1,0:T(8,128)(2,1)S(1)}, u32[]{:S(2)}, u32[]{:S(2)}) collective-permute-start(bf16[512,1408]{1,0:T(8,128)(2,1)S(1)} %fusion.22), channel_id=1, source_target_pairs={{0,4},{2,6},{4,0},{6,2},{8,12},{10,14},{12,8},{14,10},{16,20},{18,... | collective-permute-start | bytes 4325384 | tf_op jit(solution)/shard_map/ppermute | solution.py:53
  452.4 161.6 %collective-permute-start.47 = (bf16[512,1408]{1,0:T(8,128)(2,1)S(1)}, bf16[512,1408]{1,0:T(8,128)(2,1)S(1)}, u32[]{:S(2)}, u32[]{:S(2)}) collective-permute-start(bf16[512,1408]{1,0:T(8,128)(2,1)S(1)} %fusion.21), channel_id=1, source_target_pairs={{0,4},{2,6},{4,0},{6,2},{8,12},{10,14},{12,8},{14,10},{16,20},{18,... | collective-permute-start | bytes 4325384 | tf_op jit(solution)/shard_map/ppermute | solution.py:53
  454.1 102.8 %collective-permute-start.20 = (bf16[512,1024]{1,0:T(8,128)(2,1)S(1)}, bf16[512,1024]{1,0:T(8,128)(2,1)S(1)}, u32[]{:S(2)}, u32[]{:S(2)}) collective-permute-start(bf16[512,1024]{1,0:T(8,128)(2,1)S(1)} %add_convert_fusion.3), channel_id=1, source_target_pairs={{0,4},{2,6},{4,0},{6,2},{8,12},{10,14},{12,8},{14,10},{16,20},{18,... | collective-permute-start | bytes 3145736 | tf_op jit(solution)/shard_map/ppermute | solution.py:53
  472.6 106.7 %collective-permute-start.15 = (bf16[512,1024]{1,0:T(8,128)(2,1)S(1)}, bf16[512,1024]{1,0:T(8,128)(2,1)S(1)}, u32[]{:S(2)}, u32[]{:S(2)}) collective-permute-start(bf16[512,1024]{1,0:T(8,128)(2,1)S(1)} %add_convert_fusion.4), channel_id=1, source_target_pairs={{0,4},{2,6},{4,0},{6,2},{8,12},{10,14},{12,8},{14,10},{16,20},{18,... | collective-permute-start | bytes 3145736 | tf_op jit(solution)/shard_map/ppermute | solution.py:53
  556.9 44.9 %collective-permute-start.30 = (bf16[512,1024]{1,0:T(8,128)(2,1)S(1)}, bf16[512,1024]{1,0:T(8,128)(2,1)S(1)}, u32[]{:S(2)}, u32[]{:S(2)}) collective-permute-start(bf16[512,1024]{1,0:T(8,128)(2,1)S(1)} %add_convert_fusion.1), channel_id=1, source_target_pairs={{0,4},{2,6},{4,0},{6,2},{8,12},{10,14},{12,8},{14,10},{16,20},{18,... | collective-permute-start | bytes 3145736 | tf_op jit(solution)/shard_map/ppermute | solution.py:53
  579.4 53.4 %collective-permute-start.41 = (bf16[512,1408]{1,0:T(8,128)(2,1)S(1)}, bf16[512,1408]{1,0:T(8,128)(2,1)S(1)}, u32[]{:S(2)}, u32[]{:S(2)}) collective-permute-start(bf16[512,1408]{1,0:T(8,128)(2,1)S(1)} %fusion.20), channel_id=1, source_target_pairs={{0,4},{2,6},{4,0},{6,2},{8,12},{10,14},{12,8},{14,10},{16,20},{18,... | collective-permute-start | bytes 4325384 | tf_op jit(solution)/shard_map/ppermute | solution.py:53
  601.8 61.8 %collective-permute-start.35 = (bf16[512,1408]{1,0:T(8,128)(2,1)S(1)}, bf16[512,1408]{1,0:T(8,128)(2,1)S(1)}, u32[]{:S(2)}, u32[]{:S(2)}) collective-permute-start(bf16[512,1408]{1,0:T(8,128)(2,1)S(1)} %fusion.19), channel_id=1, source_target_pairs={{0,4},{2,6},{4,0},{6,2},{8,12},{10,14},{12,8},{14,10},{16,20},{18,... | collective-permute-start | bytes 4325384 | tf_op jit(solution)/shard_map/ppermute | solution.py:53
  606.5 61.8 %collective-permute-start.28 = (bf16[128,1024]{1,0:T(8,128)(2,1)S(1)}, bf16[128,1024]{1,0:T(8,128)(2,1)}, u32[]{:S(2)}, u32[]{:S(2)}) collective-permute-start(bf16[128,1024]{1,0:T(8,128)(2,1)S(1)} %add_convert_fusion.19), channel_id=1, source_target_pairs={{0,24},{2,26},{4,28},{6,30},{8,16},{10,18},{12,20},{14,22},{16,8},... | collective-permute-start | bytes 786440 | tf_op jit(solution)/shard_map/ppermute | solution.py:67
  614.0 56.7 %collective-permute-start.33 = (bf16[128,1024]{1,0:T(8,128)(2,1)S(1)}, bf16[128,1024]{1,0:T(8,128)(2,1)S(1)}, u32[]{:S(2)}, u32[]{:S(2)}) collective-permute-start(bf16[128,1024]{1,0:T(8,128)(2,1)S(1)} %add_convert_fusion.16), channel_id=1, source_target_pairs={{0,24},{2,26},{4,28},{6,30},{8,16},{10,18},{12,20},{14,22},{16,8},... | collective-permute-start | bytes 786440 | tf_op jit(solution)/shard_map/ppermute | solution.py:67
  617.9 53.4 %collective-permute-start.32 = (bf16[128,1024]{1,0:T(8,128)(2,1)S(1)}, bf16[128,1024]{1,0:T(8,128)(2,1)S(1)}, u32[]{:S(2)}, u32[]{:S(2)}) collective-permute-start(bf16[128,1024]{1,0:T(8,128)(2,1)S(1)} %add_convert_fusion.17), channel_id=1, source_target_pairs={{0,16},{2,18},{4,20},{6,22},{8,24},{10,26},{12,28},{14,30},{16,0},... | collective-permute-start | bytes 786440 | tf_op jit(solution)/shard_map/ppermute | solution.py:67
  632.7 132.2 %collective-permute-start.59 = (bf16[512,2816]{1,0:T(8,128)(2,1)}, bf16[512,2816]{1,0:T(8,128)(2,1)}, u32[]{:S(2)}, u32[]{:S(2)}) collective-permute-start(bf16[512,2816]{1,0:T(8,128)(2,1)} %add_convert_fusion), channel_id=1, source_target_pairs={{0,4},{2,6},{4,0},{6,2},{8,12},{10,14},{12,8},{14,10},{16,20},{18,... | collective-permute-start | bytes 8650760 | tf_op jit(solution)/shard_map/ppermute | solution.py:53
  663.6 9.0 collective-permute-start.31
  668.2 16.3 %collective-permute-start.27 = (bf16[128,1024]{1,0:T(8,128)(2,1)}, bf16[128,1024]{1,0:T(8,128)(2,1)}, u32[]{:S(2)}, u32[]{:S(2)}) collective-permute-start(bf16[128,1024]{1,0:T(8,128)(2,1)} %add_convert_fusion.20), channel_id=1, source_target_pairs={{0,16},{2,18},{4,20},{6,22},{8,24},{10,26},{12,28},{14,30},{16,0},... | collective-permute-start | bytes 786440 | tf_op jit(solution)/shard_map/ppermute | solution.py:67
  670.7 13.8 %collective-permute-start.26 = (bf16[128,1024]{1,0:T(8,128)(2,1)}, bf16[128,1024]{1,0:T(8,128)(2,1)}, u32[]{:S(2)}, u32[]{:S(2)}) collective-permute-start(bf16[128,1024]{1,0:T(8,128)(2,1)} %add_convert_fusion.21), channel_id=1, source_target_pairs={{0,8},{2,10},{4,12},{6,14},{8,0},{10,2},{12,4},{14,6},{16,24},{18,... | collective-permute-start | bytes 786440 | tf_op jit(solution)/shard_map/ppermute | solution.py:67
  671.3 19.2 %collective-permute-start.23 = (bf16[128,1024]{1,0:T(8,128)(2,1)}, bf16[128,1024]{1,0:T(8,128)(2,1)}, u32[]{:S(2)}, u32[]{:S(2)}) collective-permute-start(bf16[128,1024]{1,0:T(8,128)(2,1)} %add_convert_fusion.22), channel_id=1, source_target_pairs={{0,24},{2,26},{4,28},{6,30},{8,16},{10,18},{12,20},{14,22},{16,8},... | collective-permute-start | bytes 786440 | tf_op jit(solution)/shard_map/ppermute | solution.py:67
  672.6 74.5 %collective-permute-start.54 = (bf16[384,1408]{1,0:T(8,128)(2,1)}, bf16[384,1408]{1,0:T(8,128)(2,1)}, u32[]{:S(2)}, u32[]{:S(2)}) collective-permute-start(bf16[384,1408]{1,0:T(8,128)(2,1)} %fusion.26), channel_id=1, source_target_pairs={{0,8},{2,10},{4,12},{6,14},{24,16},{26,18},{28,20},{30,22},{1,9},{... | collective-permute-start | bytes 3244040 | tf_op jit(solution)/shard_map/ppermute | solution.py:67
  684.5 33.3 %collective-permute-start.22 = (bf16[128,1024]{1,0:T(8,128)(2,1)}, bf16[128,1024]{1,0:T(8,128)(2,1)S(1)}, u32[]{:S(2)}, u32[]{:S(2)}) collective-permute-start(bf16[128,1024]{1,0:T(8,128)(2,1)} %add_convert_fusion.23), channel_id=1, source_target_pairs={{0,16},{2,18},{4,20},{6,22},{8,24},{10,26},{12,28},{14,30},{16,0},... | collective-permute-start | bytes 786440 | tf_op jit(solution)/shard_map/ppermute | solution.py:67
  684.5 38.9 %collective-permute-start.21 = (bf16[128,1024]{1,0:T(8,128)(2,1)}, bf16[128,1024]{1,0:T(8,128)(2,1)S(1)}, u32[]{:S(2)}, u32[]{:S(2)}) collective-permute-start(bf16[128,1024]{1,0:T(8,128)(2,1)} %add_convert_fusion.24), channel_id=1, source_target_pairs={{0,8},{2,10},{4,12},{6,14},{8,0},{10,2},{12,4},{14,6},{16,24},{18,... | collective-permute-start | bytes 786440 | tf_op jit(solution)/shard_map/ppermute | solution.py:67
  690.4 40.0 %collective-permute-start.18 = (bf16[128,1024]{1,0:T(8,128)(2,1)}, bf16[128,1024]{1,0:T(8,128)(2,1)S(1)}, u32[]{:S(2)}, u32[]{:S(2)}) collective-permute-start(bf16[128,1024]{1,0:T(8,128)(2,1)} %add_convert_fusion.25), channel_id=1, source_target_pairs={{0,24},{2,26},{4,28},{6,30},{8,16},{10,18},{12,20},{14,22},{16,8},... | collective-permute-start | bytes 786440 | tf_op jit(solution)/shard_map/ppermute | solution.py:67
  717.8 18.9 %collective-permute-start.17 = (bf16[128,1024]{1,0:T(8,128)(2,1)}, bf16[128,1024]{1,0:T(8,128)(2,1)S(1)}, u32[]{:S(2)}, u32[]{:S(2)}) collective-permute-start(bf16[128,1024]{1,0:T(8,128)(2,1)} %add_convert_fusion.26), channel_id=1, source_target_pairs={{0,16},{2,18},{4,20},{6,22},{8,24},{10,26},{12,28},{14,30},{16,0},... | collective-permute-start | bytes 786440 | tf_op jit(solution)/shard_map/ppermute | solution.py:67
  723.4 16.9 %collective-permute-start.16 = (bf16[128,1024]{1,0:T(8,128)(2,1)}, bf16[128,1024]{1,0:T(8,128)(2,1)S(1)}, u32[]{:S(2)}, u32[]{:S(2)}) collective-permute-start(bf16[128,1024]{1,0:T(8,128)(2,1)} %add_convert_fusion.27), channel_id=1, source_target_pairs={{0,8},{2,10},{4,12},{6,14},{8,0},{10,2},{12,4},{14,6},{16,24},{18,... | collective-permute-start | bytes 786440 | tf_op jit(solution)/shard_map/ppermute | solution.py:67
  730.4 33.0 %collective-permute-start.48 = (bf16[384,1408]{1,0:T(8,128)(2,1)}, bf16[384,1408]{1,0:T(8,128)(2,1)S(1)}, u32[]{:S(2)}, u32[]{:S(2)}) collective-permute-start(bf16[384,1408]{1,0:T(8,128)(2,1)} %copy-done.47), channel_id=1, source_target_pairs={{0,8},{2,10},{4,12},{6,14},{24,16},{26,18},{28,20},{30,22},{1,9},{... | collective-permute-start | bytes 3244040 | tf_op jit(solution)/shard_map/ppermute | solution.py:67
  736.7 49.8 %collective-permute-start.42 = (bf16[384,1408]{1,0:T(8,128)(2,1)S(1)}, bf16[384,1408]{1,0:T(8,128)(2,1)S(1)}, u32[]{:S(2)}, u32[]{:S(2)}) collective-permute-start(bf16[384,1408]{1,0:T(8,128)(2,1)S(1)} %copy-done.46), channel_id=1, source_target_pairs={{0,8},{2,10},{4,12},{6,14},{24,16},{26,18},{28,20},{30,22},{1,9},{... | collective-permute-start | bytes 3244040 | tf_op jit(solution)/shard_map/ppermute | solution.py:67
  740.3 69.4 %collective-permute-start.36 = (bf16[384,1408]{1,0:T(8,128)(2,1)S(1)}, bf16[384,1408]{1,0:T(8,128)(2,1)S(1)}, u32[]{:S(2)}, u32[]{:S(2)}) collective-permute-start(bf16[384,1408]{1,0:T(8,128)(2,1)S(1)} %copy-done.44), channel_id=1, source_target_pairs={{0,8},{2,10},{4,12},{6,14},{24,16},{26,18},{28,20},{30,22},{1,9},{... | collective-permute-start | bytes 3244040 | tf_op jit(solution)/shard_map/ppermute | solution.py:67
  747.2 22.5 %collective-permute-start.55 = (bf16[128,1408]{1,0:T(8,128)(2,1)S(1)}, bf16[128,1408]{1,0:T(8,128)(2,1)S(1)}, u32[]{:S(2)}, u32[]{:S(2)}) collective-permute-start(bf16[128,1408]{1,0:T(8,128)(2,1)S(1)} %copy-done.55), channel_id=1, source_target_pairs={{8,0},{10,2},{12,4},{14,6},{16,24},{18,26},{20,28},{22,30},{9,1},{... | collective-permute-start | bytes 1081352 | tf_op jit(solution)/shard_map/ppermute | solution.py:67
  763.5 27.8 %collective-permute-start.49 = (bf16[128,1408]{1,0:T(8,128)(2,1)S(1)}, bf16[128,1408]{1,0:T(8,128)(2,1)S(1)}, u32[]{:S(2)}, u32[]{:S(2)}) collective-permute-start(bf16[128,1408]{1,0:T(8,128)(2,1)S(1)} %copy-done.54), channel_id=1, source_target_pairs={{8,0},{10,2},{12,4},{14,6},{16,24},{18,26},{20,28},{22,30},{9,1},{... | collective-permute-start | bytes 1081352 | tf_op jit(solution)/shard_map/ppermute | solution.py:67
  765.0 27.5 %collective-permute-start.43 = (bf16[128,1408]{1,0:T(8,128)(2,1)S(1)}, bf16[128,1408]{1,0:T(8,128)(2,1)S(1)}, u32[]{:S(2)}, u32[]{:S(2)}) collective-permute-start(bf16[128,1408]{1,0:T(8,128)(2,1)S(1)} %copy-done.56), channel_id=1, source_target_pairs={{8,0},{10,2},{12,4},{14,6},{16,24},{18,26},{20,28},{22,30},{9,1},{... | collective-permute-start | bytes 1081352 | tf_op jit(solution)/shard_map/ppermute | solution.py:67
  769.7 41.2 %collective-permute-start.57 = (bf16[128,1408]{1,0:T(8,128)(2,1)S(1)}, bf16[128,1408]{1,0:T(8,128)(2,1)S(1)}, u32[]{:S(2)}, u32[]{:S(2)}) collective-permute-start(bf16[128,1408]{1,0:T(8,128)(2,1)S(1)} %get-tuple-element.77), channel_id=1, source_target_pairs={{8,16},{10,18},{12,20},{14,22},{16,8},{18,10},{20,12},{22,14},{9,1... | collective-permute-start | bytes 1081352 | tf_op jit(solution)/shard_map/ppermute | solution.py:67
  786.5 67.5 %collective-permute-start.60 = (bf16[384,2816]{1,0:T(8,128)(2,1)S(1)}, bf16[384,2816]{1,0:T(8,128)(2,1)S(1)}, u32[]{:S(2)}, u32[]{:S(2)}) collective-permute-start(bf16[384,2816]{1,0:T(8,128)(2,1)S(1)} %fusion.7), channel_id=1, source_target_pairs={{0,8},{2,10},{4,12},{6,14},{24,16},{26,18},{28,20},{30,22},{1,9},{... | collective-permute-start | bytes 6488072 | tf_op jit(solution)/shard_map/ppermute | solution.py:67
  791.2 20.7 %collective-permute-start.56 = (bf16[128,1408]{1,0:T(8,128)(2,1)S(1)}, bf16[128,1408]{1,0:T(8,128)(2,1)S(1)}, u32[]{:S(2)}, u32[]{:S(2)}) collective-permute-start(bf16[128,1408]{1,0:T(8,128)(2,1)S(1)} %get-tuple-element.76), channel_id=1, source_target_pairs={{8,24},{10,26},{12,28},{14,30},{16,0},{18,2},{20,4},{22,6},{9,25},... | collective-permute-start | bytes 1081352 | tf_op jit(solution)/shard_map/ppermute | solution.py:67
  792.5 22.5 %collective-permute-start.51 = (bf16[128,1408]{1,0:T(8,128)(2,1)S(1)}, bf16[128,1408]{1,0:T(8,128)(2,1)S(1)}, u32[]{:S(2)}, u32[]{:S(2)}) collective-permute-start(bf16[128,1408]{1,0:T(8,128)(2,1)S(1)} %get-tuple-element.75), channel_id=1, source_target_pairs={{8,16},{10,18},{12,20},{14,22},{16,8},{18,10},{20,12},{22,14},{9,1... | collective-permute-start | bytes 1081352 | tf_op jit(solution)/shard_map/ppermute | solution.py:67
  809.7 14.2 %collective-permute-start.50 = (bf16[128,1408]{1,0:T(8,128)(2,1)S(1)}, bf16[128,1408]{1,0:T(8,128)(2,1)S(1)}, u32[]{:S(2)}, u32[]{:S(2)}) collective-permute-start(bf16[128,1408]{1,0:T(8,128)(2,1)S(1)} %get-tuple-element.74), channel_id=1, source_target_pairs={{8,24},{10,26},{12,28},{14,30},{16,0},{18,2},{20,4},{22,6},{9,25},... | collective-permute-start | bytes 1081352 | tf_op jit(solution)/shard_map/ppermute | solution.py:67
  811.0 13.6 %collective-permute-start.45 = (bf16[128,1408]{1,0:T(8,128)(2,1)S(1)}, bf16[128,1408]{1,0:T(8,128)(2,1)S(1)}, u32[]{:S(2)}, u32[]{:S(2)}) collective-permute-start(bf16[128,1408]{1,0:T(8,128)(2,1)S(1)} %get-tuple-element.73), channel_id=1, source_target_pairs={{8,16},{10,18},{12,20},{14,22},{16,8},{18,10},{20,12},{22,14},{9,1... | collective-permute-start | bytes 1081352 | tf_op jit(solution)/shard_map/ppermute | solution.py:67
  811.9 27.3 %collective-permute-start.44 = (bf16[128,1408]{1,0:T(8,128)(2,1)S(1)}, bf16[128,1408]{1,0:T(8,128)(2,1)S(1)}, u32[]{:S(2)}, u32[]{:S(2)}) collective-permute-start(bf16[128,1408]{1,0:T(8,128)(2,1)S(1)} %get-tuple-element.72), channel_id=1, source_target_pairs={{8,24},{10,26},{12,28},{14,30},{16,0},{18,2},{20,4},{22,6},{9,25},... | collective-permute-start | bytes 1081352 | tf_op jit(solution)/shard_map/ppermute | solution.py:67
  815.1 25.8 %collective-permute-start.37 = (bf16[128,1408]{1,0:T(8,128)(2,1)S(1)}, bf16[128,1408]{1,0:T(8,128)(2,1)S(1)}, u32[]{:S(2)}, u32[]{:S(2)}) collective-permute-start(bf16[128,1408]{1,0:T(8,128)(2,1)S(1)} %copy-done.53), channel_id=1, source_target_pairs={{8,0},{10,2},{12,4},{14,6},{16,24},{18,26},{20,28},{22,30},{9,1},{... | collective-permute-start | bytes 1081352 | tf_op jit(solution)/shard_map/ppermute | solution.py:67
  823.9 17.0 %collective-permute-start.39 = (bf16[128,1408]{1,0:T(8,128)(2,1)S(1)}, bf16[128,1408]{1,0:T(8,128)(2,1)S(1)}, u32[]{:S(2)}, u32[]{:S(2)}) collective-permute-start(bf16[128,1408]{1,0:T(8,128)(2,1)S(1)} %get-tuple-element.71), channel_id=1, source_target_pairs={{8,16},{10,18},{12,20},{14,22},{16,8},{18,10},{20,12},{22,14},{9,1... | collective-permute-start | bytes 1081352 | tf_op jit(solution)/shard_map/ppermute | solution.py:67
  824.6 25.7 %collective-permute-start.38 = (bf16[128,1408]{1,0:T(8,128)(2,1)S(1)}, bf16[128,1408]{1,0:T(8,128)(2,1)S(1)}, u32[]{:S(2)}, u32[]{:S(2)}) collective-permute-start(bf16[128,1408]{1,0:T(8,128)(2,1)S(1)} %get-tuple-element.70), channel_id=1, source_target_pairs={{8,24},{10,26},{12,28},{14,30},{16,0},{18,2},{20,4},{22,6},{9,25},... | collective-permute-start | bytes 1081352 | tf_op jit(solution)/shard_map/ppermute | solution.py:67
  852.0 15.3 %collective-permute-start.61 = (bf16[128,2816]{1,0:T(8,128)(2,1)S(1)}, bf16[128,2816]{1,0:T(8,128)(2,1)S(1)}, u32[]{:S(2)}, u32[]{:S(2)}) collective-permute-start(bf16[128,2816]{1,0:T(8,128)(2,1)S(1)} %slice.900), channel_id=1, source_target_pairs={{8,0},{10,2},{12,4},{14,6},{16,24},{18,26},{20,28},{22,30},{9,1},{... | collective-permute-start | bytes 2162696 | tf_op jit(solution)/shard_map/ppermute | solution.py:67
  854.4 13.0 %collective-permute-start.63 = (bf16[128,2816]{1,0:T(8,128)(2,1)S(1)}, bf16[128,2816]{1,0:T(8,128)(2,1)S(1)}, u32[]{:S(2)}, u32[]{:S(2)}) collective-permute-start(bf16[128,2816]{1,0:T(8,128)(2,1)S(1)} %get-tuple-element.69), channel_id=1, source_target_pairs={{8,16},{10,18},{12,20},{14,22},{16,8},{18,10},{20,12},{22,14},{9,1... | collective-permute-start | bytes 2162696 | tf_op jit(solution)/shard_map/ppermute | solution.py:67
  855.1 34.7 %collective-permute-start.62 = (bf16[128,2816]{1,0:T(8,128)(2,1)S(1)}, bf16[128,2816]{1,0:T(8,128)(2,1)S(1)}, u32[]{:S(2)}, u32[]{:S(2)}) collective-permute-start(bf16[128,2816]{1,0:T(8,128)(2,1)S(1)} %get-tuple-element.68), channel_id=1, source_target_pairs={{8,24},{10,26},{12,28},{14,30},{16,0},{18,2},{20,4},{22,6},{9,25},... | collective-permute-start | bytes 2162696 | tf_op jit(solution)/shard_map/ppermute | solution.py:67
  (94 other events, 1147.9 us)
Sparse Core Ops, SparseCore 0:
  12.8 94.1 all-gather.5
  109.2 180.7 all-gather.3

commit v5 on v4

--- a/solution.py
+++ b/solution.py
@@ -108,32 +108,12 @@
     )(order, rows)
 
 
-def scatter_product(grid, left, right, relay=False):
-    block = left.shape[0] // grid.count
-    per_mid = block * grid.slow
-    per_core = per_mid * grid.mid
-    from_core = []
-    for c in range(1, grid.cores):
-        out = times(left[c * per_core : (c + 1) * per_core], right).astype(BF16)
-        from_core.append(grid.shift(out, core=c))
-    from_mid = []
-    for m in range(1, grid.mid):
-        part = times(left[m * per_mid : (m + 1) * per_mid], right)
-        for got in from_core:
-            part = part + got[m * per_mid : (m + 1) * per_mid].astype(F32)
-        part = part.astype(BF16)
-        from_mid.append(grid.shift(part, mid=m))
-
-    def part_of(span):
-        part = times(left[span], right)
-        for got in from_core + from_mid:
-            part = part + got[span].astype(F32)
-        return part
-
-    total = part_of(slice(0, block))
+def slow_stage(grid, part_of, base, block, relay):
+    span = lambda first, last: slice(base + first * block, base + last * block)
+    total = part_of(span(0, 1))
     from_slow = []
     if relay and grid.slow == 4:
-        mine = part_of(slice(block, 4 * block)).astype(BF16)
+        mine = part_of(span(1, 4)).astype(BF16)
         got = grid.cross(mine, 1, inner=False)
         near, far, over = (slice(i * block, (i + 1) * block) for i in range(3))
         from_slow.append(got[near])
@@ -145,11 +125,44 @@
         from_slow += [grid.cross(rows, s, ends=False) for s, rows in sums.items()]
     else:
         for s in range(1, grid.slow):
-            part = part_of(slice(s * block, (s + 1) * block)).astype(BF16)
+            part = part_of(span(s, s + 1)).astype(BF16)
             from_slow.append(grid.cross(part, s))
     for got in from_slow:
         total = total + got.astype(F32)
     return total
+
+
+def scatter_product(grid, left, right, relay=False, slow_first=False):
+    block = left.shape[0] // grid.count
+    per_mid = block * grid.slow
+    per_core = per_mid * grid.mid
+    from_core = []
+    for c in range(1, grid.cores):
+        out = times(left[c * per_core : (c + 1) * per_core], right).astype(BF16)
+        from_core.append(grid.shift(out, core=c))
+
+    def part_of(span, also=()):
+        part = times(left[span], right)
+        for got in (*from_core, *also):
+            part = part + got[span].astype(F32)
+        return part
+
+    if slow_first:
+        totals = {
+            m: slow_stage(grid, part_of, m * per_mid, block, relay)
+            for m in reversed(range(grid.mid))
+        }
+        total = totals[0]
+        for m in range(1, grid.mid):
+            part = totals[m].astype(BF16)
+            got = grid.shift(part, mid=m)
+            total = total + got.astype(F32)
+        return total
+    from_mid = []
+    for m in range(1, grid.mid):
+        part = part_of(slice(m * per_mid, (m + 1) * per_mid)).astype(BF16)
+        from_mid.append(grid.shift(part, mid=m))
+    return slow_stage(grid, lambda span: part_of(span, from_mid), 0, block, relay)
 
 
 def scatter_rows(grid, rows):
@@ -319,7 +332,7 @@
     hidden = (gate * sigma * upper).astype(BF16)
     gate, upper, hidden = lax.optimization_barrier((gate, upper, hidden))
     sigma = jax.nn.sigmoid(gate)
-    down_grad = scatter_product(grid, down_cot_t, hidden, relay=True)
+    down_grad = scatter_product(grid, down_cot_t, hidden, relay=True, slow_first=True)
 
     grad_three = cotangent.astype(F32)
     grad_hidden = times(down_cot, w_down_t)

time: 908 us -> 971 us (1.069)
  waiting for transfers between devices: 530 us -> 568 us
  starting transfers between devices: 81.5 us -> 93.4 us
  local copies, waits for them, and re-layouts: 63.2 us -> 74.1 us
    ppermute x35 -> x39, waiting for transfers between devices: 152 us -> 189 us  [cross(): return lax.ppermute(rows, 'fsdp', moves)]
    ppermute x35 -> x39, starting transfers between devices: 56.7 us -> 68.7 us  [cross(): return lax.ppermute(rows, 'fsdp', moves)]
    dot_general x51 -> x52, matrix products: 123 us -> 119 us  [times(): lax.dot_general(left, right, (((1,), (0,)), ((), ())), preferred_element_...]
    unnamed x199 -> x235, local copies, waits for them, and re-layouts: 32 us -> 32.6 us
  transfers between devices with their start and end apart: 66 -> 70, of which waited for: 34 -> 33; matrix products, arithmetic and copies ran while one was open for 22% -> 22% of each run, Pallas kernels for 2% -> 2%
where the time goes in v5:
time: 971 us; the launch traced here: 963 us
  waiting for transfers between devices  568 us (58%)
  matrix products  156 us (16%)
  starting transfers between devices  93.4 us (10%)
  local copies, waits for them, and re-layouts  74.1 us (8%)
  other arithmetic  39.5 us (4%)
  between operations  16.4 us (2%)
  Pallas kernels  16.3 us (2%)
    ppermute x39, waiting for transfers between devices, cross(): return lax.ppermute(rows, 'fsdp', moves)  189 us
    ppermute x20, waiting for transfers between devices, shift(): return lax.ppermute(rows, 'fsdp', self.moves(**by))  169 us
    dot_general x52, matrix products, times(): lax.dot_general(left, right, (((1,), (0,)), ((), ())), preferred_element_...  119 us
    all_gather x1, waiting for transfers between devices, shards(): mlp_all = lax.all_gather(mlp_pack, 'fsdp', axis=1, tiled=True)  108 us
    ppermute x39, starting transfers between devices, cross(): return lax.ppermute(rows, 'fsdp', moves)  68.7 us
    all_gather x1, waiting for transfers between devices, shards(): packs = lax.all_gather(pack, 'fsdp', axis=0)  65.5 us
    ppermute x9, waiting for transfers between devices, other(): return lax.ppermute(rows, 'tp', [(0, 1), (1, 0)])  36.5 us
    unnamed x235, local copies, waits for them, and re-layouts  32.6 us
  transfers between devices with their start and end apart: 70, of which 33 were waited for; matrix products, arithmetic and copies ran while one was open for 22% of the time, Pallas kernels for 2%

profile of v5, /device:TPU:0, one launch (start us, length us, event | category | flops | bytes accessed | tf_op | source)
XLA Modules:
  0.0 963.2 jit_solution(2835802986648521316)
XLA Ops:
  12.8 2.9 fusion.237
  15.7 3.8 copy.96
  21.4 2.9 pad_maximum_fusion
  25.3 2.8 collective-permute-start
  30.3 10.6 %collective-permute-done = bf16[128,2048]{1,0:T(8,128)(2,1)S(1)} collective-permute-done((bf16[128,2048]{1,0:T(8,128)(2,1)S(1)}, bf16[128,2048]{1,0:T(8,128)(2,1)S(1)}, u32[]{:S(2)}, u32[]{:S(2)}) %collective-permute-start) | collective-permute-done | bytes 524320 | tf_op jit(solution)/shard_map/ppermute | solution.py:183
  41.6 65.5 %all-gather.6.cloned.1.call-done = bf16[8448,1024]{1,0:T(8,128)(2,1)} async-done(((bf16[528,1024]{1,0:T(8,128)(2,1)}), bf16[8448,1024]{1,0:T(8,128)(2,1)}) %all-gather.6.cloned.1.call-update) | async-done | bytes 17301520 | tf_op jit(solution)/shard_map/all_gather | solution.py:288
  110.1 11.8 %fusion.236 = (bf16[16,128,1024]{2,1,0:T(8,128)(2,1)}, bf16[16,128,1024]{2,1,0:T(8,128)(2,1)}, bf16[16,128,1024]{2,1,0:T(8,128)(2,1)}, bf16[16,128,1024]{2,1,0:T(8,128)(2,1)S(1)}) fusion(bf16[16,528,1024]{2,1,0:T(8,128)(2,1)} %bitcast.215), kind=kLoop, calls=%fused_computation.405 | loop fusion | bytes 33554432 | tf_op jit(solution)/shard_map/slice | solution.py:293
  126.4 4.4 convolution_add_fusion.18
  132.7 4.4 convolution_add_fusion.19
  149.3 10.8 %collective-permute-done.1 = bf16[128,2048]{1,0:T(8,128)(2,1)S(1)} collective-permute-done((bf16[128,2048]{1,0:T(8,128)(2,1)S(1)}, bf16[128,2048]{1,0:T(8,128)(2,1)S(1)}, u32[]{:S(2)}, u32[]{:S(2)}) %collective-permute-start.1) | collective-permute-done | bytes 524320 | tf_op jit(solution)/shard_map/ppermute | solution.py:183
  165.9 4.0 shard_map.172
  169.9 4.1 shard_map.169
  177.6 4.1 shard_map.171
  181.7 108.2 %all-gather.4.cloned.1.call-done = bf16[3,2048,2816]{1,2,0:T(8,128)(2,1)} async-done(((bf16[3,128,2816]{1,2,0:T(8,128)(2,1)}), bf16[3,2048,2816]{1,2,0:T(8,128)(2,1)}) %all-gather.4.cloned.1.call-update) | async-done | bytes 34603024 | tf_op jit(solution)/shard_map/all_gather | solution.py:290
  290.0 6.6 fusion.3
  296.5 7.3 multiply_convert_fusion.3
  303.9 7.2 multiply_convert_fusion.1
  311.1 7.1 fusion.2
  318.3 6.2 fusion.33
  326.1 2.6 convolution_convert_fusion.1
  328.7 2.6 convolution_convert_fusion.2
  331.2 2.8 convolution_convert_fusion.3
  334.0 4.7 collective-permute-done.4
  339.8 2.6 fusion.234
  343.8 2.5 convolution_convert_fusion.4
  346.8 4.1 convolution_convert_fusion
  351.0 4.6 collective-permute-done.5
  362.0 4.1 multiply_convert_fusion
  375.8 2.7 fusion.244
  380.5 4.1 shard_map.170
  384.6 6.1 fusion
  407.2 3.3 convolution_convert_fusion.5
  410.5 5.0 collective-permute-done.7
  437.7 3.4 collective-permute-done.13
  441.7 3.0 collective-permute-done.11
  444.7 2.7 fusion.70
  470.0 16.2 %collective-permute-done.25 = bf16[512,1024]{1,0:T(8,128)(2,1)S(1)} collective-permute-done((bf16[512,1024]{1,0:T(8,128)(2,1)S(1)}, bf16[512,1024]{1,0:T(8,128)(2,1)S(1)}, u32[]{:S(2)}, u32[]{:S(2)}) %collective-permute-start.25) | collective-permute-done | bytes 1048608 | tf_op jit(solution)/shard_map/ppermute | solution.py:53
  492.6 77.9 %collective-permute-done.20 = bf16[512,1024]{1,0:T(8,128)(2,1)S(1)} collective-permute-done((bf16[512,1024]{1,0:T(8,128)(2,1)S(1)}, bf16[512,1024]{1,0:T(8,128)(2,1)S(1)}, u32[]{:S(2)}, u32[]{:S(2)}) %collective-permute-start.20) | collective-permute-done | bytes 1048608 | tf_op jit(solution)/shard_map/ppermute | solution.py:53
  577.4 15.5 %collective-permute-done.15 = bf16[512,1024]{1,0:T(8,128)(2,1)S(1)} collective-permute-done((bf16[512,1024]{1,0:T(8,128)(2,1)S(1)}, bf16[512,1024]{1,0:T(8,128)(2,1)S(1)}, u32[]{:S(2)}, u32[]{:S(2)}) %collective-permute-start.15) | collective-permute-done | bytes 1048608 | tf_op jit(solution)/shard_map/ppermute | solution.py:53
  597.1 18.3 %collective-permute-done.30 = bf16[512,1024]{1,0:T(8,128)(2,1)S(1)} collective-permute-done((bf16[512,1024]{1,0:T(8,128)(2,1)S(1)}, bf16[512,1024]{1,0:T(8,128)(2,1)S(1)}, u32[]{:S(2)}, u32[]{:S(2)}) %collective-permute-start.30) | collective-permute-done | bytes 1048608 | tf_op jit(solution)/shard_map/ppermute | solution.py:53
  619.9 3.0 collective-permute-start.28
  622.9 2.8 fusion.31
  631.1 15.2 %collective-permute-done.41 = bf16[512,1408]{1,0:T(8,128)(2,1)S(1)} collective-permute-done((bf16[512,1408]{1,0:T(8,128)(2,1)S(1)}, bf16[512,1408]{1,0:T(8,128)(2,1)S(1)}, u32[]{:S(2)}, u32[]{:S(2)}) %collective-permute-start.41) | collective-permute-done | bytes 1441824 | tf_op jit(solution)/shard_map/ppermute | solution.py:53
  651.3 25.4 %collective-permute-done.35 = bf16[512,1408]{1,0:T(8,128)(2,1)S(1)} collective-permute-done((bf16[512,1408]{1,0:T(8,128)(2,1)S(1)}, bf16[512,1408]{1,0:T(8,128)(2,1)S(1)}, u32[]{:S(2)}, u32[]{:S(2)}) %collective-permute-start.35) | collective-permute-done | bytes 1441824 | tf_op jit(solution)/shard_map/ppermute | solution.py:53
  679.9 2.9 collective-permute-start.27
  684.4 3.9 collective-permute-done.31
  696.0 4.5 collective-permute-start.21
  700.4 3.4 collective-permute-done.23
  706.9 23.0 %collective-permute-done.22 = bf16[128,1024]{1,0:T(8,128)(2,1)S(1)} collective-permute-done((bf16[128,1024]{1,0:T(8,128)(2,1)}, bf16[128,1024]{1,0:T(8,128)(2,1)S(1)}, u32[]{:S(2)}, u32[]{:S(2)}) %collective-permute-start.22) | collective-permute-done | bytes 262176 | tf_op jit(solution)/shard_map/ppermute | solution.py:67
  729.9 3.3 collective-permute-start.17
  737.9 5.9 collective-permute-done.18
  748.7 3.2 collective-permute-start.42
  752.5 4.3 collective-permute-start.36
  762.3 13.3 %collective-permute-done.48 = bf16[384,1408]{1,0:T(8,128)(2,1)S(1)} collective-permute-done((bf16[384,1408]{1,0:T(8,128)(2,1)}, bf16[384,1408]{1,0:T(8,128)(2,1)S(1)}, u32[]{:S(2)}, u32[]{:S(2)}) %collective-permute-start.48) | collective-permute-done | bytes 1081376 | tf_op jit(solution)/shard_map/ppermute | solution.py:67
  777.1 21.6 %collective-permute-done.42 = bf16[384,1408]{1,0:T(8,128)(2,1)S(1)} collective-permute-done((bf16[384,1408]{1,0:T(8,128)(2,1)S(1)}, bf16[384,1408]{1,0:T(8,128)(2,1)S(1)}, u32[]{:S(2)}, u32[]{:S(2)}) %collective-permute-start.42) | collective-permute-done | bytes 1081376 | tf_op jit(solution)/shard_map/ppermute | solution.py:67
  804.6 15.9 %collective-permute-done.36 = bf16[384,1408]{1,0:T(8,128)(2,1)S(1)} collective-permute-done((bf16[384,1408]{1,0:T(8,128)(2,1)S(1)}, bf16[384,1408]{1,0:T(8,128)(2,1)S(1)}, u32[]{:S(2)}, u32[]{:S(2)}) %collective-permute-start.36) | collective-permute-done | bytes 1081376 | tf_op jit(solution)/shard_map/ppermute | solution.py:67
  820.5 4.5 collective-permute-start.63
  831.8 7.9 collective-permute-start.59
  841.4 3.4 collective-permute-done.50
  846.8 13.5 %collective-permute-done.44 = bf16[128,1408]{1,0:T(8,128)(2,1)S(1)} collective-permute-done((bf16[128,1408]{1,0:T(8,128)(2,1)S(1)}, bf16[128,1408]{1,0:T(8,128)(2,1)S(1)}, u32[]{:S(2)}, u32[]{:S(2)}) %collective-permute-start.44) | collective-permute-done | bytes 360480 | tf_op jit(solution)/shard_map/ppermute | solution.py:67
  865.0 8.7 collective-permute-done.38
  880.4 35.9 %collective-permute-done.59 = bf16[384,2816]{1,0:T(8,128)(2,1)S(1)} collective-permute-done((bf16[384,2816]{1,0:T(8,128)(2,1)S(1)}, bf16[384,2816]{1,0:T(8,128)(2,1)S(1)}, u32[]{:S(2)}, u32[]{:S(2)}) %collective-permute-start.59) | collective-permute-done | bytes 2162720 | tf_op jit(solution)/shard_map/ppermute | solution.py:67
  922.0 3.8 copy.88
  925.8 26.6 %collective-permute-done.61 = bf16[128,2816]{1,0:T(8,128)(2,1)S(1)} collective-permute-done((bf16[128,2816]{1,0:T(8,128)(2,1)S(1)}, bf16[128,2816]{1,0:T(8,128)(2,1)S(1)}, u32[]{:S(2)}, u32[]{:S(2)}) %collective-permute-start.61) | collective-permute-done | bytes 720928 | tf_op jit(solution)/shard_map/ppermute | solution.py:67
  (499 shorter events, 227.3 us)
Async XLA Ops:
  7.2 99.9 %all-gather.6.cloned.1.call-start = ((), (), s32[]{:S(2)}) async-start(), calls=%async_computation.1 | async-start | bytes 18382848 | tf_op jit(solution)/shard_map/all_gather | solution.py:288
  12.7 277.2 %all-gather.4.cloned.1.call-start = ((), (), s32[]{:S(2)}) async-start(), calls=%async_computation | async-start | bytes 36765696 | tf_op jit(solution)/shard_map/all_gather | solution.py:290
  25.3 15.6 %collective-permute-start = (bf16[128,2048]{1,0:T(8,128)(2,1)S(1)}, bf16[128,2048]{1,0:T(8,128)(2,1)S(1)}, u32[]{:S(2)}, u32[]{:S(2)}) collective-permute-start(bf16[128,2048]{1,0:T(8,128)(2,1)S(1)} %copy-done), channel_id=1, source_target_pairs={{0,1},{1,0},{2,3},{3,2},{4,5},{5,4},{6,7},{7,6},{8,9},{9,8},{10,11... | collective-permute-start | bytes 1572872 | tf_op jit(solution)/shard_map/ppermute | solution.py:183
  28.1 135.7 %collective-permute-start.2 = (bf16[128,2048]{1,0:T(8,128)(2,1)}, bf16[128,2048]{1,0:T(8,128)(2,1)}, u32[]{:S(2)}, u32[]{:S(2)}) collective-permute-start(bf16[128,2048]{1,0:T(8,128)(2,1)} %param.12), channel_id=1, source_target_pairs={{0,1},{1,0},{2,3},{3,2},{4,5},{5,4},{6,7},{7,6},{8,9},{9,8},{10,11... | collective-permute-start | bytes 1572872 | tf_op jit(solution)/shard_map/ppermute | solution.py:183
  146.0 14.0 %collective-permute-start.1 = (bf16[128,2048]{1,0:T(8,128)(2,1)S(1)}, bf16[128,2048]{1,0:T(8,128)(2,1)S(1)}, u32[]{:S(2)}, u32[]{:S(2)}) collective-permute-start(bf16[128,2048]{1,0:T(8,128)(2,1)S(1)} %slice.1261), channel_id=1, source_target_pairs={{0,1},{1,0},{2,3},{3,2},{4,5},{5,4},{6,7},{7,6},{8,9},{9,8},{10,11... | collective-permute-start | bytes 1572872 | tf_op jit(solution)/shard_map/ppermute | solution.py:183
  161.8 13.5 %collective-permute-start.3 = (bf16[128,2048]{1,0:T(8,128)(2,1)}, bf16[128,2048]{1,0:T(8,128)(2,1)}, u32[]{:S(2)}, u32[]{:S(2)}) collective-permute-start(bf16[128,2048]{1,0:T(8,128)(2,1)} %add_convert_fusion.8), channel_id=1, source_target_pairs={{0,1},{1,0},{2,3},{3,2},{4,5},{5,4},{6,7},{7,6},{8,9},{9,8},{10,11... | collective-permute-start | bytes 1572872 | tf_op jit(solution)/shard_map/ppermute | solution.py:183
  324.6 14.1 %collective-permute-start.4 = (bf16[128,2048]{1,0:T(8,128)(2,1)S(1)}, bf16[128,2048]{1,0:T(8,128)(2,1)S(1)}, u32[]{:S(2)}, u32[]{:S(2)}) collective-permute-start(bf16[128,2048]{1,0:T(8,128)(2,1)S(1)} %slice.1260), channel_id=1, source_target_pairs={{0,1},{1,0},{2,3},{3,2},{4,5},{5,4},{6,7},{7,6},{8,9},{9,8},{10,11... | collective-permute-start | bytes 1572872 | tf_op jit(solution)/shard_map/ppermute | solution.py:183
  342.3 13.2 %collective-permute-start.5 = (bf16[128,2048]{1,0:T(8,128)(2,1)S(1)}, bf16[128,2048]{1,0:T(8,128)(2,1)S(1)}, u32[]{:S(2)}, u32[]{:S(2)}) collective-permute-start(bf16[128,2048]{1,0:T(8,128)(2,1)S(1)} %get-tuple-element.58), channel_id=1, source_target_pairs={{0,1},{1,0},{2,3},{3,2},{4,5},{5,4},{6,7},{7,6},{8,9},{9,8},{10,11... | collective-permute-start | bytes 1572872 | tf_op jit(solution)/shard_map/ppermute | solution.py:183
  346.3 101.1 %collective-permute-start.52 = (bf16[1024,1408]{1,0:T(8,128)(2,1)}, bf16[1024,1408]{1,0:T(8,128)(2,1)}, u32[]{:S(2)}, u32[]{:S(2)}) collective-permute-start(bf16[1024,1408]{1,0:T(8,128)(2,1)} %convolution_convert_fusion.1), channel_id=1, source_target_pairs={{0,2},{2,0},{4,6},{6,4},{8,10},{10,8},{12,14},{14,12},{16,18},{18,... | collective-permute-start | bytes 8650760 | tf_op jit(solution)/shard_map/ppermute | solution.py:53
  346.3 104.5 %collective-permute-start.46 = (bf16[1024,1408]{1,0:T(8,128)(2,1)}, bf16[1024,1408]{1,0:T(8,128)(2,1)}, u32[]{:S(2)}, u32[]{:S(2)}) collective-permute-start(bf16[1024,1408]{1,0:T(8,128)(2,1)} %convolution_convert_fusion.2), channel_id=1, source_target_pairs={{0,2},{2,0},{4,6},{6,4},{8,10},{10,8},{12,14},{14,12},{16,18},{18,... | collective-permute-start | bytes 8650760 | tf_op jit(solution)/shard_map/ppermute | solution.py:53
  346.8 104.5 %collective-permute-start.40 = (bf16[1024,1408]{1,0:T(8,128)(2,1)}, bf16[1024,1408]{1,0:T(8,128)(2,1)}, u32[]{:S(2)}, u32[]{:S(2)}) collective-permute-start(bf16[1024,1408]{1,0:T(8,128)(2,1)} %convolution_convert_fusion.3), channel_id=1, source_target_pairs={{0,2},{2,0},{4,6},{6,4},{8,10},{10,8},{12,14},{14,12},{16,18},{18,... | collective-permute-start | bytes 8650760 | tf_op jit(solution)/shard_map/ppermute | solution.py:53
  391.6 44.5 %collective-permute-start.6 = (bf16[128,2048]{1,0:T(8,128)(2,1)}, bf16[128,2048]{1,0:T(8,128)(2,1)}, u32[]{:S(2)}, u32[]{:S(2)}) collective-permute-start(bf16[128,2048]{1,0:T(8,128)(2,1)} %slice.1259), channel_id=1, source_target_pairs={{0,1},{1,0},{2,3},{3,2},{4,5},{5,4},{6,7},{7,6},{8,9},{9,8},{10,11... | collective-permute-start | bytes 1572872 | tf_op jit(solution)/shard_map/ppermute | solution.py:183
  401.0 14.5 %collective-permute-start.7 = (bf16[128,2048]{1,0:T(8,128)(2,1)}, bf16[128,2048]{1,0:T(8,128)(2,1)}, u32[]{:S(2)}, u32[]{:S(2)}) collective-permute-start(bf16[128,2048]{1,0:T(8,128)(2,1)} %slice.1258), channel_id=1, source_target_pairs={{0,1},{1,0},{2,3},{3,2},{4,5},{5,4},{6,7},{7,6},{8,9},{9,8},{10,11... | collective-permute-start | bytes 1572872 | tf_op jit(solution)/shard_map/ppermute | solution.py:183
  441.1 19.0 %collective-permute-start.34 = (bf16[1024,1408]{1,0:T(8,128)(2,1)}, bf16[1024,1408]{1,0:T(8,128)(2,1)}, u32[]{:S(2)}, u32[]{:S(2)}) collective-permute-start(bf16[1024,1408]{1,0:T(8,128)(2,1)} %convolution_convert_fusion.4), channel_id=1, source_target_pairs={{0,2},{2,0},{4,6},{6,4},{8,10},{10,8},{12,14},{14,12},{16,18},{18,... | collective-permute-start | bytes 8650760 | tf_op jit(solution)/shard_map/ppermute | solution.py:53
  444.7 13.6 %collective-permute-start.24 = (bf16[1024,1024]{1,0:T(8,128)(2,1)}, bf16[1024,1024]{1,0:T(8,128)(2,1)}, u32[]{:S(2)}, u32[]{:S(2)}) collective-permute-start(bf16[1024,1024]{1,0:T(8,128)(2,1)} %convolution_convert_fusion.6), channel_id=1, source_target_pairs={{0,2},{2,0},{4,6},{6,4},{8,10},{10,8},{12,14},{14,12},{16,18},{18,... | collective-permute-start | bytes 6291464 | tf_op jit(solution)/shard_map/ppermute | solution.py:53
  447.4 15.8 %collective-permute-start.19 = (bf16[1024,1024]{1,0:T(8,128)(2,1)}, bf16[1024,1024]{1,0:T(8,128)(2,1)}, u32[]{:S(2)}, u32[]{:S(2)}) collective-permute-start(bf16[1024,1024]{1,0:T(8,128)(2,1)} %convolution_convert_fusion.7), channel_id=1, source_target_pairs={{0,2},{2,0},{4,6},{6,4},{8,10},{10,8},{12,14},{14,12},{16,18},{18,... | collective-permute-start | bytes 6291464 | tf_op jit(solution)/shard_map/ppermute | solution.py:53
  450.8 15.2 %collective-permute-start.14 = (bf16[1024,1024]{1,0:T(8,128)(2,1)}, bf16[1024,1024]{1,0:T(8,128)(2,1)S(1)}, u32[]{:S(2)}, u32[]{:S(2)}) collective-permute-start(bf16[1024,1024]{1,0:T(8,128)(2,1)} %convolution_convert_fusion.8), channel_id=1, source_target_pairs={{0,2},{2,0},{4,6},{6,4},{8,10},{10,8},{12,14},{14,12},{16,18},{18,... | collective-permute-start | bytes 6291464 | tf_op jit(solution)/shard_map/ppermute | solution.py:53
  451.4 16.2 %collective-permute-start.29 = (bf16[1024,1024]{1,0:T(8,128)(2,1)}, bf16[1024,1024]{1,0:T(8,128)(2,1)S(1)}, u32[]{:S(2)}, u32[]{:S(2)}) collective-permute-start(bf16[1024,1024]{1,0:T(8,128)(2,1)} %convolution_convert_fusion.5), channel_id=1, source_target_pairs={{0,2},{2,0},{4,6},{6,4},{8,10},{10,8},{12,14},{14,12},{16,18},{18,... | collective-permute-start | bytes 6291464 | tf_op jit(solution)/shard_map/ppermute | solution.py:53
  458.3 341.9 %collective-permute-start.58 = (bf16[1024,2816]{1,0:T(8,128)(2,1)}, bf16[1024,2816]{1,0:T(8,128)(2,1)}, u32[]{:S(2)}, u32[]{:S(2)}) collective-permute-start(bf16[1024,2816]{1,0:T(8,128)(2,1)} %convolution_convert_fusion), channel_id=1, source_target_pairs={{0,2},{2,0},{4,6},{6,4},{8,10},{10,8},{12,14},{14,12},{16,18},{18,... | collective-permute-start | bytes 17301512 | tf_op jit(solution)/shard_map/ppermute | solution.py:53
  460.1 26.1 %collective-permute-start.25 = (bf16[512,1024]{1,0:T(8,128)(2,1)S(1)}, bf16[512,1024]{1,0:T(8,128)(2,1)S(1)}, u32[]{:S(2)}, u32[]{:S(2)}) collective-permute-start(bf16[512,1024]{1,0:T(8,128)(2,1)S(1)} %add_convert_fusion.1), channel_id=1, source_target_pairs={{0,4},{2,6},{4,0},{6,2},{8,12},{10,14},{12,8},{14,10},{16,20},{18,... | collective-permute-start | bytes 3145736 | tf_op jit(solution)/shard_map/ppermute | solution.py:53
  463.2 156.8 %collective-permute-start.53 = (bf16[512,1408]{1,0:T(8,128)(2,1)S(1)}, bf16[512,1408]{1,0:T(8,128)(2,1)S(1)}, u32[]{:S(2)}, u32[]{:S(2)}) collective-permute-start(bf16[512,1408]{1,0:T(8,128)(2,1)S(1)} %fusion.27), channel_id=1, source_target_pairs={{0,4},{2,6},{4,0},{6,2},{8,12},{10,14},{12,8},{14,10},{16,20},{18,... | collective-permute-start | bytes 4325384 | tf_op jit(solution)/shard_map/ppermute | solution.py:53
  466.0 161.5 %collective-permute-start.47 = (bf16[512,1408]{1,0:T(8,128)(2,1)S(1)}, bf16[512,1408]{1,0:T(8,128)(2,1)S(1)}, u32[]{:S(2)}, u32[]{:S(2)}) collective-permute-start(bf16[512,1408]{1,0:T(8,128)(2,1)S(1)} %fusion.26), channel_id=1, source_target_pairs={{0,4},{2,6},{4,0},{6,2},{8,12},{10,14},{12,8},{14,10},{16,20},{18,... | collective-permute-start | bytes 4325384 | tf_op jit(solution)/shard_map/ppermute | solution.py:53
  467.5 102.9 %collective-permute-start.20 = (bf16[512,1024]{1,0:T(8,128)(2,1)S(1)}, bf16[512,1024]{1,0:T(8,128)(2,1)S(1)}, u32[]{:S(2)}, u32[]{:S(2)}) collective-permute-start(bf16[512,1024]{1,0:T(8,128)(2,1)S(1)} %add_convert_fusion.2), channel_id=1, source_target_pairs={{0,4},{2,6},{4,0},{6,2},{8,12},{10,14},{12,8},{14,10},{16,20},{18,... | collective-permute-start | bytes 3145736 | tf_op jit(solution)/shard_map/ppermute | solution.py:53
  486.2 106.7 %collective-permute-start.15 = (bf16[512,1024]{1,0:T(8,128)(2,1)S(1)}, bf16[512,1024]{1,0:T(8,128)(2,1)S(1)}, u32[]{:S(2)}, u32[]{:S(2)}) collective-permute-start(bf16[512,1024]{1,0:T(8,128)(2,1)S(1)} %add_convert_fusion.3), channel_id=1, source_target_pairs={{0,4},{2,6},{4,0},{6,2},{8,12},{10,14},{12,8},{14,10},{16,20},{18,... | collective-permute-start | bytes 3145736 | tf_op jit(solution)/shard_map/ppermute | solution.py:53
  570.5 44.9 %collective-permute-start.30 = (bf16[512,1024]{1,0:T(8,128)(2,1)S(1)}, bf16[512,1024]{1,0:T(8,128)(2,1)S(1)}, u32[]{:S(2)}, u32[]{:S(2)}) collective-permute-start(bf16[512,1024]{1,0:T(8,128)(2,1)S(1)} %add_convert_fusion), channel_id=1, source_target_pairs={{0,4},{2,6},{4,0},{6,2},{8,12},{10,14},{12,8},{14,10},{16,20},{18,... | collective-permute-start | bytes 3145736 | tf_op jit(solution)/shard_map/ppermute | solution.py:53
  592.9 53.4 %collective-permute-start.41 = (bf16[512,1408]{1,0:T(8,128)(2,1)S(1)}, bf16[512,1408]{1,0:T(8,128)(2,1)S(1)}, u32[]{:S(2)}, u32[]{:S(2)}) collective-permute-start(bf16[512,1408]{1,0:T(8,128)(2,1)S(1)} %fusion.25), channel_id=1, source_target_pairs={{0,4},{2,6},{4,0},{6,2},{8,12},{10,14},{12,8},{14,10},{16,20},{18,... | collective-permute-start | bytes 4325384 | tf_op jit(solution)/shard_map/ppermute | solution.py:53
  615.4 61.3 %collective-permute-start.35 = (bf16[512,1408]{1,0:T(8,128)(2,1)S(1)}, bf16[512,1408]{1,0:T(8,128)(2,1)S(1)}, u32[]{:S(2)}, u32[]{:S(2)}) collective-permute-start(bf16[512,1408]{1,0:T(8,128)(2,1)S(1)} %fusion.24), channel_id=1, source_target_pairs={{0,4},{2,6},{4,0},{6,2},{8,12},{10,14},{12,8},{14,10},{16,20},{18,... | collective-permute-start | bytes 4325384 | tf_op jit(solution)/shard_map/ppermute | solution.py:53
  619.9 60.0 %collective-permute-start.28 = (bf16[128,1024]{1,0:T(8,128)(2,1)S(1)}, bf16[128,1024]{1,0:T(8,128)(2,1)S(1)}, u32[]{:S(2)}, u32[]{:S(2)}) collective-permute-start(bf16[128,1024]{1,0:T(8,128)(2,1)S(1)} %add_convert_fusion.20), channel_id=1, source_target_pairs={{0,24},{2,26},{4,28},{6,30},{8,16},{10,18},{12,20},{14,22},{16,8},... | collective-permute-start | bytes 786440 | tf_op jit(solution)/shard_map/ppermute | solution.py:67
  627.5 55.4 %collective-permute-start.33 = (bf16[128,1024]{1,0:T(8,128)(2,1)S(1)}, bf16[128,1024]{1,0:T(8,128)(2,1)S(1)}, u32[]{:S(2)}, u32[]{:S(2)}) collective-permute-start(bf16[128,1024]{1,0:T(8,128)(2,1)S(1)} %add_convert_fusion.17), channel_id=1, source_target_pairs={{0,24},{2,26},{4,28},{6,30},{8,16},{10,18},{12,20},{14,22},{16,8},... | collective-permute-start | bytes 786440 | tf_op jit(solution)/shard_map/ppermute | solution.py:67
  646.3 37.0 %collective-permute-start.32 = (bf16[128,1024]{1,0:T(8,128)(2,1)S(1)}, bf16[128,1024]{1,0:T(8,128)(2,1)S(1)}, u32[]{:S(2)}, u32[]{:S(2)}) collective-permute-start(bf16[128,1024]{1,0:T(8,128)(2,1)S(1)} %add_convert_fusion.18), channel_id=1, source_target_pairs={{0,16},{2,18},{4,20},{6,22},{8,24},{10,26},{12,28},{14,30},{16,0},... | collective-permute-start | bytes 786440 | tf_op jit(solution)/shard_map/ppermute | solution.py:67
  676.7 11.6 %collective-permute-start.31 = (bf16[128,1024]{1,0:T(8,128)(2,1)S(1)}, bf16[128,1024]{1,0:T(8,128)(2,1)S(1)}, u32[]{:S(2)}, u32[]{:S(2)}) collective-permute-start(bf16[128,1024]{1,0:T(8,128)(2,1)S(1)} %add_convert_fusion.19), channel_id=1, source_target_pairs={{0,8},{2,10},{4,12},{6,14},{8,0},{10,2},{12,4},{14,6},{16,24},{18,... | collective-permute-start | bytes 786440 | tf_op jit(solution)/shard_map/ppermute | solution.py:67
  679.9 16.0 %collective-permute-start.27 = (bf16[128,1024]{1,0:T(8,128)(2,1)}, bf16[128,1024]{1,0:T(8,128)(2,1)}, u32[]{:S(2)}, u32[]{:S(2)}) collective-permute-start(bf16[128,1024]{1,0:T(8,128)(2,1)} %add_convert_fusion.21), channel_id=1, source_target_pairs={{0,16},{2,18},{4,20},{6,22},{8,24},{10,26},{12,28},{14,30},{16,0},... | collective-permute-start | bytes 786440 | tf_op jit(solution)/shard_map/ppermute | solution.py:67
  682.8 13.1 %collective-permute-start.26 = (bf16[128,1024]{1,0:T(8,128)(2,1)}, bf16[128,1024]{1,0:T(8,128)(2,1)}, u32[]{:S(2)}, u32[]{:S(2)}) collective-permute-start(bf16[128,1024]{1,0:T(8,128)(2,1)} %add_convert_fusion.22), channel_id=1, source_target_pairs={{0,8},{2,10},{4,12},{6,14},{8,0},{10,2},{12,4},{14,6},{16,24},{18,... | collective-permute-start | bytes 786440 | tf_op jit(solution)/shard_map/ppermute | solution.py:67
  683.4 20.5 %collective-permute-start.23 = (bf16[128,1024]{1,0:T(8,128)(2,1)}, bf16[128,1024]{1,0:T(8,128)(2,1)}, u32[]{:S(2)}, u32[]{:S(2)}) collective-permute-start(bf16[128,1024]{1,0:T(8,128)(2,1)} %add_convert_fusion.23), channel_id=1, source_target_pairs={{0,24},{2,26},{4,28},{6,30},{8,16},{10,18},{12,20},{14,22},{16,8},... | collective-permute-start | bytes 786440 | tf_op jit(solution)/shard_map/ppermute | solution.py:67
  688.3 71.1 %collective-permute-start.54 = (bf16[384,1408]{1,0:T(8,128)(2,1)}, bf16[384,1408]{1,0:T(8,128)(2,1)}, u32[]{:S(2)}, u32[]{:S(2)}) collective-permute-start(bf16[384,1408]{1,0:T(8,128)(2,1)} %fusion.31), channel_id=1, source_target_pairs={{0,8},{2,10},{4,12},{6,14},{24,16},{26,18},{28,20},{30,22},{1,9},{... | collective-permute-start | bytes 3244040 | tf_op jit(solution)/shard_map/ppermute | solution.py:67
  695.9 34.0 %collective-permute-start.22 = (bf16[128,1024]{1,0:T(8,128)(2,1)}, bf16[128,1024]{1,0:T(8,128)(2,1)S(1)}, u32[]{:S(2)}, u32[]{:S(2)}) collective-permute-start(bf16[128,1024]{1,0:T(8,128)(2,1)} %add_convert_fusion.24), channel_id=1, source_target_pairs={{0,16},{2,18},{4,20},{6,22},{8,24},{10,26},{12,28},{14,30},{16,0},... | collective-permute-start | bytes 786440 | tf_op jit(solution)/shard_map/ppermute | solution.py:67
  696.0 39.6 %collective-permute-start.21 = (bf16[128,1024]{1,0:T(8,128)(2,1)}, bf16[128,1024]{1,0:T(8,128)(2,1)S(1)}, u32[]{:S(2)}, u32[]{:S(2)}) collective-permute-start(bf16[128,1024]{1,0:T(8,128)(2,1)} %add_convert_fusion.25), channel_id=1, source_target_pairs={{0,8},{2,10},{4,12},{6,14},{8,0},{10,2},{12,4},{14,6},{16,24},{18,... | collective-permute-start | bytes 786440 | tf_op jit(solution)/shard_map/ppermute | solution.py:67
  703.8 39.9 %collective-permute-start.18 = (bf16[128,1024]{1,0:T(8,128)(2,1)}, bf16[128,1024]{1,0:T(8,128)(2,1)S(1)}, u32[]{:S(2)}, u32[]{:S(2)}) collective-permute-start(bf16[128,1024]{1,0:T(8,128)(2,1)} %add_convert_fusion.26), channel_id=1, source_target_pairs={{0,24},{2,26},{4,28},{6,30},{8,16},{10,18},{12,20},{14,22},{16,8},... | collective-permute-start | bytes 786440 | tf_op jit(solution)/shard_map/ppermute | solution.py:67
  729.9 18.8 %collective-permute-start.17 = (bf16[128,1024]{1,0:T(8,128)(2,1)}, bf16[128,1024]{1,0:T(8,128)(2,1)S(1)}, u32[]{:S(2)}, u32[]{:S(2)}) collective-permute-start(bf16[128,1024]{1,0:T(8,128)(2,1)} %add_convert_fusion.27), channel_id=1, source_target_pairs={{0,16},{2,18},{4,20},{6,22},{8,24},{10,26},{12,28},{14,30},{16,0},... | collective-permute-start | bytes 786440 | tf_op jit(solution)/shard_map/ppermute | solution.py:67
  735.5 16.9 %collective-permute-start.16 = (bf16[128,1024]{1,0:T(8,128)(2,1)}, bf16[128,1024]{1,0:T(8,128)(2,1)S(1)}, u32[]{:S(2)}, u32[]{:S(2)}) collective-permute-start(bf16[128,1024]{1,0:T(8,128)(2,1)} %add_convert_fusion.28), channel_id=1, source_target_pairs={{0,8},{2,10},{4,12},{6,14},{8,0},{10,2},{12,4},{14,6},{16,24},{18,... | collective-permute-start | bytes 786440 | tf_op jit(solution)/shard_map/ppermute | solution.py:67
  743.8 31.9 %collective-permute-start.48 = (bf16[384,1408]{1,0:T(8,128)(2,1)}, bf16[384,1408]{1,0:T(8,128)(2,1)S(1)}, u32[]{:S(2)}, u32[]{:S(2)}) collective-permute-start(bf16[384,1408]{1,0:T(8,128)(2,1)} %copy-done.55), channel_id=1, source_target_pairs={{0,8},{2,10},{4,12},{6,14},{24,16},{26,18},{28,20},{30,22},{1,9},{... | collective-permute-start | bytes 3244040 | tf_op jit(solution)/shard_map/ppermute | solution.py:67
  748.7 50.0 %collective-permute-start.42 = (bf16[384,1408]{1,0:T(8,128)(2,1)S(1)}, bf16[384,1408]{1,0:T(8,128)(2,1)S(1)}, u32[]{:S(2)}, u32[]{:S(2)}) collective-permute-start(bf16[384,1408]{1,0:T(8,128)(2,1)S(1)} %copy-done.54), channel_id=1, source_target_pairs={{0,8},{2,10},{4,12},{6,14},{24,16},{26,18},{28,20},{30,22},{1,9},{... | collective-permute-start | bytes 3244040 | tf_op jit(solution)/shard_map/ppermute | solution.py:67
  752.5 68.0 %collective-permute-start.36 = (bf16[384,1408]{1,0:T(8,128)(2,1)S(1)}, bf16[384,1408]{1,0:T(8,128)(2,1)S(1)}, u32[]{:S(2)}, u32[]{:S(2)}) collective-permute-start(bf16[384,1408]{1,0:T(8,128)(2,1)S(1)} %copy-done.52), channel_id=1, source_target_pairs={{0,8},{2,10},{4,12},{6,14},{24,16},{26,18},{28,20},{30,22},{1,9},{... | collective-permute-start | bytes 3244040 | tf_op jit(solution)/shard_map/ppermute | solution.py:67
  759.4 43.9 %collective-permute-start.55 = (bf16[128,1408]{1,0:T(8,128)(2,1)S(1)}, bf16[128,1408]{1,0:T(8,128)(2,1)S(1)}, u32[]{:S(2)}, u32[]{:S(2)}) collective-permute-start(bf16[128,1408]{1,0:T(8,128)(2,1)S(1)} %copy-done.64), channel_id=1, source_target_pairs={{8,0},{10,2},{12,4},{14,6},{16,24},{18,26},{20,28},{22,30},{9,1},{... | collective-permute-start | bytes 1081352 | tf_op jit(solution)/shard_map/ppermute | solution.py:67
  775.6 49.5 %collective-permute-start.49 = (bf16[128,1408]{1,0:T(8,128)(2,1)S(1)}, bf16[128,1408]{1,0:T(8,128)(2,1)S(1)}, u32[]{:S(2)}, u32[]{:S(2)}) collective-permute-start(bf16[128,1408]{1,0:T(8,128)(2,1)S(1)} %copy-done.62), channel_id=1, source_target_pairs={{8,0},{10,2},{12,4},{14,6},{16,24},{18,26},{20,28},{22,30},{9,1},{... | collective-permute-start | bytes 1081352 | tf_op jit(solution)/shard_map/ppermute | solution.py:67
  798.7 27.2 %collective-permute-start.43 = (bf16[128,1408]{1,0:T(8,128)(2,1)S(1)}, bf16[128,1408]{1,0:T(8,128)(2,1)S(1)}, u32[]{:S(2)}, u32[]{:S(2)}) collective-permute-start(bf16[128,1408]{1,0:T(8,128)(2,1)S(1)} %copy-done.63), channel_id=1, source_target_pairs={{8,0},{10,2},{12,4},{14,6},{16,24},{18,26},{20,28},{22,30},{9,1},{... | collective-permute-start | bytes 1081352 | tf_op jit(solution)/shard_map/ppermute | solution.py:67
  800.2 27.0 %collective-permute-start.57 = (bf16[128,1408]{1,0:T(8,128)(2,1)S(1)}, bf16[128,1408]{1,0:T(8,128)(2,1)S(1)}, u32[]{:S(2)}, u32[]{:S(2)}) collective-permute-start(bf16[128,1408]{1,0:T(8,128)(2,1)S(1)} %get-tuple-element.79), channel_id=1, source_target_pairs={{8,16},{10,18},{12,20},{14,22},{16,8},{18,10},{20,12},{22,14},{9,1... | collective-permute-start | bytes 1081352 | tf_op jit(solution)/shard_map/ppermute | solution.py:67
  803.3 24.6 %collective-permute-start.56 = (bf16[128,1408]{1,0:T(8,128)(2,1)S(1)}, bf16[128,1408]{1,0:T(8,128)(2,1)S(1)}, u32[]{:S(2)}, u32[]{:S(2)}) collective-permute-start(bf16[128,1408]{1,0:T(8,128)(2,1)S(1)} %get-tuple-element.78), channel_id=1, source_target_pairs={{8,24},{10,26},{12,28},{14,30},{16,0},{18,2},{20,4},{22,6},{9,25},... | collective-permute-start | bytes 1081352 | tf_op jit(solution)/shard_map/ppermute | solution.py:67
  820.5 57.6 %collective-permute-start.63 = (bf16[384,2816]{1,0:T(8,128)(2,1)S(1)}, bf16[384,2816]{1,0:T(8,128)(2,1)S(1)}, u32[]{:S(2)}, u32[]{:S(2)}) collective-permute-start(bf16[384,2816]{1,0:T(8,128)(2,1)S(1)} %fusion.7), channel_id=1, source_target_pairs={{0,8},{2,10},{4,12},{6,14},{24,16},{26,18},{28,20},{30,22},{1,9},{... | collective-permute-start | bytes 6488072 | tf_op jit(solution)/shard_map/ppermute | solution.py:67
  825.2 6.6 collective-permute-start.51
  825.9 18.9 %collective-permute-start.50 = (bf16[128,1408]{1,0:T(8,128)(2,1)S(1)}, bf16[128,1408]{1,0:T(8,128)(2,1)S(1)}, u32[]{:S(2)}, u32[]{:S(2)}) collective-permute-start(bf16[128,1408]{1,0:T(8,128)(2,1)S(1)} %get-tuple-element.76), channel_id=1, source_target_pairs={{8,24},{10,26},{12,28},{14,30},{16,0},{18,2},{20,4},{22,6},{9,25},... | collective-permute-start | bytes 1081352 | tf_op jit(solution)/shard_map/ppermute | solution.py:67
  827.2 18.9 %collective-permute-start.45 = (bf16[128,1408]{1,0:T(8,128)(2,1)S(1)}, bf16[128,1408]{1,0:T(8,128)(2,1)S(1)}, u32[]{:S(2)}, u32[]{:S(2)}) collective-permute-start(bf16[128,1408]{1,0:T(8,128)(2,1)S(1)} %get-tuple-element.75), channel_id=1, source_target_pairs={{8,16},{10,18},{12,20},{14,22},{16,8},{18,10},{20,12},{22,14},{9,1... | collective-permute-start | bytes 1081352 | tf_op jit(solution)/shard_map/ppermute | solution.py:67
  827.9 32.4 %collective-permute-start.44 = (bf16[128,1408]{1,0:T(8,128)(2,1)S(1)}, bf16[128,1408]{1,0:T(8,128)(2,1)S(1)}, u32[]{:S(2)}, u32[]{:S(2)}) collective-permute-start(bf16[128,1408]{1,0:T(8,128)(2,1)S(1)} %get-tuple-element.74), channel_id=1, source_target_pairs={{8,24},{10,26},{12,28},{14,30},{16,0},{18,2},{20,4},{22,6},{9,25},... | collective-permute-start | bytes 1081352 | tf_op jit(solution)/shard_map/ppermute | solution.py:67
  831.8 84.6 %collective-permute-start.59 = (bf16[384,2816]{1,0:T(8,128)(2,1)S(1)}, bf16[384,2816]{1,0:T(8,128)(2,1)S(1)}, u32[]{:S(2)}, u32[]{:S(2)}) collective-permute-start(bf16[384,2816]{1,0:T(8,128)(2,1)S(1)} %fusion.6), channel_id=1, source_target_pairs={{0,8},{2,10},{4,12},{6,14},{24,16},{26,18},{28,20},{30,22},{1,9},{... | collective-permute-start | bytes 6488072 | tf_op jit(solution)/shard_map/ppermute | solution.py:67
  844.8 20.2 %collective-permute-start.37 = (bf16[128,1408]{1,0:T(8,128)(2,1)S(1)}, bf16[128,1408]{1,0:T(8,128)(2,1)S(1)}, u32[]{:S(2)}, u32[]{:S(2)}) collective-permute-start(bf16[128,1408]{1,0:T(8,128)(2,1)S(1)} %copy-done.61), channel_id=1, source_target_pairs={{8,0},{10,2},{12,4},{14,6},{16,24},{18,26},{20,28},{22,30},{9,1},{... | collective-permute-start | bytes 1081352 | tf_op jit(solution)/shard_map/ppermute | solution.py:67
  846.1 18.9 %collective-permute-start.39 = (bf16[128,1408]{1,0:T(8,128)(2,1)S(1)}, bf16[128,1408]{1,0:T(8,128)(2,1)S(1)}, u32[]{:S(2)}, u32[]{:S(2)}) collective-permute-start(bf16[128,1408]{1,0:T(8,128)(2,1)S(1)} %get-tuple-element.73), channel_id=1, source_target_pairs={{8,16},{10,18},{12,20},{14,22},{16,8},{18,10},{20,12},{22,14},{9,1... | collective-permute-start | bytes 1081352 | tf_op jit(solution)/shard_map/ppermute | solution.py:67
  860.3 13.4 %collective-permute-start.38 = (bf16[128,1408]{1,0:T(8,128)(2,1)S(1)}, bf16[128,1408]{1,0:T(8,128)(2,1)S(1)}, u32[]{:S(2)}, u32[]{:S(2)}) collective-permute-start(bf16[128,1408]{1,0:T(8,128)(2,1)S(1)} %get-tuple-element.72), channel_id=1, source_target_pairs={{8,24},{10,26},{12,28},{14,30},{16,0},{18,2},{20,4},{22,6},{9,25},... | collective-permute-start | bytes 1081352 | tf_op jit(solution)/shard_map/ppermute | solution.py:67
  875.5 41.9 %collective-permute-start.64 = (bf16[128,2816]{1,0:T(8,128)(2,1)S(1)}, bf16[128,2816]{1,0:T(8,128)(2,1)S(1)}, u32[]{:S(2)}, u32[]{:S(2)}) collective-permute-start(bf16[128,2816]{1,0:T(8,128)(2,1)S(1)} %slice.930), channel_id=1, source_target_pairs={{8,0},{10,2},{12,4},{14,6},{16,24},{18,26},{20,28},{22,30},{9,1},{... | collective-permute-start | bytes 2162696 | tf_op jit(solution)/shard_map/ppermute | solution.py:67
  876.8 49.0 %collective-permute-start.60 = (bf16[128,2816]{1,0:T(8,128)(2,1)S(1)}, bf16[128,2816]{1,0:T(8,128)(2,1)S(1)}, u32[]{:S(2)}, u32[]{:S(2)}) collective-permute-start(bf16[128,2816]{1,0:T(8,128)(2,1)S(1)} %slice.920), channel_id=1, source_target_pairs={{8,0},{10,2},{12,4},{14,6},{16,24},{18,26},{20,28},{22,30},{9,1},{... | collective-permute-start | bytes 2162696 | tf_op jit(solution)/shard_map/ppermute | solution.py:67
  878.4 40.3 %collective-permute-start.66 = (bf16[128,2816]{1,0:T(8,128)(2,1)S(1)}, bf16[128,2816]{1,0:T(8,128)(2,1)S(1)}, u32[]{:S(2)}, u32[]{:S(2)}) collective-permute-start(bf16[128,2816]{1,0:T(8,128)(2,1)S(1)} %get-tuple-element.71), channel_id=1, source_target_pairs={{8,16},{10,18},{12,20},{14,22},{16,8},{18,10},{20,12},{22,14},{9,1... | collective-permute-start | bytes 2162696 | tf_op jit(solution)/shard_map/ppermute | solution.py:67
  879.1 39.6 %collective-permute-start.65 = (bf16[128,2816]{1,0:T(8,128)(2,1)S(1)}, bf16[128,2816]{1,0:T(8,128)(2,1)S(1)}, u32[]{:S(2)}, u32[]{:S(2)}) collective-permute-start(bf16[128,2816]{1,0:T(8,128)(2,1)S(1)} %get-tuple-element.70), channel_id=1, source_target_pairs={{8,24},{10,26},{12,28},{14,30},{16,0},{18,2},{20,4},{22,6},{9,25},... | collective-permute-start | bytes 2162696 | tf_op jit(solution)/shard_map/ppermute | solution.py:67
  916.7 9.1 collective-permute-start.62
  917.4 35.0 %collective-permute-start.61 = (bf16[128,2816]{1,0:T(8,128)(2,1)S(1)}, bf16[128,2816]{1,0:T(8,128)(2,1)S(1)}, u32[]{:S(2)}, u32[]{:S(2)}) collective-permute-start(bf16[128,2816]{1,0:T(8,128)(2,1)S(1)} %get-tuple-element.68), channel_id=1, source_target_pairs={{8,24},{10,26},{12,28},{14,30},{16,0},{18,2},{20,4},{22,6},{9,25},... | collective-permute-start | bytes 2162696 | tf_op jit(solution)/shard_map/ppermute | solution.py:67
  920.6 31.8 %collective-permute-start.67 = (bf16[128,2816]{1,0:T(8,128)(2,1)S(1)}, bf16[128,2816]{1,0:T(8,128)(2,1)S(1)}, u32[]{:S(2)}, u32[]{:S(2)}) collective-permute-start(bf16[128,2816]{1,0:T(8,128)(2,1)S(1)} %fusion.19), channel_id=1, source_target_pairs={{0,4},{2,6},{4,0},{6,2},{8,12},{10,14},{12,8},{14,10},{16,20},{18,... | collective-permute-start | bytes 2162696 | tf_op jit(solution)/shard_map/ppermute | solution.py:53
  (116 other events, 1746.0 us)
Sparse Core Ops, SparseCore 0:
  12.8 94.1 all-gather.5
  109.2 180.7 all-gather.3
